TPU v7x, 32 devices: a whole 2x2x4 slice. The times are simulated.
32 devices in a mesh: dp: 8 (over z, core), ctx: 4 (over y, x).
Axes of the slice: x: 2, y: 2, z: 4, core: 2. Of those that a mesh axis runs over, the one named last changes fastest.
Arguments:
- video: bfloat16 [64, 32, 64, 128], P('dp', 'ctx'), parts along dimension 0, may hold values from -6 to 6
- conv_weight: bfloat16 [3, 3, 3, 128, 256], replicated, may hold values from -0.109375 to 0.109375
- latent_weight: bfloat16 [256, 16], replicated, may hold values from -0.375 to 0.375
- embed_weight: bfloat16 [64, 3072], replicated, may hold values from -0.75 to 0.75
- modulation: float32 [32, 3072], P('dp'), parts along dimension 0, may hold values from -3 to 3
- qkv_weight: bfloat16 [3072, 3, 2048], P(None, None, 'ctx'), may hold values from -0.109375 to 0.109375
- qk_gain: float32 [2, 128], replicated, may hold values from 0.5 to 2
- text: bfloat16 [2048, 3072], P('dp'), parts along dimension 0, may hold values from -6 to 6
- text_weight: bfloat16 [3072, 2, 2048], P(None, None, 'ctx'), may hold values from -0.109375 to 0.109375
Outputs:
- attended: bfloat16 [8192, 2048], P(('dp', 'ctx')), parts along dimension 0
There are 8 independent parts, one for each index of `dp`. A program takes and returns all parts, laid end to end along the dimension named above; an argument that names none is the same for every part. Nothing has to cross between parts.
All inputs are finite; a program needn't handle non-finite values.
Results may differ from a plain program's by a relative error of at most 0.0074.
Values may be sent and summed in bfloat16 or wider, within the bound.
No kernel may reach another device: no remote copies, remote signals or barrier semaphores. Data moves between devices by JAX's collectives and lax.ppermute only.
A program may use at most 128 MiB of HBM per device.

v0:
```python
import math

import jax
import jax.numpy as jnp
from jax import lax
from jax.sharding import PartitionSpec as P

D = 3072
HS = 128


def shifted(x, axis, by):
    devices = lax.axis_size(axis)
    pairs = [(i, i + by) for i in range(devices) if 0 <= i + by < devices]
    return lax.ppermute(x, axis, pairs)


def layer_norm(values):
    centred = values - jnp.mean(values, -1, keepdims=True)
    return centred * lax.rsqrt(jnp.mean(centred * centred, -1, keepdims=True) + 1e-06)


def head_norm(values, gain):
    return values * lax.rsqrt(jnp.mean(values * values, -1, keepdims=True) + 1e-06) * gain


def patchify(latent):
    frames, rows, cols, chans = latent.shape
    shaped = latent.reshape(frames, rows // 2, 2, cols // 2, 2, chans)
    return shaped.transpose(0, 1, 3, 2, 4, 5).reshape(frames, rows // 2, cols // 2, 4 * chans)


def attend(query_block, key_rows, value_rows):
    logits = jnp.einsum(
        "bhd,khd->hbk", query_block, key_rows, preferred_element_type=jnp.float32
    ) / math.sqrt(HS)
    expd = jnp.exp(logits - jnp.max(logits, -1, keepdims=True))
    weights = (expd / jnp.sum(expd, -1, keepdims=True)).astype(jnp.bfloat16)
    return jnp.einsum(
        "hbk,khd->bhd", weights, value_rows, preferred_element_type=jnp.float32
    ).astype(jnp.bfloat16)


def shards(
    video,
    conv_weight,
    latent_weight,
    embed_weight,
    modulation,
    qkv_weight,
    qk_gain,
    text,
    text_weight,
):
    upper_rim = shifted(video[:, -1:], "ctx", 1)
    framed = jnp.concatenate([upper_rim, video], 1)
    framed = jnp.concatenate([framed[:1], framed[:1], framed], 0)
    framed = jnp.pad(framed, ((0, 0), (0, 0), (1, 0), (0, 0)))
    conv = lax.conv_general_dilated(
        framed[None],
        conv_weight,
        (1, 2, 2),
        "VALID",
        dimension_numbers=("NDHWC", "DHWIO", "NDHWC"),
        preferred_element_type=jnp.float32,
    )[0]
    activated = jax.nn.silu(conv).astype(jnp.bfloat16)
    latent = jnp.dot(activated, latent_weight, preferred_element_type=jnp.float32).astype(
        jnp.bfloat16
    )
    tile_patches = patchify(latent)
    width_in = tile_patches.shape[3]
    token_rows = lax.all_to_all(
        tile_patches, "ctx", split_axis=0, concat_axis=1, tiled=True
    ).reshape(-1, width_in)
    embedded = jnp.dot(token_rows, embed_weight, preferred_element_type=jnp.float32)
    stream = (layer_norm(embedded) * (1.0 + modulation[1]) + modulation[0]).astype(jnp.bfloat16)
    text_stream = (
        layer_norm(text.astype(jnp.float32)) * (1.0 + modulation[3]) + modulation[2]
    ).astype(jnp.bfloat16)
    text_count = text.shape[0]
    local_heads = qkv_weight.shape[2] // HS
    flat_weight = qkv_weight.reshape(D, -1)
    projected = jnp.dot(
        lax.all_gather(stream, "ctx", axis=0, tiled=True),
        flat_weight,
        preferred_element_type=jnp.float32,
    )
    count = projected.shape[0]
    projected = projected.reshape(count, 3, local_heads, HS)
    queries = head_norm(projected[:, 0], qk_gain[0]).astype(jnp.bfloat16)
    keys_own = head_norm(projected[:, 1], qk_gain[1]).astype(jnp.bfloat16)
    values_own = projected[:, 2].astype(jnp.bfloat16)
    text_projected = jnp.dot(
        text_stream, text_weight.reshape(D, -1), preferred_element_type=jnp.float32
    )
    text_projected = text_projected.reshape(text_count, 2, local_heads, HS)
    text_keys = head_norm(text_projected[:, 0], qk_gain[1]).astype(jnp.bfloat16)
    text_values = text_projected[:, 1].astype(jnp.bfloat16)
    key_rows = jnp.concatenate([text_keys, keys_own], 0)
    value_rows = jnp.concatenate([text_values, values_own], 0)
    block = 512 if count % 512 == 0 else count
    blocks = queries.reshape(count // block, block, local_heads, HS)
    result = lax.map(lambda query_block: attend(query_block, key_rows, value_rows), blocks)
    result = result.reshape(count, local_heads * HS)
    return lax.all_to_all(result, "ctx", split_axis=0, concat_axis=1, tiled=True)


def solution(mesh):
    in_specs = (
        P("dp", "ctx", None, None),
        P(),
        P(),
        P(),
        P("dp", None),
        P(None, None, "ctx"),
        P(),
        P("dp", None),
        P(None, None, "ctx"),
    )
    out_specs = P(("dp", "ctx"), None)
    return jax.shard_map(shards, mesh=mesh, in_specs=in_specs, out_specs=out_specs, check_vma=False)
```

profile of v0, /device:TPU:0, one launch (start us, length us, event | category | flops | bytes accessed | tf_op | source)
XLA Modules:
  0.0 192.1 jit_solution(4728737379839621711)
XLA Ops:
  6.5 1.0 slice.43
  7.6 4.8 %collective-permute-start = (bf16[8,1,64,128]{3,2,1,0:T(8,128)(2,1)S(1)}, bf16[8,1,64,128]{3,2,1,0:T(8,128)(2,1)S(1)}, u32[]{:S(2)}, u32[]{:S(2)}) collective-permute-start(bf16[8,1,64,128]{3,2,1,0:T(8,128)(2,1)S(1)} %slice.43), channel_id=1, source_target_pairs={{0,1},{1,2},{2,3},{4,5},{5,6},{6,7},{8,9},{9,10},{10,11},{12,13},{... | collective-permute-start | bytes 393224 | tf_op jit(solution)/shard_map/ppermute | solution.py:15
  12.4 2.7 %collective-permute-done = bf16[8,1,64,128]{3,2,1,0:T(8,128)(2,1)S(1)} collective-permute-done((bf16[8,1,64,128]{3,2,1,0:T(8,128)(2,1)S(1)}, bf16[8,1,64,128]{3,2,1,0:T(8,128)(2,1)S(1)}, u32[]{:S(2)}, u32[]{:S(2)}) %collective-permute-start) | collective-permute-done | bytes 131104 | tf_op jit(solution)/shard_map/ppermute | solution.py:15
  15.2 1.4 constant_dynamic-update-slice_fusion
  16.6 0.7 fusion.49
  17.3 1.4 pad.5
  18.7 4.6 %reshape.97 = bf16[10,9,1,8,10,128]{5,4,3,1,0,2:T(8,128)(2,1)} reshape(bf16[10,9,1,80,128]{4,3,1,0,2:T(8,128)(2,1)} %pad.5) | data formatting | bytes 3686400 | tf_op jit(solution)/shard_map/conv_general_dilated | solution.py:59
  23.3 2.4 %copy.26 = bf16[10,9,1,8,10,128]{5,3,4,1,0,2:T(8,128)(2,1)S(1)} copy(bf16[10,9,1,8,10,128]{5,4,3,1,0,2:T(8,128)(2,1)} %reshape.97) | data formatting | bytes 3686400 | tf_op jit(solution)/shard_map/conv_general_dilated | solution.py:59
  25.9 2.6 %fusion.57 = f32[8,4,8,5,256]{4,2,3,1,0:T(8,128)S(1)} fusion(bf16[3,3,3,128,256]{4,3,2,1,0:T(8,128)(2,1)S(1)} %copy-done, bf16[10,9,1,7,2,128]{5,3,4,1,0,2:T(8,128)(2,1)S(1)} %slice.59, bf16[10,9,1,8,10,128]{5,3,4,1,0,2:T(8,128)(2,1)S(1)} %copy.26, pred[8,5]{0,1:T(8,128)(4,1)S(1)} %copy-done.9), kind=kOutput, calls=%fused_computation.60 | convolution fusion | flops 2271887360 | bytes 5245992 | tf_op jit(solution)/shard_map/conv_general_dilated | solution.py:59
  28.5 0.8 copy.27
  29.3 0.3 multiply_convert_fusion.1
  29.6 0.5 convolution_convert_fusion
  30.1 0.2 copy.29
  30.3 0.2 copy.30
  30.7 0.7 reshape.112
  31.5 4.7 %all-to-all-start = ((bf16[4,2,2048]{2,1,0:T(2,128)(2,1)}), bf16[4,2,2048]{2,1,0:T(2,128)(2,1)S(1)}, u32[]{:S(2)}, u32[]{:S(2)}) async-start(bf16[4,2,2048]{2,1,0:T(2,128)(2,1)} %reshape.112), calls=%async_computation | async-start | bytes 65536 | tf_op jit(solution)/shard_map/all_to_all | solution.py:73
  36.2 4.7 %all-to-all-done = bf16[4,2,2048]{2,1,0:T(2,128)(2,1)S(1)} async-done(((bf16[4,2,2048]{2,1,0:T(2,128)(2,1)}), bf16[4,2,2048]{2,1,0:T(2,128)(2,1)S(1)}, u32[]{:S(2)}, u32[]{:S(2)}) %all-to-all-start) | async-done | bytes 32800 | tf_op jit(solution)/shard_map/all_to_all | solution.py:73
  41.1 0.6 fusion.73
  41.7 0.5 multiply_reduce_fusion.1
  42.2 1.9 add_convert_fusion
  44.1 12.9 %copy.32 = bf16[3072,3,512]{0,2,1:T(8,128)(2,1)} copy(bf16[3072,3,512]{2,0,1:T(8,128)(2,1)} %param.16) | data formatting | bytes 18874368 | tf_op args[5]
  57.0 7.5 %copy.47 = bf16[384,8,2,512]{3,1,2,0:T(8,128)(2,1)} copy(bf16[384,8,2,512]{3,2,1,0:T(2,128)(2,1)} %bitcast.112) | data formatting | bytes 12582912
  64.5 8.8 %copy.35 = bf16[1024,3072]{1,0:T(8,128)(2,1)} copy(bf16[1024,3072]{0,1:T(8,128)(2,1)} %bitcast.109) | data formatting | bytes 12582912 | tf_op jit(solution)/shard_map/dot_general | solution.py:94
  73.3 0.3 convert_reduce_fusion
  73.6 0.6 fusion.34
  74.2 4.0 %fusion.51 = f32[256,2,4,128]{3,0,2,1:T(8,128)S(1)} fusion(bf16[2,4,128,3072]{3,2,1,0:T(8,128)(2,1)} %bitcast.113, bf16[256,3072]{1,0:T(8,128)(2,1)S(1)} %copy-done.2, f32[3072]{0:T(1024)S(1)} %bitcast.124, f32[3072]{0:T(1024)S(1)} %bitcast.123, f32[256]{0:T(256)S(1)} %add_rsqrt_fusion.3, f32[256]{0:T(256)S(1)} %broadcast_multiply_fusion), kind=kOutput, calls=%fused_computation.55 | convolution fusion | flops 1615331328 | bytes 8939520 | tf_op jit(solution)/shard_map/dot_general | solution.py:94
  78.2 0.2 multiply_reduce_fusion.4
  78.5 0.2 multiply_convert_fusion.2
  78.7 35.2 %all-gather.2.cloned.1.call-done = bf16[1024,3072]{1,0:T(8,128)(2,1)} async-done(((bf16[256,3072]{1,0:T(8,128)(2,1)}), bf16[1024,3072]{1,0:T(8,128)(2,1)}) %all-gather.2.cloned.1.call-update) | async-done | bytes 6291472 | tf_op jit(solution)/shard_map/all_gather | solution.py:85
  113.9 13.3 %fusion.26 = f32[1024,3,4,128]{3,0,2,1:T(8,128)S(1)} fusion(bf16[3,4,128,3072]{3,2,1,0:T(8,128)(2,1)} %bitcast.110, bf16[1024,3072]{1,0:T(8,128)(2,1)} %all-gather.2.cloned.1.call-done), kind=kOutput, calls=%fused_computation.19 | convolution fusion | flops 9663676416 | bytes 22020096 | tf_op jit(solution)/shard_map/dot_general | solution.py:84
  127.2 0.6 multiply_reduce_fusion.2
  127.9 0.6 multiply_reduce_fusion.3
  128.6 0.7 multiply_convert_fusion
  129.3 1.5 fusion.46
  130.8 1.3 pad_maximum_fusion
  132.1 31.1 %while.10 = (s32[]{:T(128)}, bf16[2,512,4,128]{3,2,1,0:T(4,128)(2,1)}, bf16[2,512,4,128]{3,1,2,0:T(8,128)(2,1)}, bf16[1280,4,128]{2,0,1:T(8,128)(2,1)S(1)}, bf16[1280,4,128]{2,0,1:T(8,128)(2,1)}, /*index=5*/s32[]{:T(128)}) while((s32[]{:T(128)}, bf16[2,512,4,128]{3,2,1,0:T(4,128)(2,1)}, bf16[2,512,4,128]{3,1,2,0:T(8,128)(2,1)}, ...), condition=%wide.region_10.11_spmd, body=%wide.region_7.10_spmd.sunk | while | flops 1355547904 | bytes 34095744 | solution.py:104
  132.1 8.1 %fusion.90 = (f32[4,512]{1,0:T(4,128)S(1)}, f32[4,512,1280]{2,1,0:T(8,128)}) fusion(bf16[1280,4,128]{2,0,1:T(8,128)(2,1)S(1)} %get-tuple-element.107, bf16[2,512,4,128]{3,1,2,0:T(8,128)(2,1)} %get-tuple-element.106, s32[]{:T(128)} %get-tuple-element.98), kind=kOutput, calls=%fused_computation.91.clone.1 | convolution fusion | flops 678954240 | bytes 12329472 | tf_op jit(solution)/shard_map/while/body/eval_jaxpr/sub | solution.py:37
  140.3 6.0 %fusion.91 = bf16[1,512,4,128]{3,1,2,0:T(8,128)(2,1)S(1)} fusion(bf16[1280,4,128]{2,0,1:T(8,128)(2,1)} %get-tuple-element.108, f32[4,512,1280]{2,1,0:T(8,128)} %get-tuple-element.90, f32[4,512]{1,0:T(4,128)S(1)} %get-tuple-element.91), kind=kOutput, calls=%fused_computation.8.clone.1 | convolution fusion | flops 676593664 | bytes 12328960 | tf_op jit(solution)/shard_map/while/body/eval_jaxpr/hbk,khd->bhd/dot_general | solution.py:39
  146.2 0.4 copy_dynamic-update-slice_fusion.2
  146.7 1.0 copy-done.4
  147.7 8.1 %fusion.90 = (f32[4,512]{1,0:T(4,128)S(1)}, f32[4,512,1280]{2,1,0:T(8,128)}) fusion(bf16[1280,4,128]{2,0,1:T(8,128)(2,1)S(1)} %get-tuple-element.107, bf16[2,512,4,128]{3,1,2,0:T(8,128)(2,1)} %get-tuple-element.106, s32[]{:T(128)} %get-tuple-element.98), kind=kOutput, calls=%fused_computation.91.clone.1 | convolution fusion | flops 678954240 | bytes 12329472 | tf_op jit(solution)/shard_map/while/body/eval_jaxpr/sub | solution.py:37
  155.8 6.0 %fusion.91 = bf16[1,512,4,128]{3,1,2,0:T(8,128)(2,1)S(1)} fusion(bf16[1280,4,128]{2,0,1:T(8,128)(2,1)} %get-tuple-element.108, f32[4,512,1280]{2,1,0:T(8,128)} %get-tuple-element.90, f32[4,512]{1,0:T(4,128)S(1)} %get-tuple-element.91), kind=kOutput, calls=%fused_computation.8.clone.1 | convolution fusion | flops 676593664 | bytes 12328960 | tf_op jit(solution)/shard_map/while/body/eval_jaxpr/hbk,khd->bhd/dot_general | solution.py:39
  161.8 0.4 copy_dynamic-update-slice_fusion.2
  162.2 1.0 copy-done.4
  163.2 1.5 all_to_all.28
  164.7 17.7 %all_to_all.34 = bf16[4,256,512]{2,1,0:T(8,128)(2,1)} all-to-all(bf16[4,256,512]{2,1,0:T(8,128)(2,1)S(1)} %all_to_all.28), channel_id=1, replica_groups=mesh['dp'=8,'ctx'=4] {'ctx'}, dimensions={0} | all-to-all | bytes 2097152 | tf_op jit(solution)/shard_map/all_to_all | solution.py:106
  182.4 1.5 copy.37
  183.9 1.4 copy.38
  (42 shorter events, 0.8 us)
Async XLA Ops:
  6.5 19.3 %copy-start = (bf16[3,3,3,128,256]{4,3,2,1,0:T(8,128)(2,1)S(1)}, bf16[3,3,3,128,256]{4,3,2,1,0:T(8,128)(2,1)}, u32[]{:S(2)}) copy-start(bf16[3,3,3,128,256]{4,3,2,1,0:T(8,128)(2,1)} %param.12) | copy-start | bytes 5308420
  7.6 7.6 %collective-permute-start = (bf16[8,1,64,128]{3,2,1,0:T(8,128)(2,1)S(1)}, bf16[8,1,64,128]{3,2,1,0:T(8,128)(2,1)S(1)}, u32[]{:S(2)}, u32[]{:S(2)}) collective-permute-start(bf16[8,1,64,128]{3,2,1,0:T(8,128)(2,1)S(1)} %slice.43), channel_id=1, source_target_pairs={{0,1},{1,2},{2,3},{4,5},{5,6},{6,7},{8,9},{9,10},{10,11},{12,13},{... | collective-permute-start | bytes 393224 | tf_op jit(solution)/shard_map/ppermute | solution.py:15
  23.3 2.6 %copy-start.9 = (pred[8,5]{0,1:T(8,128)(4,1)S(1)}, pred[8,5]{0,1:T(8,128)(4,1)}, u32[]{:S(2)}) copy-start(pred[8,5]{0,1:T(8,128)(4,1)} %constant.50) | copy-start | bytes 124
  28.5 1.1 copy-start.8
  28.5 7.7 %copy-start.6 = (f32[4,3072]{1,0:T(4,128)S(1)}, f32[4,3072]{1,0:T(4,128)}, u32[]{:S(2)}) copy-start(f32[4,3072]{1,0:T(4,128)} %param.15) | copy-start | bytes 147460
  29.3 11.8 %copy-start.5 = (bf16[64,3072]{1,0:T(8,128)(2,1)S(1)}, bf16[64,3072]{1,0:T(8,128)(2,1)}, u32[]{:S(2)}) copy-start(bf16[64,3072]{1,0:T(8,128)(2,1)} %param.14) | copy-start | bytes 1179652
  31.5 9.5 %all-to-all-start = ((bf16[4,2,2048]{2,1,0:T(2,128)(2,1)}), bf16[4,2,2048]{2,1,0:T(2,128)(2,1)S(1)}, u32[]{:S(2)}, u32[]{:S(2)}) async-start(bf16[4,2,2048]{2,1,0:T(2,128)(2,1)} %reshape.112), calls=%async_computation | async-start | bytes 65536 | tf_op jit(solution)/shard_map/all_to_all | solution.py:73
  36.2 77.7 %all-gather.2.cloned.1.call-start = ((), (), s32[]{:S(2)}) async-start(), calls=%async_computation.2 | async-start | bytes 7864320 | tf_op jit(solution)/shard_map/all_gather | solution.py:85
  64.5 8.8 %copy-start.2 = (bf16[256,3072]{1,0:T(8,128)(2,1)S(1)}, bf16[256,3072]{1,0:T(8,128)(2,1)}, u32[]{:S(2)}) copy-start(bf16[256,3072]{1,0:T(8,128)(2,1)} %param.18) | copy-start | bytes 4718596
  74.2 4.2 %copy-start.7 = (f32[2,128]{1,0:T(2,128)S(1)}, f32[2,128]{1,0:T(2,128)}, u32[]{:S(2)}) copy-start(f32[2,128]{1,0:T(2,128)} %param.17) | copy-start | bytes 3076
  140.3 6.0 %copy-start.3 = (bf16[2,512,4,128]{3,2,1,0:T(4,128)(2,1)S(1)}, bf16[2,512,4,128]{3,2,1,0:T(4,128)(2,1)}, u32[]{:S(2)}) copy-start(bf16[2,512,4,128]{3,2,1,0:T(4,128)(2,1)} %get-tuple-element.99) | copy-start | bytes 3145732 | tf_op jit(solution)/shard_map/while
  146.7 1.0 copy-start.4
  155.8 6.0 %copy-start.3 = (bf16[2,512,4,128]{3,2,1,0:T(4,128)(2,1)S(1)}, bf16[2,512,4,128]{3,2,1,0:T(4,128)(2,1)}, u32[]{:S(2)}) copy-start(bf16[2,512,4,128]{3,2,1,0:T(4,128)(2,1)} %get-tuple-element.99) | copy-start | bytes 3145732 | tf_op jit(solution)/shard_map/while
  162.2 1.0 copy-start.4
  164.7 20.6 %copy-start.1 = (bf16[3,3,3,128,256]{4,3,2,1,0:T(8,128)(2,1)S(1)}, bf16[3,3,3,128,256]{4,3,2,1,0:T(8,128)(2,1)}, u32[]{:S(2)}) copy-start(bf16[3,3,3,128,256]{4,3,2,1,0:T(8,128)(2,1)} %param.12) | copy-start | bytes 5308420
Sparse Core Ops, SparseCore 0:
  44.2 69.6 all-gather.1
where the time goes:
time: 193 us; the launch traced here: 192 us
  local copies, waits for them, and re-layouts  49.8 us (26%)
  matrix products  49.2 us (25%)
  waiting for transfers between devices  42.6 us (22%)
  blocking collectives  17.7 us (9%)
  between operations  13.7 us (7%)
  starting transfers between devices  9.56 us (5%)
  other arithmetic  9.49 us (5%)
    all_gather x1, waiting for transfers between devices, shards(): lax.all_gather(stream, 'ctx', axis=0, tiled=True)  35.2 us
    unnamed x21, local copies, waits for them, and re-layouts  21.3 us
    all_to_all x1, blocking collectives, shards(): lax.all_to_all(result, 'ctx', split_axis=0, concat_axis=1, tiled=True)  17.7 us
    sub x2, matrix products, attend(): expd = jnp.exp(logits - jnp.max(logits, -1, keepdims=True))  16.3 us
    dot_general x1, matrix products, shards(): jnp.dot(lax.all_gather(stream, 'ctx', axis=0, tiled=True), flat_weight, p...  13.3 us
    dot_general x2, matrix products, attend(): jnp.einsum('hbk,khd->bhd', weights, value_rows, preferred_element_type=jn...  11.9 us
    dot_general x1, local copies, waits for them, and re-layouts, shards(): jnp.dot(text_stream, text_weight.reshape(D, -1), preferred_element_type=j...  8.79 us
    conv_general_dilated x4, local copies, waits for them, and re-layouts, shards(): lax.conv_general_dilated(framed[None], conv_weight, (1, 2, 2), 'VALID', d...  7.91 us
  transfers between devices with their start and end apart: 3, of which 3 were waited for; matrix products, arithmetic and copies ran while one was open for 18% of the time, Pallas kernels for 0%

commit v1 on v0

v1 whole, which is shorter than its diff:
```python
import math

import jax
import jax.numpy as jnp
from jax import lax
from jax.experimental import pallas as pl
from jax.experimental.pallas import tpu as pltpu
from jax.sharding import PartitionSpec as P

HS = 128
EPS = 1e-06
F32 = jnp.float32
BF16 = jnp.bfloat16
VMEM = pltpu.VMEM
VMEM_LIMIT = 56 * 1024 * 1024


def vmem_spec():
    return pl.BlockSpec(memory_space=pltpu.VMEM)


def hbm_spec():
    return pl.BlockSpec(memory_space=pl.ANY)


def smem_spec():
    return pl.BlockSpec(memory_space=pltpu.SMEM)


def params():
    return pltpu.CompilerParams(vmem_limit_bytes=VMEM_LIMIT)


def cost(flops, bytes_accessed, transcendentals=0):
    return pl.CostEstimate(
        flops=int(flops), bytes_accessed=int(bytes_accessed), transcendentals=int(transcendentals)
    )


def nbytes(*arrays):
    return sum(math.prod(a.shape) * a.dtype.itemsize for a in arrays)


def split(x):
    hi = x.astype(BF16)
    return hi, (x - hi.astype(F32)).astype(BF16)


def dot(a, b):
    return jnp.dot(a, b, preferred_element_type=F32)


def dot_nt(a, b):
    return lax.dot_general(a, b, (((1,), (1,)), ((), ())), preferred_element_type=F32)


def fold_kernel(chunks, e_ref, mod_ref, w_hbm, rhs0_ref, rhs1_ref, shift_ref, gram_ref, w_buf, lhs_ref, acc_ref, sem):
    parts, depth, width = w_hbm.shape
    rows = depth // chunks

    def copy(c):
        at = pl.ds(c * rows, rows)
        return pltpu.make_async_copy(w_hbm.at[:, at], w_buf.at[:, at], sem.at[c])

    for c in range(chunks):
        copy(c).start()
    pi = e_ref.shape[0]
    e = e_ref[...].astype(F32)
    centred = e - jnp.mean(e, -1, keepdims=True)
    hi, lo = split(centred * (1.0 + mod_ref[1:2, :]))
    lhs_ref[0:pi, :] = hi
    lhs_ref[pi : 2 * pi, :] = lo
    shift_hi, shift_lo = split(mod_ref[0:1, :])
    lhs_ref[2 * pi :, :] = jnp.concatenate(
        [shift_hi.astype(F32), shift_lo.astype(F32), jnp.zeros((14, depth), F32)], 0
    ).astype(BF16)
    chi, clo = split(jnp.concatenate([centred, centred], 0))
    gram = dot_nt(chi, chi) + dot_nt(chi, clo) + dot_nt(clo, chi)
    row = lax.broadcasted_iota(jnp.int32, gram.shape, 0) // pi
    col = lax.broadcasted_iota(jnp.int32, gram.shape, 1) // pi
    ghi, glo = split(jnp.where(row == col, gram * (1.0 / depth), 0.0))
    gram_ref[...] = jnp.concatenate([ghi, glo], 0)
    for c in range(chunks):
        copy(c).wait()
        lhs = lhs_ref[:, c * rows : (c + 1) * rows]
        for p in range(parts):
            at = slice(p * width, (p + 1) * width)
            term = dot(lhs, w_buf[p, c * rows : (c + 1) * rows, :])
            if c == 0:
                acc_ref[:, at] = term
            else:
                acc_ref[:, at] += term
    total = acc_ref[...]
    hi, lo = split(total[:pi] + total[pi : 2 * pi])
    none = jnp.zeros_like(hi)
    rhs0_ref[...] = jnp.concatenate([hi, none, lo, none], 0)
    rhs1_ref[...] = jnp.concatenate([none, hi, none, lo], 0)
    shift_ref[...] = total[2 * pi : 2 * pi + 1] + total[2 * pi + 1 : 2 * pi + 2]


def fold(embed_weight, modulation, weight):
    parts, depth, width = weight.shape
    pi = embed_weight.shape[0]
    cols = parts * width
    chunks = 6
    return pl.pallas_call(
        lambda *refs: fold_kernel(chunks, *refs),
        out_shape=(
            jax.ShapeDtypeStruct((4 * pi, cols), BF16),
            jax.ShapeDtypeStruct((4 * pi, cols), BF16),
            jax.ShapeDtypeStruct((1, cols), F32),
            jax.ShapeDtypeStruct((4 * pi, 2 * pi), BF16),
        ),
        in_specs=[vmem_spec(), vmem_spec(), hbm_spec()],
        out_specs=(vmem_spec(),) * 4,
        scratch_shapes=[
            VMEM((parts, depth, width), BF16),
            VMEM((2 * pi + 16, depth), BF16),
            VMEM((2 * pi + 16, cols), F32),
            pltpu.SemaphoreType.DMA((chunks,)),
        ],
        compiler_params=params(),
        cost_estimate=cost(2 * 144 * depth * cols, nbytes(weight, embed_weight, modulation)),
        name="fold",
    )(embed_weight, modulation, weight)


def text_kernel(chunks, text_ref, mod_ref, gain_ref, w_hbm, key_ref, value_ref, w_buf, stream_ref, acc_ref, sem):
    depth, parts, width = w_hbm.shape
    rows = depth // chunks

    def copy(c):
        at = pl.ds(c * rows, rows)
        return pltpu.make_async_copy(w_hbm.at[at], w_buf.at[at], sem.at[c])

    for c in range(chunks):
        copy(c).start()
    text = text_ref[...].astype(F32)
    centred = text - jnp.mean(text, -1, keepdims=True)
    normed = centred * lax.rsqrt(jnp.mean(centred * centred, -1, keepdims=True) + EPS)
    stream_ref[...] = (normed * (1.0 + mod_ref[3:4, :]) + mod_ref[2:3, :]).astype(BF16)
    step = 128
    row = lax.broadcasted_iota(jnp.int32, (2 * step, 2 * step), 0)
    col = lax.broadcasted_iota(jnp.int32, (2 * step, 2 * step), 1)
    pick = jnp.where(col == 2 * (row % step) + row // step, 1.0, 0.0).astype(BF16)
    flat = w_buf.reshape(depth * parts, width)
    for c in range(chunks):
        copy(c).wait()
        pieces = ([], [])
        for s in range(rows // step):
            at = 2 * (c * rows + s * step)
            both = dot(pick, flat[at : at + 2 * step, :]).astype(BF16)
            pieces[0].append(both[:step])
            pieces[1].append(both[step:])
        stream = stream_ref[:, c * rows : (c + 1) * rows]
        for p in range(2):
            term = dot(stream, jnp.concatenate(pieces[p], 0))
            if c == 0:
                acc_ref[p] = term
            else:
                acc_ref[p] += term
    for h in range(width // HS):
        at = slice(h * HS, (h + 1) * HS)
        key = acc_ref[0, :, at]
        scale = lax.rsqrt(jnp.mean(key * key, -1, keepdims=True) + EPS)
        key_ref[h] = (key * scale * gain_ref[1:2, :]).astype(BF16)
        value_ref[h] = acc_ref[1, :, at].astype(BF16)


def text_side(text, modulation, gain, weight):
    depth, parts, width = weight.shape
    count = text.shape[0]
    heads = width // HS
    chunks = 6
    return pl.pallas_call(
        lambda *refs: text_kernel(chunks, *refs),
        out_shape=(jax.ShapeDtypeStruct((heads, count, HS), BF16),) * 2,
        in_specs=[vmem_spec(), vmem_spec(), vmem_spec(), hbm_spec()],
        out_specs=(vmem_spec(),) * 2,
        scratch_shapes=[
            VMEM((depth, parts, width), BF16),
            VMEM((count, depth), BF16),
            VMEM((parts, count, width), F32),
            pltpu.SemaphoreType.DMA((chunks,)),
        ],
        compiler_params=params(),
        cost_estimate=cost(4 * count * depth * parts * width, nbytes(weight, text, modulation)),
        name="text_side",
    )(text, modulation, gain, weight)


def conv_kernel(video_ref, halo_ref, weight_ref, latent_ref, out_ref, wide_ref, even_ref, odd_ref, left_ref, spread_ref):
    frames, rows, cols, chans = video_ref.shape
    block = cols + 8
    half = cols // 2
    quarter = cols // 4
    for r in range(rows + 1):
        for f in range(frames):
            base = (r * frames + f) * block
            pixels = halo_ref[f, 0] if r == 0 else video_ref[f, r - 1]
            wide_ref[base : base + 8, :] = jnp.zeros((8, chans), F32)
            wide_ref[base + 8 : base + block, :] = pixels.astype(F32)
            at = [wide_ref[pl.ds(base + 7 + o, quarter, stride=4), :] for o in range(5)]
            even = jnp.concatenate([at[1], at[3]], 0).astype(BF16)
            odd = jnp.concatenate([at[2], at[4]], 0).astype(BF16)
            left = jnp.concatenate([at[0], at[2]], 0).astype(BF16)
            for t in (range(3) if f == 0 else (f + 2,)):
                even_ref[r, t] = even
                odd_ref[r, t] = odd
                left_ref[r, t] = left
    lat, mid = latent_ref.shape
    tall = rows // 2
    spread_ref[...] = jnp.zeros_like(spread_ref)
    for s in range(2 * tall):
        spread_ref[s * lat : (s + 1) * lat, s * mid : (s + 1) * mid] = latent_ref[...]
    pieces = []
    for j in range(tall):
        taps = []
        for kt in range(3):
            for kr in range(3):
                for ref in (left_ref, even_ref, odd_ref):
                    taps.append(ref[2 * j + kr, kt : kt + frames].reshape(frames * half, chans))
        conv = dot(jnp.concatenate(taps, 1), weight_ref[...])
        act = (conv * (1.0 / (1.0 + jnp.exp(-conv)))).astype(BF16)
        for b in range(2):
            pieces.append(
                jnp.concatenate(
                    [act[f * half + b * quarter : f * half + (b + 1) * quarter] for f in range(frames)], 0
                )
            )
    out_ref[...] = dot_nt(jnp.concatenate(pieces, 1), spread_ref[...]).astype(BF16)


def conv_side(video, halo, conv_weight, latent_weight):
    frames, rows, cols, chans = video.shape
    mid = conv_weight.shape[-1]
    lat = latent_weight.shape[1]
    weight = conv_weight.reshape(-1, mid)
    latent = latent_weight.T
    half = cols // 2
    tall = rows // 2
    return pl.pallas_call(
        conv_kernel,
        out_shape=jax.ShapeDtypeStruct((frames * half // 2, 2 * tall * lat), BF16),
        in_specs=[vmem_spec()] * 4,
        out_specs=vmem_spec(),
        scratch_shapes=[VMEM(((rows + 1) * frames * (cols + 8), chans), F32)]
        + [VMEM((rows + 1, frames + 2, half, chans), BF16)] * 3
        + [VMEM((2 * tall * lat, 2 * tall * mid), BF16)],
        compiler_params=params(),
        cost_estimate=cost(2 * frames * tall * half * 27 * chans * mid, nbytes(video, halo, weight)),
        name="conv_side",
    )(video, halo, weight, latent)


def qkv_kernel(order, frames, *refs):
    n = len(order)
    me_ref = refs[0]
    patch_refs = refs[1 : 1 + n]
    rhs_refs = refs[1 + n : 3 + n]
    shift_ref, gram_ref, gain_ref, tkey_ref, tvalue_ref = refs[3 + n : 8 + n]
    query_refs = refs[8 + n : 8 + 2 * n]
    key_ref, value_ref, patch_scr = refs[8 + 2 * n :]
    me = me_ref[0]
    heads, count, _ = tkey_ref.shape
    rows = patch_refs[0].shape[0]
    for k, ref in zip(order, patch_refs):
        patch_scr[pl.ds(pl.multiple_of((me ^ k) * rows, rows), rows), :] = ref[...]
    for h in range(heads):
        key_ref[h, 0:count, :] = tkey_ref[h]
        value_ref[h, 0:count, :] = tvalue_ref[h]
    own = frames // n
    span = rows // n
    grain = span // own
    pieces = []
    for k in order:
        for s in range(n):
            at = pl.multiple_of((me ^ k) * span, span) + s * rows
            pieces.append(patch_scr[pl.ds(pl.multiple_of(at, span), span), :])
    x = jnp.concatenate(pieces, 0)
    xx = jnp.concatenate([x, x], 1)
    quad = dot(xx, gram_ref[...]) * x.astype(F32)
    lane = lax.broadcasted_iota(jnp.int32, quad.shape, 1)
    low = lane < quad.shape[1] // 2
    width = heads * HS
    gain_q = gain_ref[0:1, :] * (math.log2(math.e) / math.sqrt(HS))
    gain_k = gain_ref[1:2, :]
    for i in range(2):
        var = jnp.sum(jnp.where(low if i == 0 else ~low, quad, 0.0), -1, keepdims=True)
        rstd = lax.rsqrt(jnp.maximum(var, 0.0) + EPS)
        for p in range(3):
            for h0 in range(0, heads, 2):
                at = slice(p * width + h0 * HS, p * width + (h0 + 2) * HS)
                pair = dot(xx, rhs_refs[i][:, at]) * rstd + shift_ref[:, at]
                for h in (h0, h0 + 1):
                    v = pair[:, (h - h0) * HS : (h - h0 + 1) * HS]
                    if p < 2:
                        v = v * lax.rsqrt(jnp.mean(v * v, -1, keepdims=True) + EPS)
                        v = v * (gain_q if p == 0 else gain_k)
                    v = v.astype(BF16)
                    for k in range(n):
                        block = v[k * rows : (k + 1) * rows]
                        if p == 0:
                            for s in range(n):
                                for f in range(own):
                                    to = f * (n * 2 * grain) + (s * 2 + i) * grain
                                    come = s * span + f * grain
                                    query_refs[k][h, to : to + grain, :] = block[come : come + grain]
                        else:
                            ref = key_ref if p == 1 else value_ref
                            to = count + (2 * k + i) * rows
                            ref[h, to : to + rows, :] = block


def qkv_side(order, frames, me, patches, rhs0, rhs1, shift, gram, gain, tkey, tvalue):
    n = len(order)
    heads, count, _ = tkey.shape
    rows = patches[0].shape[0]
    total = count + 2 * n * rows
    outs = pl.pallas_call(
        lambda *refs: qkv_kernel(order, frames, *refs),
        out_shape=(jax.ShapeDtypeStruct((heads, 2 * rows, HS), BF16),) * n
        + (jax.ShapeDtypeStruct((heads, total, HS), BF16),) * 2,
        in_specs=[smem_spec()] + [vmem_spec()] * (n + 7),
        out_specs=(vmem_spec(),) * (n + 2),
        scratch_shapes=[VMEM((n * rows, rows), BF16)],
        compiler_params=params(),
        cost_estimate=cost(2 * 2 * n * rows * 256 * 3 * heads * HS, 4 * nbytes(rhs0)),
        name="qkv_side",
    )(me, *patches, rhs0, rhs1, shift, gram, gain, tkey, tvalue)
    return outs[:n], outs[n], outs[n + 1]


def attend_kernel(query_ref, key_ref, value_ref, out_ref):
    heads, total, _ = key_ref.shape
    step = 256
    for h in range(heads):
        query = query_ref[h]
        acc = None
        for c in range(0, total, step):
            logits = dot_nt(query, key_ref[h, c : c + step, :])
            weights = jnp.exp2(logits)
            fold_sum = weights[:, :HS] + weights[:, HS:]
            term = dot(weights.astype(BF16), value_ref[h, c : c + step, :])
            if acc is None:
                acc, norm = term, fold_sum
            else:
                acc, norm = acc + term, norm + fold_sum
        norm = jnp.sum(norm, -1, keepdims=True)
        out_ref[:, h * HS : (h + 1) * HS] = (acc / norm).astype(BF16)


def attend(query, key, value):
    heads, rows, _ = query.shape
    total = key.shape[1]
    return pl.pallas_call(
        attend_kernel,
        out_shape=jax.ShapeDtypeStruct((rows, heads * HS), BF16),
        in_specs=[vmem_spec()] * 3,
        out_specs=vmem_spec(),
        compiler_params=params(),
        cost_estimate=cost(
            4 * heads * rows * total * HS, nbytes(query, key, value), heads * rows * total
        ),
        name="attend",
    )(query, key, value)


def gather_kernel(order, me_ref, *refs):
    n = len(order)
    out_ref, sem = refs[n:]
    width = refs[0].shape[1]
    copies = []
    for j, k in enumerate(order):
        at = pl.multiple_of((me_ref[0] ^ k) * width, width)
        copies.append(pltpu.make_async_copy(refs[j], out_ref.at[:, pl.ds(at, width)], sem.at[j]))
    for c in copies:
        c.start()
    for c in copies:
        c.wait()


def side_by_side(order, me, blocks):
    n = len(order)
    rows, width = blocks[0].shape
    return pl.pallas_call(
        lambda *refs: gather_kernel(order, *refs),
        out_shape=jax.ShapeDtypeStruct((rows, n * width), BF16),
        in_specs=[smem_spec()] + [hbm_spec()] * n,
        out_specs=hbm_spec(),
        scratch_shapes=[pltpu.SemaphoreType.DMA((n,))],
        cost_estimate=cost(0, 2 * n * nbytes(blocks[0])),
        name="side_by_side",
    )(me, *blocks)


def shards(video, conv_weight, latent_weight, embed_weight, modulation, qkv_weight, qk_gain, text, text_weight):
    n = lax.axis_size("ctx")
    frames = video.shape[0]
    me = lax.axis_index("ctx").astype(jnp.int32).reshape(1)

    def swap(x, k):
        return lax.ppermute(x, "ctx", [(i, i ^ k) for i in range(n)])

    halo = lax.ppermute(video[:, -1:], "ctx", [(i, i + 1) for i in range(n - 1)])
    rhs0, rhs1, shift, gram = fold(embed_weight, modulation, qkv_weight.transpose(1, 0, 2))
    patches = conv_side(video, halo, conv_weight, latent_weight)
    order = tuple(range(n - 1, -1, -1))
    received = [swap(patches, k) if k else patches for k in order]
    tkey, tvalue = text_side(text, modulation, qk_gain, text_weight)
    queries, key, value = qkv_side(
        order, frames, me, received, rhs0, rhs1, shift, gram, qk_gain, tkey, tvalue
    )
    blocks = []
    for query, k in zip(queries, order):
        block = attend(query, key, value)
        blocks.append(swap(block, k) if k else block)
    return side_by_side(order, me, blocks)


def solution(mesh):
    in_specs = (
        P("dp", "ctx", None, None),
        P(),
        P(),
        P(),
        P("dp", None),
        P(None, None, "ctx"),
        P(),
        P("dp", None),
        P(None, None, "ctx"),
    )
    out_specs = P(("dp", "ctx"), None)
    return jax.shard_map(shards, mesh=mesh, in_specs=in_specs, out_specs=out_specs, check_vma=False)
```

time: 193 us -> 97.3 us (0.50)
  Pallas kernels: 0 us -> 76.5 us
  matrix products: 49.2 us -> 0 us
  local copies, waits for them, and re-layouts: 49.8 us -> 2.89 us
  waiting for transfers between devices: 42.6 us -> 5.48 us
  blocking collectives: 17.7 us -> 0 us
  between operations: 13.7 us -> 0.27 us
  other arithmetic: 9.49 us -> 0 us
  starting transfers between devices: 9.56 us -> 11.8 us
    pallas_call x0 -> x9, Pallas kernels: none -> 76.5 us  [the longest x1 32.9 us: side_by_side(): pl.pallas_call(lambda *refs: gather_kernel(order, *refs), out_shape=jax.S...]
    all_gather x1 -> x0, waiting for transfers between devices: 35.2 us -> none  [shards(): lax.all_gather(stream, 'ctx', axis=0, tiled=True)]
    dot_general x6 -> x0, matrix products: 30.3 us -> none  [the longest x1 13.3 us: shards(): jnp.dot(lax.all_gather(stream, 'ctx', axis=0, tiled=True), flat_weight, p...]
    unnamed x21 -> x18, local copies, waits for them, and re-layouts: 21.3 us -> 1.98 us
    all_to_all x1 -> x0, blocking collectives: 17.7 us -> none  [shards(): lax.all_to_all(result, 'ctx', split_axis=0, concat_axis=1, tiled=True)]
    sub x2 -> x0, matrix products: 16.3 us -> none  [attend(): expd = jnp.exp(logits - jnp.max(logits, -1, keepdims=True))]
    dot_general x1 -> x0, local copies, waits for them, and re-layouts: 8.79 us -> none  [shards(): jnp.dot(text_stream, text_weight.reshape(D, -1), preferred_element_type=j...]
    conv_general_dilated x4 -> x0, local copies, waits for them, and re-layouts: 7.91 us -> none  [shards(): lax.conv_general_dilated(framed[None], conv_weight, (1, 2, 2), 'VALID', d...]
  transfers between devices with their start and end apart: 3 -> 7, of which waited for: 3 -> 3; matrix products, arithmetic and copies ran while one was open for 18% -> 0% of each run, Pallas kernels for 0% -> 20%
where the time goes in v1:
time: 97.3 us; the launch traced here: 97 us
  Pallas kernels  76.5 us (79%)
  starting transfers between devices  11.8 us (12%)
  waiting for transfers between devices  5.48 us (6%)
  local copies, waits for them, and re-layouts  2.89 us (3%)
    pallas_call x1, Pallas kernels, side_by_side(): pl.pallas_call(lambda *refs: gather_kernel(order, *refs), out_shape=jax.S...  32.9 us
    pallas_call x4, Pallas kernels, attend(): pl.pallas_call(attend_kernel, out_shape=jax.ShapeDtypeStruct((rows, heads...  19.4 us
    pallas_call x1, Pallas kernels, text_side(): pl.pallas_call(lambda *refs: text_kernel(chunks, *refs), out_shape=(jax.S...  7.38 us
    ppermute x6, starting transfers between devices, swap(): return lax.ppermute(x, 'ctx', [(i, i ^ k) for i in range(n)])  6.98 us
    pallas_call x1, Pallas kernels, fold(): pl.pallas_call(lambda *refs: fold_kernel(chunks, *refs), out_shape=(jax.S...  6.85 us
    ppermute x6, waiting for transfers between devices, swap(): return lax.ppermute(x, 'ctx', [(i, i ^ k) for i in range(n)])  5.48 us
    pallas_call x1, Pallas kernels, qkv_side(): pl.pallas_call(lambda *refs: qkv_kernel(order, frames, *refs), out_shape=...  5.02 us
    pallas_call x1, Pallas kernels, conv_side(): pl.pallas_call(conv_kernel, out_shape=jax.ShapeDtypeStruct((frames * half...  4.98 us
  transfers between devices with their start and end apart: 7, of which 3 were waited for; matrix products, arithmetic and copies ran while one was open for 0% of the time, Pallas kernels for 20%

profile of v1, /device:TPU:0, one launch (start us, length us, event | category | flops | bytes accessed | tf_op | source)
XLA Modules:
  0.0 97.0 jit_solution(10975869856730066374)
XLA Ops:
  0.0 0.9 slice.3
  0.9 4.8 %collective-permute-start = (bf16[8,1,64,128]{3,2,1,0:T(8,128)(2,1)S(1)}, bf16[8,1,64,128]{3,2,1,0:T(8,128)(2,1)S(1)}, u32[]{:S(2)}, u32[]{:S(2)}) collective-permute-start(bf16[8,1,64,128]{3,2,1,0:T(8,128)(2,1)S(1)} %slice.3), channel_id=1, source_target_pairs={{0,1},{1,2},{2,3},{4,5},{5,6},{6,7},{8,9},{9,10},{10,11},{12,13},{... | collective-permute-start | bytes 393224 | tf_op jit(solution)/shard_map/ppermute | solution.py:405
  5.8 7.4 %text_side.1 = (bf16[4,256,128]{2,1,0:T(8,128)(2,1)}, bf16[4,256,128]{2,1,0:T(8,128)(2,1)}) custom-call(bf16[256,3072]{1,0:T(8,128)(2,1)} %refs_0_.3, f32[4,3072]{1,0:T(4,128)} %refs_1_.3, f32[2,128]{1,0:T(2,128)} %refs_9_.1, bf16[3072,2,512]{2,1,0:T(2,128)(2,1)} %refs_3_.1), custom_call_target="tpu_custom_call" | custom-call | flops 3221225472 | bytes 7913472 | tf_op jit(solution)/shard_map/text_side/pallas_call | solution.py:175
  13.2 0.0 collective-permute-done.halo_ref
  13.2 0.0 copy-start.5
  13.2 0.6 copy-done.5
  13.8 5.0 %conv_side.1.refs_4_ = bf16[128,128]{1,0:T(8,128)(2,1)} custom-call(bf16[8,8,64,128]{3,2,1,0:T(8,128)(2,1)} %video_ref.1, bf16[8,1,64,128]{3,2,1,0:T(8,128)(2,1)} %copy-done.5, bf16[3456,256]{1,0:T(8,128)(2,1)} %bitcast.5, bf16[16,256]{1,0:T(8,128)(2,1)} %bitcast.6), custom_call_target="tpu_custom_call" | custom-call | flops 1811939328 | bytes 2949120 | tf_op jit(solution)/shard_map/conv_side/pallas_call | solution.py:242
  18.8 1.5 %collective-permute-start.3 = (bf16[128,128]{1,0:T(8,128)(2,1)}, bf16[128,128]{1,0:T(8,128)(2,1)S(1)}, u32[]{:S(2)}, u32[]{:S(2)}) collective-permute-start(bf16[128,128]{1,0:T(8,128)(2,1)} %conv_side.1.refs_4_), channel_id=1, source_target_pairs={{0,1},{1,0},{2,3},{3,2},{4,5},{5,4},{6,7},{7,6},{8,9},{9,8},{10,11... | collective-permute-start | bytes 98312 | tf_op jit(solution)/shard_map/ppermute | solution.py:403
  20.3 0.0 collective-permute-start.2
  20.3 2.0 %collective-permute-start.1 = (bf16[128,128]{1,0:T(8,128)(2,1)}, bf16[128,128]{1,0:T(8,128)(2,1)S(1)}, u32[]{:S(2)}, u32[]{:S(2)}) collective-permute-start(bf16[128,128]{1,0:T(8,128)(2,1)} %conv_side.1.refs_4_), channel_id=1, source_target_pairs={{0,3},{1,2},{2,1},{3,0},{4,7},{5,6},{6,5},{7,4},{8,11},{9,10},{10,... | collective-permute-start | bytes 98312 | tf_op jit(solution)/shard_map/ppermute | solution.py:403
  22.3 6.9 %fold.1 = (bf16[256,1536]{1,0:T(8,128)(2,1)}, bf16[256,1536]{1,0:T(8,128)(2,1)}, f32[1,1536]{1,0:T(1,128)}, bf16[256,128]{1,0:T(8,128)(2,1)}) custom-call(bf16[64,3072]{1,0:T(8,128)(2,1)} %refs_0_.2, f32[4,3072]{1,0:T(4,128)} %refs_1_.3, bf16[3,3072,512]{2,1,0:T(8,128)(2,1)} %bitcast.4), custom_call_target="tpu_custom_call" | custom-call | flops 1358954496 | bytes 9879552 | tf_op jit(solution)/shard_map/fold/pallas_call | solution.py:106
  29.2 0.0 collective-permute-done.3.refs_3_
  29.2 0.0 copy-start.6
  29.2 0.0 collective-permute-done.2.refs_2_
  29.2 0.0 copy-start.7
  29.2 0.0 collective-permute-done.1.refs_1_
  29.2 0.0 copy-start.8
  29.2 0.6 copy-done.6
  29.8 0.0 copy-done.7
  29.8 0.0 copy-done.8
  29.8 5.0 %qkv_side.1 = (bf16[4,256,128]{2,1,0:T(8,128)(2,1)}, bf16[4,256,128]{2,1,0:T(8,128)(2,1)}, bf16[4,256,128]{2,1,0:T(8,128)(2,1)}, bf16[4,256,128]{2,1,0:T(8,128)(...) custom-call(s32[1]{0:T(128)} %bitcast.refs_0_, bf16[128,128]{1,0:T(8,128)(2,1)} %copy-done.8, ...), custom_call_target="tpu_custom_call" | custom-call | flops 805306368 | bytes 3145728 | tf_op jit(solution)/shard_map/qkv_side/pallas_call | solution.py:320
  34.9 4.9 %attend.4 = bf16[256,512]{1,0:T(8,128)(2,1)} custom-call(bf16[4,256,128]{2,1,0:T(8,128)(2,1)} %get-tuple-element.23.query_ref, bf16[4,1280,128]{2,1,0:T(8,128)(2,1)} %get-tuple-element.24.key_ref, bf16[4,1280,128]{2,1,0:T(8,128)(2,1)} %get-tuple-element.25.value_ref), custom_call_target="tpu_custom_call" | custom-call | flops 671088640 | bytes 2883584 | tf_op jit(solution)/shard_map/attend/pallas_call | solution.py:356
  39.8 4.8 %attend.5 = bf16[256,512]{1,0:T(8,128)(2,1)} custom-call(bf16[4,256,128]{2,1,0:T(8,128)(2,1)} %get-tuple-element.26.query_ref, bf16[4,1280,128]{2,1,0:T(8,128)(2,1)} %get-tuple-element.24.key_ref, bf16[4,1280,128]{2,1,0:T(8,128)(2,1)} %get-tuple-element.25.value_ref), custom_call_target="tpu_custom_call" | custom-call | flops 671088640 | bytes 2883584 | tf_op jit(solution)/shard_map/attend/pallas_call | solution.py:356
  44.6 0.0 copy-start.2
  44.6 0.0 copy-start
  44.6 4.8 %attend.6 = bf16[256,512]{1,0:T(8,128)(2,1)} custom-call(bf16[4,256,128]{2,1,0:T(8,128)(2,1)} %get-tuple-element.27.query_ref, bf16[4,1280,128]{2,1,0:T(8,128)(2,1)} %get-tuple-element.24.key_ref, bf16[4,1280,128]{2,1,0:T(8,128)(2,1)} %get-tuple-element.25.value_ref), custom_call_target="tpu_custom_call" | custom-call | flops 671088640 | bytes 2883584 | tf_op jit(solution)/shard_map/attend/pallas_call | solution.py:356
  49.4 1.5 %collective-permute-start.6 = (bf16[256,512]{1,0:T(8,128)(2,1)}, bf16[256,512]{1,0:T(8,128)(2,1)S(1)}, u32[]{:S(2)}, u32[]{:S(2)}) collective-permute-start(bf16[256,512]{1,0:T(8,128)(2,1)} %attend.6), channel_id=1, source_target_pairs={{0,1},{1,0},{2,3},{3,2},{4,5},{5,4},{6,7},{7,6},{8,9},{9,8},{10,11... | collective-permute-start | bytes 786440 | tf_op jit(solution)/shard_map/ppermute | solution.py:403
  50.9 0.0 copy-done.2
  50.9 0.0 collective-permute-start.5
  51.0 0.0 copy-done
  51.0 1.9 %collective-permute-start.4 = (bf16[256,512]{1,0:T(8,128)(2,1)S(1)}, bf16[256,512]{1,0:T(8,128)(2,1)S(1)}, u32[]{:S(2)}, u32[]{:S(2)}) collective-permute-start(bf16[256,512]{1,0:T(8,128)(2,1)S(1)} %copy-done), channel_id=1, source_target_pairs={{0,3},{1,2},{2,1},{3,0},{4,7},{5,6},{6,5},{7,4},{8,11},{9,10},{10,... | collective-permute-start | bytes 786440 | tf_op jit(solution)/shard_map/ppermute | solution.py:403
  52.9 4.8 %attend.7.refs_4_ = bf16[256,512]{1,0:T(8,128)(2,1)} custom-call(bf16[4,256,128]{2,1,0:T(8,128)(2,1)} %get-tuple-element.28.query_ref, bf16[4,1280,128]{2,1,0:T(8,128)(2,1)} %get-tuple-element.24.key_ref, bf16[4,1280,128]{2,1,0:T(8,128)(2,1)} %get-tuple-element.25.value_ref), custom_call_target="tpu_custom_call" | custom-call | flops 671088640 | bytes 2883584 | tf_op jit(solution)/shard_map/attend/pallas_call | solution.py:356
  57.7 1.2 %collective-permute-done.6.refs_3_ = bf16[256,512]{1,0:T(8,128)(2,1)S(1)} collective-permute-done((bf16[256,512]{1,0:T(8,128)(2,1)}, bf16[256,512]{1,0:T(8,128)(2,1)S(1)}, u32[]{:S(2)}, u32[]{:S(2)}) %collective-permute-start.6) | collective-permute-done | bytes 262176 | tf_op jit(solution)/shard_map/ppermute | solution.py:403
  58.9 0.0 copy-start.1
  58.9 1.0 %collective-permute-done.5.refs_2_ = bf16[256,512]{1,0:T(8,128)(2,1)S(1)} collective-permute-done((bf16[256,512]{1,0:T(8,128)(2,1)S(1)}, bf16[256,512]{1,0:T(8,128)(2,1)S(1)}, u32[]{:S(2)}, u32[]{:S(2)}) %collective-permute-start.5) | collective-permute-done | bytes 262176 | tf_op jit(solution)/shard_map/ppermute | solution.py:403
  59.9 0.0 copy-start.3
  59.9 3.3 %collective-permute-done.4.refs_1_ = bf16[256,512]{1,0:T(8,128)(2,1)S(1)} collective-permute-done((bf16[256,512]{1,0:T(8,128)(2,1)S(1)}, bf16[256,512]{1,0:T(8,128)(2,1)S(1)}, u32[]{:S(2)}, u32[]{:S(2)}) %collective-permute-start.4) | collective-permute-done | bytes 262176 | tf_op jit(solution)/shard_map/ppermute | solution.py:403
  63.2 0.0 copy-done.1
  63.2 0.0 copy-done.3
  63.2 0.0 copy-start.4
  63.2 0.7 copy-done.4
  63.9 32.9 %side_by_side.1 = bf16[256,2048]{1,0:T(8,128)(2,1)} custom-call(s32[1]{0:T(128)} %bitcast.refs_0_, bf16[256,512]{1,0:T(8,128)(2,1)} %copy-done.4, bf16[256,512]{1,0:T(8,128)(2,1)} %copy-done.3, bf16[256,512]{1,0:T(8,128)(2,1)} %copy-done.1, bf16[256,512]{1,0:T(8,128)(2,1)} %attend.7.refs_4_), custom_call_target="tpu_custom_call" | custom-call | bytes 2097152 | tf_op jit(solution)/shard_map/side_by_side/pallas_call | solution.py:386
Async XLA Ops:
  0.9 12.2 %collective-permute-start = (bf16[8,1,64,128]{3,2,1,0:T(8,128)(2,1)S(1)}, bf16[8,1,64,128]{3,2,1,0:T(8,128)(2,1)S(1)}, u32[]{:S(2)}, u32[]{:S(2)}) collective-permute-start(bf16[8,1,64,128]{3,2,1,0:T(8,128)(2,1)S(1)} %slice.3), channel_id=1, source_target_pairs={{0,1},{1,2},{2,3},{4,5},{5,6},{6,7},{8,9},{9,10},{10,11},{12,13},{... | collective-permute-start | bytes 393224 | tf_op jit(solution)/shard_map/ppermute | solution.py:405
  13.2 0.7 copy-start.5
  18.8 10.4 %collective-permute-start.3 = (bf16[128,128]{1,0:T(8,128)(2,1)}, bf16[128,128]{1,0:T(8,128)(2,1)S(1)}, u32[]{:S(2)}, u32[]{:S(2)}) collective-permute-start(bf16[128,128]{1,0:T(8,128)(2,1)} %conv_side.1.refs_4_), channel_id=1, source_target_pairs={{0,1},{1,0},{2,3},{3,2},{4,5},{5,4},{6,7},{7,6},{8,9},{9,8},{10,11... | collective-permute-start | bytes 98312 | tf_op jit(solution)/shard_map/ppermute | solution.py:403
  20.3 8.9 %collective-permute-start.2 = (bf16[128,128]{1,0:T(8,128)(2,1)}, bf16[128,128]{1,0:T(8,128)(2,1)S(1)}, u32[]{:S(2)}, u32[]{:S(2)}) collective-permute-start(bf16[128,128]{1,0:T(8,128)(2,1)} %conv_side.1.refs_4_), channel_id=1, source_target_pairs={{0,2},{1,3},{2,0},{3,1},{4,6},{5,7},{6,4},{7,5},{8,10},{9,11},{10,... | collective-permute-start | bytes 98312 | tf_op jit(solution)/shard_map/ppermute | solution.py:403
  20.3 8.9 %collective-permute-start.1 = (bf16[128,128]{1,0:T(8,128)(2,1)}, bf16[128,128]{1,0:T(8,128)(2,1)S(1)}, u32[]{:S(2)}, u32[]{:S(2)}) collective-permute-start(bf16[128,128]{1,0:T(8,128)(2,1)} %conv_side.1.refs_4_), channel_id=1, source_target_pairs={{0,3},{1,2},{2,1},{3,0},{4,7},{5,6},{6,5},{7,4},{8,11},{9,10},{10,... | collective-permute-start | bytes 98312 | tf_op jit(solution)/shard_map/ppermute | solution.py:403
  29.2 0.6 copy-start.6
  29.2 0.6 copy-start.7
  29.2 0.6 copy-start.8
  44.6 6.3 %copy-start.2 = (bf16[256,512]{1,0:T(8,128)(2,1)S(1)}, bf16[256,512]{1,0:T(8,128)(2,1)}, u32[]{:S(2)}) copy-start(bf16[256,512]{1,0:T(8,128)(2,1)} %attend.5) | copy-start | bytes 786436
  44.6 6.4 %copy-start = (bf16[256,512]{1,0:T(8,128)(2,1)S(1)}, bf16[256,512]{1,0:T(8,128)(2,1)}, u32[]{:S(2)}) copy-start(bf16[256,512]{1,0:T(8,128)(2,1)} %attend.4) | copy-start | bytes 786436
  49.4 9.5 %collective-permute-start.6 = (bf16[256,512]{1,0:T(8,128)(2,1)}, bf16[256,512]{1,0:T(8,128)(2,1)S(1)}, u32[]{:S(2)}, u32[]{:S(2)}) collective-permute-start(bf16[256,512]{1,0:T(8,128)(2,1)} %attend.6), channel_id=1, source_target_pairs={{0,1},{1,0},{2,3},{3,2},{4,5},{5,4},{6,7},{7,6},{8,9},{9,8},{10,11... | collective-permute-start | bytes 786440 | tf_op jit(solution)/shard_map/ppermute | solution.py:403
  50.9 9.0 %collective-permute-start.5 = (bf16[256,512]{1,0:T(8,128)(2,1)S(1)}, bf16[256,512]{1,0:T(8,128)(2,1)S(1)}, u32[]{:S(2)}, u32[]{:S(2)}) collective-permute-start(bf16[256,512]{1,0:T(8,128)(2,1)S(1)} %copy-done.2), channel_id=1, source_target_pairs={{0,2},{1,3},{2,0},{3,1},{4,6},{5,7},{6,4},{7,5},{8,10},{9,11},{10,... | collective-permute-start | bytes 786440 | tf_op jit(solution)/shard_map/ppermute | solution.py:403
  51.0 12.2 %collective-permute-start.4 = (bf16[256,512]{1,0:T(8,128)(2,1)S(1)}, bf16[256,512]{1,0:T(8,128)(2,1)S(1)}, u32[]{:S(2)}, u32[]{:S(2)}) collective-permute-start(bf16[256,512]{1,0:T(8,128)(2,1)S(1)} %copy-done), channel_id=1, source_target_pairs={{0,3},{1,2},{2,1},{3,0},{4,7},{5,6},{6,5},{7,4},{8,11},{9,10},{10,... | collective-permute-start | bytes 786440 | tf_op jit(solution)/shard_map/ppermute | solution.py:403
  58.9 4.3 %copy-start.1 = (bf16[256,512]{1,0:T(8,128)(2,1)}, bf16[256,512]{1,0:T(8,128)(2,1)S(1)}, u32[]{:S(2)}) copy-start(bf16[256,512]{1,0:T(8,128)(2,1)S(1)} %collective-permute-done.6.refs_3_) | copy-start | bytes 786436
  59.9 3.3 %copy-start.3 = (bf16[256,512]{1,0:T(8,128)(2,1)}, bf16[256,512]{1,0:T(8,128)(2,1)S(1)}, u32[]{:S(2)}) copy-start(bf16[256,512]{1,0:T(8,128)(2,1)S(1)} %collective-permute-done.5.refs_2_) | copy-start | bytes 786436
  63.2 0.7 copy-start.4

commit v2 on v1

--- a/solution.py
+++ b/solution.py
@@ -12,7 +12,7 @@
 F32 = jnp.float32
 BF16 = jnp.bfloat16
 VMEM = pltpu.VMEM
-VMEM_LIMIT = 56 * 1024 * 1024
+MIB = 1024 * 1024
 
 
 def vmem_spec():
@@ -20,15 +20,15 @@
 
 
 def hbm_spec():
-    return pl.BlockSpec(memory_space=pl.ANY)
+    return pl.BlockSpec(memory_space=pltpu.HBM)
 
 
 def smem_spec():
     return pl.BlockSpec(memory_space=pltpu.SMEM)
 
 
-def params():
-    return pltpu.CompilerParams(vmem_limit_bytes=VMEM_LIMIT)
+def params(mib):
+    return pltpu.CompilerParams(vmem_limit_bytes=mib * MIB)
 
 
 def cost(flops, bytes_accessed, transcendentals=0):
@@ -54,16 +54,57 @@
     return lax.dot_general(a, b, (((1,), (1,)), ((), ())), preferred_element_type=F32)
 
 
-def fold_kernel(chunks, e_ref, mod_ref, w_hbm, rhs0_ref, rhs1_ref, shift_ref, gram_ref, w_buf, lhs_ref, acc_ref, sem):
+def fold_kernel(
+    chunks,
+    e_hbm,
+    mod_hbm,
+    w_hbm,
+    text_hbm,
+    video_hbm,
+    conv_hbm,
+    rhs0_ref,
+    rhs1_ref,
+    shift_ref,
+    gram_ref,
+    stream_ref,
+    video_ref,
+    conv_ref,
+    e_ref,
+    mod_ref,
+    text_ref,
+    w_buf,
+    lhs_ref,
+    acc_ref,
+    sem,
+    w_sem,
+):
     parts, depth, width = w_hbm.shape
     rows = depth // chunks
+    small = [
+        pltpu.make_async_copy(src, dst, sem.at[i])
+        for i, (src, dst) in enumerate(
+            (
+                (e_hbm, e_ref),
+                (mod_hbm, mod_ref),
+                (text_hbm, text_ref),
+                (video_hbm, video_ref),
+                (conv_hbm, conv_ref),
+            )
+        )
+    ]
 
     def copy(c):
         at = pl.ds(c * rows, rows)
-        return pltpu.make_async_copy(w_hbm.at[:, at], w_buf.at[:, at], sem.at[c])
-
+        return pltpu.make_async_copy(w_hbm.at[:, at], w_buf.at[:, at], w_sem.at[c])
+
+    small[0].start()
+    small[1].start()
     for c in range(chunks):
         copy(c).start()
+    for c in small[2:]:
+        c.start()
+    small[0].wait()
+    small[1].wait()
     pi = e_ref.shape[0]
     e = e_ref[...].astype(F32)
     centred = e - jnp.mean(e, -1, keepdims=True)
@@ -96,9 +137,16 @@
     rhs0_ref[...] = jnp.concatenate([hi, none, lo, none], 0)
     rhs1_ref[...] = jnp.concatenate([none, hi, none, lo], 0)
     shift_ref[...] = total[2 * pi : 2 * pi + 1] + total[2 * pi + 1 : 2 * pi + 2]
-
-
-def fold(embed_weight, modulation, weight):
+    small[2].wait()
+    text = text_ref[...].astype(F32)
+    centred = text - jnp.mean(text, -1, keepdims=True)
+    normed = centred * lax.rsqrt(jnp.mean(centred * centred, -1, keepdims=True) + EPS)
+    stream_ref[...] = (normed * (1.0 + mod_ref[3:4, :]) + mod_ref[2:3, :]).astype(BF16)
+    small[3].wait()
+    small[4].wait()
+
+
+def fold(embed_weight, modulation, weight, text, video, conv_weight):
     parts, depth, width = weight.shape
     pi = embed_weight.shape[0]
     cols = parts * width
@@ -110,49 +158,46 @@
             jax.ShapeDtypeStruct((4 * pi, cols), BF16),
             jax.ShapeDtypeStruct((1, cols), F32),
             jax.ShapeDtypeStruct((4 * pi, 2 * pi), BF16),
+            jax.ShapeDtypeStruct(text.shape, BF16),
+            jax.ShapeDtypeStruct(video.shape, BF16),
+            jax.ShapeDtypeStruct(conv_weight.shape, BF16),
         ),
-        in_specs=[vmem_spec(), vmem_spec(), hbm_spec()],
-        out_specs=(vmem_spec(),) * 4,
+        in_specs=[hbm_spec()] * 6,
+        out_specs=(vmem_spec(),) * 7,
         scratch_shapes=[
+            VMEM(embed_weight.shape, BF16),
+            VMEM(modulation.shape, F32),
+            VMEM(text.shape, BF16),
             VMEM((parts, depth, width), BF16),
             VMEM((2 * pi + 16, depth), BF16),
             VMEM((2 * pi + 16, cols), F32),
+            pltpu.SemaphoreType.DMA((5,)),
             pltpu.SemaphoreType.DMA((chunks,)),
         ],
-        compiler_params=params(),
-        cost_estimate=cost(2 * 144 * depth * cols, nbytes(weight, embed_weight, modulation)),
+        compiler_params=params(32),
+        cost_estimate=cost(
+            2 * 144 * depth * cols, nbytes(weight, embed_weight, modulation, text, video, conv_weight)
+        ),
         name="fold",
-    )(embed_weight, modulation, weight)
-
-
-def text_kernel(chunks, text_ref, mod_ref, gain_ref, w_hbm, key_ref, value_ref, w_buf, stream_ref, acc_ref, sem):
-    depth, parts, width = w_hbm.shape
-    rows = depth // chunks
-
-    def copy(c):
-        at = pl.ds(c * rows, rows)
-        return pltpu.make_async_copy(w_hbm.at[at], w_buf.at[at], sem.at[c])
-
-    for c in range(chunks):
-        copy(c).start()
-    text = text_ref[...].astype(F32)
-    centred = text - jnp.mean(text, -1, keepdims=True)
-    normed = centred * lax.rsqrt(jnp.mean(centred * centred, -1, keepdims=True) + EPS)
-    stream_ref[...] = (normed * (1.0 + mod_ref[3:4, :]) + mod_ref[2:3, :]).astype(BF16)
+    )(*[pltpu.with_memory_space_constraint(a, pltpu.HBM) for a in (embed_weight, modulation, weight, text, video, conv_weight)])
+
+
+def text_kernel(stream_ref, gain_ref, w_ref, key_ref, value_ref, acc_ref):
+    depth, parts, width = w_ref.shape
     step = 128
+    group = 4
     row = lax.broadcasted_iota(jnp.int32, (2 * step, 2 * step), 0)
     col = lax.broadcasted_iota(jnp.int32, (2 * step, 2 * step), 1)
     pick = jnp.where(col == 2 * (row % step) + row // step, 1.0, 0.0).astype(BF16)
-    flat = w_buf.reshape(depth * parts, width)
-    for c in range(chunks):
-        copy(c).wait()
+    flat = w_ref.reshape(depth * parts, width)
+    for c in range(depth // (group * step)):
         pieces = ([], [])
-        for s in range(rows // step):
-            at = 2 * (c * rows + s * step)
+        for s in range(group):
+            at = 2 * (c * group + s) * step
             both = dot(pick, flat[at : at + 2 * step, :]).astype(BF16)
             pieces[0].append(both[:step])
             pieces[1].append(both[step:])
-        stream = stream_ref[:, c * rows : (c + 1) * rows]
+        stream = stream_ref[:, c * group * step : (c + 1) * group * step]
         for p in range(2):
             term = dot(stream, jnp.concatenate(pieces[p], 0))
             if c == 0:
@@ -167,29 +212,45 @@
         value_ref[h] = acc_ref[1, :, at].astype(BF16)
 
 
-def text_side(text, modulation, gain, weight):
+def text_side(stream, gain, weight):
     depth, parts, width = weight.shape
-    count = text.shape[0]
+    count = stream.shape[0]
     heads = width // HS
-    chunks = 6
     return pl.pallas_call(
-        lambda *refs: text_kernel(chunks, *refs),
+        text_kernel,
         out_shape=(jax.ShapeDtypeStruct((heads, count, HS), BF16),) * 2,
-        in_specs=[vmem_spec(), vmem_spec(), vmem_spec(), hbm_spec()],
+        in_specs=[vmem_spec()] * 3,
         out_specs=(vmem_spec(),) * 2,
-        scratch_shapes=[
-            VMEM((depth, parts, width), BF16),
-            VMEM((count, depth), BF16),
-            VMEM((parts, count, width), F32),
-            pltpu.SemaphoreType.DMA((chunks,)),
-        ],
-        compiler_params=params(),
-        cost_estimate=cost(4 * count * depth * parts * width, nbytes(weight, text, modulation)),
+        scratch_shapes=[VMEM((parts, count, width), F32)],
+        compiler_params=params(12),
+        cost_estimate=cost(4 * count * depth * parts * width, nbytes(weight, stream)),
         name="text_side",
-    )(text, modulation, gain, weight)
-
-
-def conv_kernel(video_ref, halo_ref, weight_ref, latent_ref, out_ref, wide_ref, even_ref, odd_ref, left_ref, spread_ref):
+    )(stream, gain, weight)
+
+
+def conv_kernel(
+    chunks,
+    video_ref,
+    halo_ref,
+    weight_ref,
+    latent_ref,
+    text_hbm,
+    out_ref,
+    text_ref,
+    wide_ref,
+    even_ref,
+    odd_ref,
+    left_ref,
+    spread_ref,
+    sem,
+):
+    deep = text_hbm.shape[0] // chunks
+    ahead = [
+        pltpu.make_async_copy(text_hbm.at[pl.ds(c * deep, deep)], text_ref.at[pl.ds(c * deep, deep)], sem.at[c])
+        for c in range(chunks)
+    ]
+    for copy in ahead:
+        copy.start()
     frames, rows, cols, chans = video_ref.shape
     block = cols + 8
     half = cols // 2
@@ -229,28 +290,35 @@
                 )
             )
     out_ref[...] = dot_nt(jnp.concatenate(pieces, 1), spread_ref[...]).astype(BF16)
-
-
-def conv_side(video, halo, conv_weight, latent_weight):
+    for copy in ahead:
+        copy.wait()
+
+
+def conv_side(video, halo, weight, latent_weight, text_weight):
     frames, rows, cols, chans = video.shape
-    mid = conv_weight.shape[-1]
+    mid = weight.shape[-1]
     lat = latent_weight.shape[1]
-    weight = conv_weight.reshape(-1, mid)
     latent = latent_weight.T
     half = cols // 2
     tall = rows // 2
+    chunks = 4
     return pl.pallas_call(
-        conv_kernel,
-        out_shape=jax.ShapeDtypeStruct((frames * half // 2, 2 * tall * lat), BF16),
-        in_specs=[vmem_spec()] * 4,
-        out_specs=vmem_spec(),
+        lambda *refs: conv_kernel(chunks, *refs),
+        out_shape=(
+            jax.ShapeDtypeStruct((frames * half // 2, 2 * tall * lat), BF16),
+            jax.ShapeDtypeStruct(text_weight.shape, BF16),
+        ),
+        in_specs=[vmem_spec()] * 4 + [hbm_spec()],
+        out_specs=(vmem_spec(),) * 2,
         scratch_shapes=[VMEM(((rows + 1) * frames * (cols + 8), chans), F32)]
         + [VMEM((rows + 1, frames + 2, half, chans), BF16)] * 3
-        + [VMEM((2 * tall * lat, 2 * tall * mid), BF16)],
-        compiler_params=params(),
-        cost_estimate=cost(2 * frames * tall * half * 27 * chans * mid, nbytes(video, halo, weight)),
+        + [VMEM((2 * tall * lat, 2 * tall * mid), BF16), pltpu.SemaphoreType.DMA((chunks,))],
+        compiler_params=params(24),
+        cost_estimate=cost(
+            2 * frames * tall * half * 27 * chans * mid, nbytes(video, halo, weight, text_weight)
+        ),
         name="conv_side",
-    )(video, halo, weight, latent)
+    )(video, halo, weight, latent, pltpu.with_memory_space_constraint(text_weight, pltpu.HBM))
 
 
 def qkv_kernel(order, frames, *refs):
@@ -324,7 +392,7 @@
         in_specs=[smem_spec()] + [vmem_spec()] * (n + 7),
         out_specs=(vmem_spec(),) * (n + 2),
         scratch_shapes=[VMEM((n * rows, rows), BF16)],
-        compiler_params=params(),
+        compiler_params=params(16),
         cost_estimate=cost(2 * 2 * n * rows * 256 * 3 * heads * HS, 4 * nbytes(rhs0)),
         name="qkv_side",
     )(me, *patches, rhs0, rhs1, shift, gram, gain, tkey, tvalue)
@@ -333,21 +401,14 @@
 
 def attend_kernel(query_ref, key_ref, value_ref, out_ref):
     heads, total, _ = key_ref.shape
-    step = 256
     for h in range(heads):
-        query = query_ref[h]
-        acc = None
-        for c in range(0, total, step):
-            logits = dot_nt(query, key_ref[h, c : c + step, :])
-            weights = jnp.exp2(logits)
-            fold_sum = weights[:, :HS] + weights[:, HS:]
-            term = dot(weights.astype(BF16), value_ref[h, c : c + step, :])
-            if acc is None:
-                acc, norm = term, fold_sum
-            else:
-                acc, norm = acc + term, norm + fold_sum
+        weights = jnp.exp2(dot_nt(query_ref[h], key_ref[h]))
+        norm = weights[:, :HS]
+        for c in range(HS, total, HS):
+            norm = norm + weights[:, c : c + HS]
         norm = jnp.sum(norm, -1, keepdims=True)
-        out_ref[:, h * HS : (h + 1) * HS] = (acc / norm).astype(BF16)
+        attended = dot(weights.astype(BF16), value_ref[h])
+        out_ref[:, h * HS : (h + 1) * HS] = (attended / norm).astype(BF16)
 
 
 def attend(query, key, value):
@@ -358,10 +419,8 @@
         out_shape=jax.ShapeDtypeStruct((rows, heads * HS), BF16),
         in_specs=[vmem_spec()] * 3,
         out_specs=vmem_spec(),
-        compiler_params=params(),
-        cost_estimate=cost(
-            4 * heads * rows * total * HS, nbytes(query, key, value), heads * rows * total
-        ),
+        compiler_params=params(8),
+        cost_estimate=cost(heads * rows * HS, nbytes(query)),
         name="attend",
     )(query, key, value)
 
@@ -386,9 +445,10 @@
     return pl.pallas_call(
         lambda *refs: gather_kernel(order, *refs),
         out_shape=jax.ShapeDtypeStruct((rows, n * width), BF16),
-        in_specs=[smem_spec()] + [hbm_spec()] * n,
+        in_specs=[smem_spec()] + [vmem_spec()] * n,
         out_specs=hbm_spec(),
         scratch_shapes=[pltpu.SemaphoreType.DMA((n,))],
+        compiler_params=params(4),
         cost_estimate=cost(0, 2 * n * nbytes(blocks[0])),
         name="side_by_side",
     )(me, *blocks)
@@ -403,11 +463,18 @@
         return lax.ppermute(x, "ctx", [(i, i ^ k) for i in range(n)])
 
     halo = lax.ppermute(video[:, -1:], "ctx", [(i, i + 1) for i in range(n - 1)])
-    rhs0, rhs1, shift, gram = fold(embed_weight, modulation, qkv_weight.transpose(1, 0, 2))
-    patches = conv_side(video, halo, conv_weight, latent_weight)
+    rhs0, rhs1, shift, gram, stream, tile, taps = fold(
+        embed_weight,
+        modulation,
+        qkv_weight.transpose(1, 0, 2),
+        text,
+        video,
+        conv_weight.reshape(-1, conv_weight.shape[-1]),
+    )
+    patches, text_near = conv_side(tile, halo, taps, latent_weight, text_weight)
     order = tuple(range(n - 1, -1, -1))
     received = [swap(patches, k) if k else patches for k in order]
-    tkey, tvalue = text_side(text, modulation, qk_gain, text_weight)
+    tkey, tvalue = text_side(stream, qk_gain, text_near)
     queries, key, value = qkv_side(
         order, frames, me, received, rhs0, rhs1, shift, gram, qk_gain, tkey, tvalue
     )

time: 97.3 us -> 44.1 us (0.45)
  Pallas kernels: 76.5 us -> 23.5 us
  local copies, waits for them, and re-layouts: 2.89 us -> 0.93 us
  waiting for transfers between devices: 5.48 us -> 7.14 us
    pallas_call x1, Pallas kernels: 32.9 us -> 1 us  [side_by_side(): pl.pallas_call(lambda *refs: gather_kernel(order, *refs), out_shape=jax.S...]
    pallas_call x4, Pallas kernels: 19.4 us -> 6.33 us  [attend(): pl.pallas_call(attend_kernel, out_shape=jax.ShapeDtypeStruct((rows, heads...]
    pallas_call x2, Pallas kernels: 12.4 us -> 6.53 us  [the longest x1 3.65 us: text_side(): pl.pallas_call(text_kernel, out_shape=(jax.ShapeDtypeStruct((heads, count...]
    pallas_call x1, Pallas kernels: 5.02 us -> 2 us  [qkv_side(): pl.pallas_call(lambda *refs: qkv_kernel(order, frames, *refs), out_shape=...]
    unnamed x18 -> x4, local copies, waits for them, and re-layouts: 1.98 us -> 0.01 us
    ppermute x6, waiting for transfers between devices: 5.48 us -> 7.13 us  [swap(): return lax.ppermute(x, 'ctx', [(i, i ^ k) for i in range(n)])]
  transfers between devices with their start and end apart: 7 -> 7, of which waited for: 3 -> 1; matrix products, arithmetic and copies ran while one was open for 0% -> 0% of each run, Pallas kernels for 20% -> 36%
where the time goes in v2:
time: 44.1 us; the launch traced here: 44 us
  Pallas kernels  23.5 us (53%)
  starting transfers between devices  12.1 us (27%)
  waiting for transfers between devices  7.14 us (16%)
  local copies, waits for them, and re-layouts  0.93 us (2%)
    pallas_call x1, Pallas kernels, fold(): pl.pallas_call(lambda *refs: fold_kernel(chunks, *refs), out_shape=(jax.S...  7.66 us
    ppermute x6, starting transfers between devices, swap(): return lax.ppermute(x, 'ctx', [(i, i ^ k) for i in range(n)])  7.24 us
    ppermute x6, waiting for transfers between devices, swap(): return lax.ppermute(x, 'ctx', [(i, i ^ k) for i in range(n)])  7.13 us
    pallas_call x4, Pallas kernels, attend(): pl.pallas_call(attend_kernel, out_shape=jax.ShapeDtypeStruct((rows, heads...  6.33 us
    ppermute x1, starting transfers between devices, shards(): lax.ppermute(video[:, -1:], 'ctx', [(i, i + 1) for i in range(n - 1)])  4.85 us
    pallas_call x1, Pallas kernels, text_side(): pl.pallas_call(text_kernel, out_shape=(jax.ShapeDtypeStruct((heads, count...  3.65 us
    pallas_call x1, Pallas kernels, conv_side(): pl.pallas_call(lambda *refs: conv_kernel(chunks, *refs), out_shape=(jax.S...  2.88 us
    pallas_call x1, Pallas kernels, qkv_side(): pl.pallas_call(lambda *refs: qkv_kernel(order, frames, *refs), out_shape=...  2 us
  transfers between devices with their start and end apart: 7, of which 1 were waited for; matrix products, arithmetic and copies ran while one was open for 0% of the time, Pallas kernels for 36%

profile of v2, /device:TPU:0, one launch (start us, length us, event | category | flops | bytes accessed | tf_op | source)
XLA Modules:
  0.0 44.0 jit_solution(15783727126456427903)
XLA Ops:
  0.0 0.9 %slice.3 = bf16[8,1,64,128]{3,2,1,0:T(8,128)(2,1)S(1)} slice(bf16[8,8,64,128]{3,2,1,0:T(8,128)(2,1)} %refs_4_.2), slice={[0:8], [7:8], [0:64], [0:128]} | slice | bytes 262144 | tf_op jit(solution)/shard_map/slice | solution.py:465
  0.9 4.8 %collective-permute-start = (bf16[8,1,64,128]{3,2,1,0:T(8,128)(2,1)S(1)}, bf16[8,1,64,128]{3,2,1,0:T(8,128)(2,1)S(1)}, u32[]{:S(2)}, u32[]{:S(2)}) collective-permute-start(bf16[8,1,64,128]{3,2,1,0:T(8,128)(2,1)S(1)} %slice.3), channel_id=1, source_target_pairs={{0,1},{1,2},{2,3},{4,5},{5,6},{6,7},{8,9},{9,10},{10,11},{12,13},{... | collective-permute-start | bytes 393224 | tf_op jit(solution)/shard_map/ppermute | solution.py:465
  5.8 0.0 copy-start
  5.8 7.7 %fold.1 = (bf16[256,1536]{1,0:T(8,128)(2,1)S(1)}, bf16[256,1536]{1,0:T(8,128)(2,1)S(1)}, f32[1,1536]{1,0:T(1,128)S(1)}, bf16[256,128]{1,0:T(8,128)(2,1)S(1)}, bf...) custom-call(bf16[64,3072]{1,0:T(8,128)(2,1)} %refs_0_.1, ...), custom_call_target="tpu_custom_call" | custom-call | flops 1358954496 | bytes 14270464 | tf_op jit(solution)/shard_map/fold/pallas_call | solution.py:154
  13.5 0.0 collective-permute-done.refs_1_
  13.5 0.0 copy-done
  13.5 0.0 copy-start.1
  13.5 2.9 %conv_side.1 = (bf16[128,128]{1,0:T(8,128)(2,1)S(1)}, bf16[3072,2,512]{2,1,0:T(2,128)(2,1)S(1)}) custom-call(bf16[8,8,64,128]{3,2,1,0:T(8,128)(2,1)S(1)} %get-tuple-element.22.refs_0_, bf16[8,1,64,128]{3,2,1,0:T(8,128)(2,1)S(1)} %collective-permute-done.refs_1_, bf16[3456,256]{1,0:T(8,128)(2,1)S(1)} %get-tuple-element.23.refs_2_, ...), custom_call_target="tpu_custom_call" | custom-call | flops 1811939328 | bytes 9240576 | tf_op jit(solution)/shard_map/conv_side/pallas_call | solution.py:305
  16.4 0.4 collective-permute-start.1
  16.8 2.6 %collective-permute-start.2 = (bf16[128,128]{1,0:T(8,128)(2,1)S(1)}, bf16[128,128]{1,0:T(8,128)(2,1)S(1)}, u32[]{:S(2)}, u32[]{:S(2)}) collective-permute-start(bf16[128,128]{1,0:T(8,128)(2,1)S(1)} %get-tuple-element.24.refs_4_), channel_id=1, source_target_pairs={{0,2},{1,3},{2,0},{3,1},{4,6},{5,7},{6,4},{7,5},{8,10},{9,11},{10,... | collective-permute-start | bytes 98312 | tf_op jit(solution)/shard_map/ppermute | solution.py:463
  19.4 0.5 %collective-permute-start.3 = (bf16[128,128]{1,0:T(8,128)(2,1)S(1)}, bf16[128,128]{1,0:T(8,128)(2,1)S(1)}, u32[]{:S(2)}, u32[]{:S(2)}) collective-permute-start(bf16[128,128]{1,0:T(8,128)(2,1)S(1)} %get-tuple-element.24.refs_4_), channel_id=1, source_target_pairs={{0,1},{1,0},{2,3},{3,2},{4,5},{5,4},{6,7},{7,6},{8,9},{9,8},{10,11... | collective-permute-start | bytes 98312 | tf_op jit(solution)/shard_map/ppermute | solution.py:463
  19.9 0.0 copy-done.1
  19.9 3.6 %text_side.1 = (bf16[4,256,128]{2,1,0:T(8,128)(2,1)S(1)}, bf16[4,256,128]{2,1,0:T(8,128)(2,1)S(1)}) custom-call(bf16[256,3072]{1,0:T(8,128)(2,1)S(1)} %get-tuple-element.29.stream_ref, f32[2,128]{1,0:T(2,128)S(1)} %copy-done.1, bf16[3072,2,512]{2,1,0:T(2,128)(2,1)S(1)} %get-tuple-element.30.w_ref), custom_call_target="tpu_custom_call" | custom-call | flops 3221225472 | bytes 7864320 | tf_op jit(solution)/shard_map/text_side/pallas_call | solution.py:219
  23.6 0.0 collective-permute-done.1.refs_1_
  23.6 0.0 collective-permute-done.2.refs_2_
  23.6 0.0 collective-permute-done.3.refs_3_
  23.6 2.0 %qkv_side.1 = (bf16[4,256,128]{2,1,0:T(8,128)(2,1)S(1)}, bf16[4,256,128]{2,1,0:T(8,128)(2,1)S(1)}, bf16[4,256,128]{2,1,0:T(8,128)(2,1)S(1)}, bf16[4,256,128]{2,1...) custom-call(s32[1]{0:T(128)} %bitcast.refs_0_, ...), custom_call_target="tpu_custom_call" | custom-call | flops 805306368 | bytes 3145728 | tf_op jit(solution)/shard_map/qkv_side/pallas_call | solution.py:388
  25.6 1.7 %attend.6 = bf16[256,512]{1,0:T(8,128)(2,1)S(1)} custom-call(bf16[4,256,128]{2,1,0:T(8,128)(2,1)S(1)} %get-tuple-element.37.query_ref, bf16[4,1280,128]{2,1,0:T(8,128)(2,1)S(1)} %get-tuple-element.34.key_ref, bf16[4,1280,128]{2,1,0:T(8,128)(2,1)S(1)} %get-tuple-element.35.value_ref), custom_call_target="tpu_custom_call" | custom-call | flops 131072 | bytes 262144 | tf_op jit(solution)/shard_map/attend/pallas_call | solution.py:417
  27.4 1.5 %collective-permute-start.6 = (bf16[256,512]{1,0:T(8,128)(2,1)S(1)}, bf16[256,512]{1,0:T(8,128)(2,1)S(1)}, u32[]{:S(2)}, u32[]{:S(2)}) collective-permute-start(bf16[256,512]{1,0:T(8,128)(2,1)S(1)} %attend.6), channel_id=1, source_target_pairs={{0,1},{1,0},{2,3},{3,2},{4,5},{5,4},{6,7},{7,6},{8,9},{9,8},{10,11... | collective-permute-start | bytes 786440 | tf_op jit(solution)/shard_map/ppermute | solution.py:463
  28.9 1.5 %attend.5 = bf16[256,512]{1,0:T(8,128)(2,1)S(1)} custom-call(bf16[4,256,128]{2,1,0:T(8,128)(2,1)S(1)} %get-tuple-element.36.query_ref, bf16[4,1280,128]{2,1,0:T(8,128)(2,1)S(1)} %get-tuple-element.34.key_ref, bf16[4,1280,128]{2,1,0:T(8,128)(2,1)S(1)} %get-tuple-element.35.value_ref), custom_call_target="tpu_custom_call" | custom-call | flops 131072 | bytes 262144 | tf_op jit(solution)/shard_map/attend/pallas_call | solution.py:417
  30.5 0.3 collective-permute-start.5
  30.8 1.5 %attend.4 = bf16[256,512]{1,0:T(8,128)(2,1)S(1)} custom-call(bf16[4,256,128]{2,1,0:T(8,128)(2,1)S(1)} %get-tuple-element.33.query_ref, bf16[4,1280,128]{2,1,0:T(8,128)(2,1)S(1)} %get-tuple-element.34.key_ref, bf16[4,1280,128]{2,1,0:T(8,128)(2,1)S(1)} %get-tuple-element.35.value_ref), custom_call_target="tpu_custom_call" | custom-call | flops 131072 | bytes 262144 | tf_op jit(solution)/shard_map/attend/pallas_call | solution.py:417
  32.3 1.8 %collective-permute-start.4 = (bf16[256,512]{1,0:T(8,128)(2,1)S(1)}, bf16[256,512]{1,0:T(8,128)(2,1)S(1)}, u32[]{:S(2)}, u32[]{:S(2)}) collective-permute-start(bf16[256,512]{1,0:T(8,128)(2,1)S(1)} %attend.4), channel_id=1, source_target_pairs={{0,3},{1,2},{2,1},{3,0},{4,7},{5,6},{6,5},{7,4},{8,11},{9,10},{10,... | collective-permute-start | bytes 786440 | tf_op jit(solution)/shard_map/ppermute | solution.py:463
  34.1 1.5 %attend.7.refs_4_ = bf16[256,512]{1,0:T(8,128)(2,1)S(1)} custom-call(bf16[4,256,128]{2,1,0:T(8,128)(2,1)S(1)} %get-tuple-element.38.query_ref, bf16[4,1280,128]{2,1,0:T(8,128)(2,1)S(1)} %get-tuple-element.34.key_ref, bf16[4,1280,128]{2,1,0:T(8,128)(2,1)S(1)} %get-tuple-element.35.value_ref), custom_call_target="tpu_custom_call" | custom-call | flops 131072 | bytes 262144 | tf_op jit(solution)/shard_map/attend/pallas_call | solution.py:417
  35.7 0.0 collective-permute-done.6.refs_3_
  35.7 7.1 %collective-permute-done.5.refs_2_ = bf16[256,512]{1,0:T(8,128)(2,1)S(1)} collective-permute-done((bf16[256,512]{1,0:T(8,128)(2,1)S(1)}, bf16[256,512]{1,0:T(8,128)(2,1)S(1)}, u32[]{:S(2)}, u32[]{:S(2)}) %collective-permute-start.5) | collective-permute-done | bytes 262176 | tf_op jit(solution)/shard_map/ppermute | solution.py:463
  42.8 0.0 collective-permute-done.4.refs_1_
  42.8 1.0 %side_by_side.1 = bf16[256,2048]{1,0:T(8,128)(2,1)} custom-call(s32[1]{0:T(128)} %bitcast.refs_0_, bf16[256,512]{1,0:T(8,128)(2,1)S(1)} %collective-permute-done.4.refs_1_, bf16[256,512]{1,0:T(8,128)(2,1)S(1)} %collective-permute-done.5.refs_2_, bf16[256,512]{1,0:T(8,128)(2,1)S(1)} %collective-permute-done.6.refs_3_, bf16[256,512]{1,0:T(8,128)(2,1)S(1)} %attend.7.refs_4_), custom_call_target="tpu_custom_call" | custom-call | bytes 2097152 | tf_op jit(solution)/shard_map/side_by_side/pallas_call | solution.py:445
Async XLA Ops:
  0.9 12.5 %collective-permute-start = (bf16[8,1,64,128]{3,2,1,0:T(8,128)(2,1)S(1)}, bf16[8,1,64,128]{3,2,1,0:T(8,128)(2,1)S(1)}, u32[]{:S(2)}, u32[]{:S(2)}) collective-permute-start(bf16[8,1,64,128]{3,2,1,0:T(8,128)(2,1)S(1)} %slice.3), channel_id=1, source_target_pairs={{0,1},{1,2},{2,3},{4,5},{5,6},{6,7},{8,9},{9,10},{10,11},{12,13},{... | collective-permute-start | bytes 393224 | tf_op jit(solution)/shard_map/ppermute | solution.py:465
  5.8 7.7 %copy-start = (bf16[256,16]{0,1:T(8,128)(2,1)S(1)}, bf16[256,16]{0,1:T(8,128)(2,1)}, u32[]{:S(2)}) copy-start(bf16[256,16]{0,1:T(8,128)(2,1)} %param.11) | copy-start | bytes 24580
  13.5 6.5 %copy-start.1 = (f32[2,128]{1,0:T(2,128)S(1)}, f32[2,128]{1,0:T(2,128)}, u32[]{:S(2)}) copy-start(f32[2,128]{1,0:T(2,128)} %refs_9_.1) | copy-start | bytes 3076
  16.4 7.2 %collective-permute-start.1 = (bf16[128,128]{1,0:T(8,128)(2,1)S(1)}, bf16[128,128]{1,0:T(8,128)(2,1)S(1)}, u32[]{:S(2)}, u32[]{:S(2)}) collective-permute-start(bf16[128,128]{1,0:T(8,128)(2,1)S(1)} %get-tuple-element.24.refs_4_), channel_id=1, source_target_pairs={{0,3},{1,2},{2,1},{3,0},{4,7},{5,6},{6,5},{7,4},{8,11},{9,10},{10,... | collective-permute-start | bytes 98312 | tf_op jit(solution)/shard_map/ppermute | solution.py:463
  16.8 6.8 %collective-permute-start.2 = (bf16[128,128]{1,0:T(8,128)(2,1)S(1)}, bf16[128,128]{1,0:T(8,128)(2,1)S(1)}, u32[]{:S(2)}, u32[]{:S(2)}) collective-permute-start(bf16[128,128]{1,0:T(8,128)(2,1)S(1)} %get-tuple-element.24.refs_4_), channel_id=1, source_target_pairs={{0,2},{1,3},{2,0},{3,1},{4,6},{5,7},{6,4},{7,5},{8,10},{9,11},{10,... | collective-permute-start | bytes 98312 | tf_op jit(solution)/shard_map/ppermute | solution.py:463
  19.4 4.2 %collective-permute-start.3 = (bf16[128,128]{1,0:T(8,128)(2,1)S(1)}, bf16[128,128]{1,0:T(8,128)(2,1)S(1)}, u32[]{:S(2)}, u32[]{:S(2)}) collective-permute-start(bf16[128,128]{1,0:T(8,128)(2,1)S(1)} %get-tuple-element.24.refs_4_), channel_id=1, source_target_pairs={{0,1},{1,0},{2,3},{3,2},{4,5},{5,4},{6,7},{7,6},{8,9},{9,8},{10,11... | collective-permute-start | bytes 98312 | tf_op jit(solution)/shard_map/ppermute | solution.py:463
  27.4 8.3 %collective-permute-start.6 = (bf16[256,512]{1,0:T(8,128)(2,1)S(1)}, bf16[256,512]{1,0:T(8,128)(2,1)S(1)}, u32[]{:S(2)}, u32[]{:S(2)}) collective-permute-start(bf16[256,512]{1,0:T(8,128)(2,1)S(1)} %attend.6), channel_id=1, source_target_pairs={{0,1},{1,0},{2,3},{3,2},{4,5},{5,4},{6,7},{7,6},{8,9},{9,8},{10,11... | collective-permute-start | bytes 786440 | tf_op jit(solution)/shard_map/ppermute | solution.py:463
  30.5 12.3 %collective-permute-start.5 = (bf16[256,512]{1,0:T(8,128)(2,1)S(1)}, bf16[256,512]{1,0:T(8,128)(2,1)S(1)}, u32[]{:S(2)}, u32[]{:S(2)}) collective-permute-start(bf16[256,512]{1,0:T(8,128)(2,1)S(1)} %attend.5), channel_id=1, source_target_pairs={{0,2},{1,3},{2,0},{3,1},{4,6},{5,7},{6,4},{7,5},{8,10},{9,11},{10,... | collective-permute-start | bytes 786440 | tf_op jit(solution)/shard_map/ppermute | solution.py:463
  32.3 10.5 %collective-permute-start.4 = (bf16[256,512]{1,0:T(8,128)(2,1)S(1)}, bf16[256,512]{1,0:T(8,128)(2,1)S(1)}, u32[]{:S(2)}, u32[]{:S(2)}) collective-permute-start(bf16[256,512]{1,0:T(8,128)(2,1)S(1)} %attend.4), channel_id=1, source_target_pairs={{0,3},{1,2},{2,1},{3,0},{4,7},{5,6},{6,5},{7,4},{8,11},{9,10},{10,... | collective-permute-start | bytes 786440 | tf_op jit(solution)/shard_map/ppermute | solution.py:463

commit v3 on v2

--- a/solution.py
+++ b/solution.py
@@ -115,8 +115,12 @@
     lhs_ref[2 * pi :, :] = jnp.concatenate(
         [shift_hi.astype(F32), shift_lo.astype(F32), jnp.zeros((14, depth), F32)], 0
     ).astype(BF16)
-    chi, clo = split(jnp.concatenate([centred, centred], 0))
-    gram = dot_nt(chi, chi) + dot_nt(chi, clo) + dot_nt(clo, chi)
+    both = jnp.concatenate(split(centred), 0)
+    gram = dot_nt(both, both)
+    lane = lax.broadcasted_iota(jnp.int32, (pi, 2 * pi), 1)
+    gram = gram[:pi] + jnp.where(lane < pi, gram[pi:], 0.0)
+    gram = gram + pltpu.roll(gram, pi, 1)
+    gram = jnp.concatenate([gram, gram], 0)
     row = lax.broadcasted_iota(jnp.int32, gram.shape, 0) // pi
     col = lax.broadcasted_iota(jnp.int32, gram.shape, 1) // pi
     ghi, glo = split(jnp.where(row == col, gram * (1.0 / depth), 0.0))
@@ -321,14 +325,57 @@
     )(video, halo, weight, latent, pltpu.with_memory_space_constraint(text_weight, pltpu.HBM))
 
 
-def qkv_kernel(order, frames, *refs):
+def head_norm(v, gain):
+    return (v * lax.rsqrt(jnp.mean(v * v, -1, keepdims=True) + EPS) * gain).astype(BF16)
+
+
+def token_scales(x, xx, gram_ref):
+    quad = dot(xx, gram_ref[...]) * x.astype(F32)
+    lane = lax.broadcasted_iota(jnp.int32, quad.shape, 1)
+    low = lane < quad.shape[1] // 2
+    scales = []
+    for i in range(2):
+        var = jnp.sum(jnp.where(low if i == 0 else ~low, quad, 0.0), -1, keepdims=True)
+        scales.append(lax.rsqrt(jnp.maximum(var, 0.0) + EPS))
+    return scales
+
+
+def block_queries(n, own, x, xx, scales, rhs_refs, shift_ref, gain_ref, query_ref):
+    heads = query_ref.shape[0]
+    span = x.shape[0] // n
+    grain = span // own
+    gain = gain_ref[0:1, :] * (math.log2(math.e) / math.sqrt(HS))
+    for i in range(2):
+        at = slice(0, heads * HS)
+        projected = dot(xx, rhs_refs[i][:, at]) * scales[i] + shift_ref[:, at]
+        for h in range(heads):
+            v = head_norm(projected[:, h * HS : (h + 1) * HS], gain)
+            for s in range(n):
+                for f in range(own):
+                    to = f * (n * 2 * grain) + (s * 2 + i) * grain
+                    come = s * span + f * grain
+                    query_ref[h, to : to + grain, :] = v[come : come + grain]
+
+
+def attention(query_ref, key_ref, value_ref, out_ref):
+    heads, total, _ = key_ref.shape
+    for h in range(heads):
+        weights = jnp.exp2(dot_nt(query_ref[h], key_ref[h]))
+        norm = weights[:, :HS]
+        for c in range(HS, total, HS):
+            norm = norm + weights[:, c : c + HS]
+        norm = jnp.sum(norm, -1, keepdims=True)
+        attended = dot(weights.astype(BF16), value_ref[h])
+        out_ref[:, h * HS : (h + 1) * HS] = (attended / norm).astype(BF16)
+
+
+def first_kernel(order, frames, *refs):
     n = len(order)
     me_ref = refs[0]
     patch_refs = refs[1 : 1 + n]
     rhs_refs = refs[1 + n : 3 + n]
     shift_ref, gram_ref, gain_ref, tkey_ref, tvalue_ref = refs[3 + n : 8 + n]
-    query_refs = refs[8 + n : 8 + 2 * n]
-    key_ref, value_ref, patch_scr = refs[8 + 2 * n :]
+    out_ref, x_ref, key_ref, value_ref, patch_scr, query_ref = refs[8 + n :]
     me = me_ref[0]
     heads, count, _ = tkey_ref.shape
     rows = patch_refs[0].shape[0]
@@ -339,119 +386,173 @@
         value_ref[h, 0:count, :] = tvalue_ref[h]
     own = frames // n
     span = rows // n
-    grain = span // own
-    pieces = []
-    for k in order:
+    for j, k in enumerate(order):
         for s in range(n):
             at = pl.multiple_of((me ^ k) * span, span) + s * rows
-            pieces.append(patch_scr[pl.ds(pl.multiple_of(at, span), span), :])
-    x = jnp.concatenate(pieces, 0)
+            x_ref[j * rows + s * span : j * rows + (s + 1) * span, :] = patch_scr[
+                pl.ds(pl.multiple_of(at, span), span), :
+            ]
+    x = x_ref[...]
     xx = jnp.concatenate([x, x], 1)
-    quad = dot(xx, gram_ref[...]) * x.astype(F32)
-    lane = lax.broadcasted_iota(jnp.int32, quad.shape, 1)
-    low = lane < quad.shape[1] // 2
+    scales = token_scales(x, xx, gram_ref)
     width = heads * HS
-    gain_q = gain_ref[0:1, :] * (math.log2(math.e) / math.sqrt(HS))
-    gain_k = gain_ref[1:2, :]
     for i in range(2):
-        var = jnp.sum(jnp.where(low if i == 0 else ~low, quad, 0.0), -1, keepdims=True)
-        rstd = lax.rsqrt(jnp.maximum(var, 0.0) + EPS)
-        for p in range(3):
+        for p in (1, 2):
             for h0 in range(0, heads, 2):
                 at = slice(p * width + h0 * HS, p * width + (h0 + 2) * HS)
-                pair = dot(xx, rhs_refs[i][:, at]) * rstd + shift_ref[:, at]
+                pair = dot(xx, rhs_refs[i][:, at]) * scales[i] + shift_ref[:, at]
                 for h in (h0, h0 + 1):
                     v = pair[:, (h - h0) * HS : (h - h0 + 1) * HS]
-                    if p < 2:
-                        v = v * lax.rsqrt(jnp.mean(v * v, -1, keepdims=True) + EPS)
-                        v = v * (gain_q if p == 0 else gain_k)
-                    v = v.astype(BF16)
-                    for k in range(n):
-                        block = v[k * rows : (k + 1) * rows]
-                        if p == 0:
-                            for s in range(n):
-                                for f in range(own):
-                                    to = f * (n * 2 * grain) + (s * 2 + i) * grain
-                                    come = s * span + f * grain
-                                    query_refs[k][h, to : to + grain, :] = block[come : come + grain]
-                        else:
-                            ref = key_ref if p == 1 else value_ref
-                            to = count + (2 * k + i) * rows
-                            ref[h, to : to + rows, :] = block
-
-
-def qkv_side(order, frames, me, patches, rhs0, rhs1, shift, gram, gain, tkey, tvalue):
+                    to = slice(count + i * n * rows, count + (i + 1) * n * rows)
+                    if p == 1:
+                        key_ref[h, to, :] = head_norm(v, gain_ref[1:2, :])
+                    else:
+                        value_ref[h, to, :] = v.astype(BF16)
+    block_queries(
+        n, own, x[:rows], xx[:rows], [v[:rows] for v in scales], rhs_refs, shift_ref, gain_ref, query_ref
+    )
+    attention(query_ref, key_ref, value_ref, out_ref)
+
+
+def first_block(order, frames, me, patches, rhs0, rhs1, shift, gram, gain, tkey, tvalue):
     n = len(order)
     heads, count, _ = tkey.shape
     rows = patches[0].shape[0]
     total = count + 2 * n * rows
-    outs = pl.pallas_call(
-        lambda *refs: qkv_kernel(order, frames, *refs),
-        out_shape=(jax.ShapeDtypeStruct((heads, 2 * rows, HS), BF16),) * n
-        + (jax.ShapeDtypeStruct((heads, total, HS), BF16),) * 2,
+    return pl.pallas_call(
+        lambda *refs: first_kernel(order, frames, *refs),
+        out_shape=(
+            jax.ShapeDtypeStruct((2 * rows, heads * HS), BF16),
+            jax.ShapeDtypeStruct((n * rows, rows), BF16),
+            jax.ShapeDtypeStruct((heads, total, HS), BF16),
+            jax.ShapeDtypeStruct((heads, total, HS), BF16),
+        ),
         in_specs=[smem_spec()] + [vmem_spec()] * (n + 7),
-        out_specs=(vmem_spec(),) * (n + 2),
-        scratch_shapes=[VMEM((n * rows, rows), BF16)],
+        out_specs=(vmem_spec(),) * 4,
+        scratch_shapes=[VMEM((n * rows, rows), BF16), VMEM((heads, 2 * rows, HS), BF16)],
         compiler_params=params(16),
         cost_estimate=cost(2 * 2 * n * rows * 256 * 3 * heads * HS, 4 * nbytes(rhs0)),
-        name="qkv_side",
+        name="first_block",
     )(me, *patches, rhs0, rhs1, shift, gram, gain, tkey, tvalue)
-    return outs[:n], outs[n], outs[n + 1]
-
-
-def attend_kernel(query_ref, key_ref, value_ref, out_ref):
-    heads, total, _ = key_ref.shape
-    for h in range(heads):
-        weights = jnp.exp2(dot_nt(query_ref[h], key_ref[h]))
-        norm = weights[:, :HS]
-        for c in range(HS, total, HS):
-            norm = norm + weights[:, c : c + HS]
-        norm = jnp.sum(norm, -1, keepdims=True)
-        attended = dot(weights.astype(BF16), value_ref[h])
-        out_ref[:, h * HS : (h + 1) * HS] = (attended / norm).astype(BF16)
-
-
-def attend(query, key, value):
-    heads, rows, _ = query.shape
-    total = key.shape[1]
+
+
+def attend_kernel(
+    n, own, j, x_ref, rhs0_ref, rhs1_ref, shift_ref, gram_ref, gain_ref, key_ref, value_ref, out_ref, query_ref
+):
+    rows = x_ref.shape[1]
+    x = x_ref[j * rows : (j + 1) * rows, :]
+    xx = jnp.concatenate([x, x], 1)
+    scales = token_scales(x, xx, gram_ref)
+    block_queries(n, own, x, xx, scales, (rhs0_ref, rhs1_ref), shift_ref, gain_ref, query_ref)
+    attention(query_ref, key_ref, value_ref, out_ref)
+
+
+def attend(n, frames, j, x, rhs0, rhs1, shift, gram, gain, key, value):
+    heads = key.shape[0]
+    rows = x.shape[1]
     return pl.pallas_call(
-        attend_kernel,
-        out_shape=jax.ShapeDtypeStruct((rows, heads * HS), BF16),
-        in_specs=[vmem_spec()] * 3,
+        lambda *refs: attend_kernel(n, frames // n, j, *refs),
+        out_shape=jax.ShapeDtypeStruct((2 * rows, heads * HS), BF16),
+        in_specs=[vmem_spec()] * 8,
         out_specs=vmem_spec(),
-        compiler_params=params(8),
-        cost_estimate=cost(heads * rows * HS, nbytes(query)),
+        scratch_shapes=[VMEM((heads, 2 * rows, HS), BF16)],
+        compiler_params=params(12),
+        cost_estimate=cost(heads * rows * HS, 2 * nbytes(x)),
         name="attend",
-    )(query, key, value)
-
-
-def gather_kernel(order, me_ref, *refs):
+    )(x, rhs0, rhs1, shift, gram, gain, key, value)
+
+
+def place(block, me, k, out_ref, sem):
+    width = block.shape[1]
+    at = pl.multiple_of((me ^ k) * width, width)
+    return pltpu.make_async_copy(block, out_ref.at[:, pl.ds(at, width)], sem)
+
+
+def own_kernel(
+    n,
+    own,
+    far,
+    me_ref,
+    far_ref,
+    x_ref,
+    rhs0_ref,
+    rhs1_ref,
+    shift_ref,
+    gram_ref,
+    gain_ref,
+    key_ref,
+    value_ref,
+    out_ref,
+    query_ref,
+    block_ref,
+    sem,
+):
+    first = place(far_ref, me_ref[0], far, out_ref, sem.at[0])
+    first.start()
+    attend_kernel(
+        n,
+        own,
+        n - 1,
+        x_ref,
+        rhs0_ref,
+        rhs1_ref,
+        shift_ref,
+        gram_ref,
+        gain_ref,
+        key_ref,
+        value_ref,
+        block_ref,
+        query_ref,
+    )
+    second = place(block_ref, me_ref[0], 0, out_ref, sem.at[1])
+    second.start()
+    first.wait()
+    second.wait()
+
+
+def own_block(n, frames, far, me, far_block, x, rhs0, rhs1, shift, gram, gain, key, value):
+    heads = key.shape[0]
+    rows = x.shape[1]
+    width = heads * HS
+    return pl.pallas_call(
+        lambda *refs: own_kernel(n, frames // n, far, *refs),
+        out_shape=jax.ShapeDtypeStruct((2 * rows, n * width), BF16),
+        in_specs=[smem_spec()] + [vmem_spec()] * 9,
+        out_specs=hbm_spec(),
+        scratch_shapes=[
+            VMEM((heads, 2 * rows, HS), BF16),
+            VMEM((2 * rows, width), BF16),
+            pltpu.SemaphoreType.DMA((2,)),
+        ],
+        compiler_params=params(12),
+        cost_estimate=cost(heads * rows * HS, 2 * nbytes(x)),
+        name="own_block",
+    )(me, far_block, x, rhs0, rhs1, shift, gram, gain, key, value)
+
+
+def rest_kernel(order, me_ref, out_in_ref, *refs):
     n = len(order)
     out_ref, sem = refs[n:]
-    width = refs[0].shape[1]
-    copies = []
-    for j, k in enumerate(order):
-        at = pl.multiple_of((me_ref[0] ^ k) * width, width)
-        copies.append(pltpu.make_async_copy(refs[j], out_ref.at[:, pl.ds(at, width)], sem.at[j]))
+    copies = [place(refs[j], me_ref[0], k, out_ref, sem.at[j]) for j, k in enumerate(order)]
     for c in copies:
         c.start()
     for c in copies:
         c.wait()
 
 
-def side_by_side(order, me, blocks):
+def rest(order, me, out, blocks):
     n = len(order)
-    rows, width = blocks[0].shape
     return pl.pallas_call(
-        lambda *refs: gather_kernel(order, *refs),
-        out_shape=jax.ShapeDtypeStruct((rows, n * width), BF16),
-        in_specs=[smem_spec()] + [vmem_spec()] * n,
+        lambda *refs: rest_kernel(order, *refs),
+        out_shape=jax.ShapeDtypeStruct(out.shape, BF16),
+        in_specs=[smem_spec(), hbm_spec()] + [vmem_spec()] * n,
         out_specs=hbm_spec(),
         scratch_shapes=[pltpu.SemaphoreType.DMA((n,))],
+        input_output_aliases={1: 0},
         compiler_params=params(4),
         cost_estimate=cost(0, 2 * n * nbytes(blocks[0])),
-        name="side_by_side",
-    )(me, *blocks)
+        name="rest",
+    )(me, out, *blocks)
 
 
 def shards(video, conv_weight, latent_weight, embed_weight, modulation, qkv_weight, qk_gain, text, text_weight):
@@ -475,14 +576,14 @@
     order = tuple(range(n - 1, -1, -1))
     received = [swap(patches, k) if k else patches for k in order]
     tkey, tvalue = text_side(stream, qk_gain, text_near)
-    queries, key, value = qkv_side(
+    block, x, key, value = first_block(
         order, frames, me, received, rhs0, rhs1, shift, gram, qk_gain, tkey, tvalue
     )
-    blocks = []
-    for query, k in zip(queries, order):
-        block = attend(query, key, value)
-        blocks.append(swap(block, k) if k else block)
-    return side_by_side(order, me, blocks)
+    far_block = swap(block, order[0])
+    common = (x, rhs0, rhs1, shift, gram, qk_gain, key, value)
+    blocks = [swap(attend(n, frames, j, *common), order[j]) for j in range(1, n - 1)]
+    out = own_block(n, frames, order[0], me, far_block, *common)
+    return rest(order[1 : n - 1], me, out, blocks)
 
 
 def solution(mesh):

time: 44.1 us -> 41.4 us (0.939)
  waiting for transfers between devices: 7.14 us -> 4.3 us
    ppermute x6, waiting for transfers between devices: 7.13 us -> 4.3 us  [swap(): return lax.ppermute(x, 'ctx', [(i, i ^ k) for i in range(n)])]
    pallas_call x6 -> x5, Pallas kernels: 9.32 us -> 10.3 us  [the longest x2 4.03 us: attend(): pl.pallas_call(lambda *refs: attend_kernel(n, frames // n, j, *refs), out...]
    pallas_call x1, Pallas kernels: 7.66 us -> 6.83 us  [fold(): pl.pallas_call(lambda *refs: fold_kernel(chunks, *refs), out_shape=(jax.S...]
  transfers between devices with their start and end apart: 7 -> 7, of which waited for: 1 -> 3; matrix products, arithmetic and copies ran while one was open for 0% -> 0% of each run, Pallas kernels for 36% -> 42%
where the time goes in v3:
time: 41.4 us; the launch traced here: 41.2 us
  Pallas kernels  23.7 us (57%)
  starting transfers between devices  12.1 us (29%)
  waiting for transfers between devices  4.3 us (10%)
  local copies, waits for them, and re-layouts  0.93 us (2%)
    ppermute x6, starting transfers between devices, swap(): return lax.ppermute(x, 'ctx', [(i, i ^ k) for i in range(n)])  7.24 us
    pallas_call x1, Pallas kernels, fold(): pl.pallas_call(lambda *refs: fold_kernel(chunks, *refs), out_shape=(jax.S...  6.83 us
    ppermute x1, starting transfers between devices, shards(): lax.ppermute(video[:, -1:], 'ctx', [(i, i + 1) for i in range(n - 1)])  4.85 us
    ppermute x6, waiting for transfers between devices, swap(): return lax.ppermute(x, 'ctx', [(i, i ^ k) for i in range(n)])  4.3 us
    pallas_call x2, Pallas kernels, attend(): pl.pallas_call(lambda *refs: attend_kernel(n, frames // n, j, *refs), out...  4.03 us
    pallas_call x1, Pallas kernels, text_side(): pl.pallas_call(text_kernel, out_shape=(jax.ShapeDtypeStruct((heads, count...  3.65 us
    pallas_call x1, Pallas kernels, conv_side(): pl.pallas_call(lambda *refs: conv_kernel(chunks, *refs), out_shape=(jax.S...  2.88 us
    pallas_call x1, Pallas kernels, first_block(): pl.pallas_call(lambda *refs: first_kernel(order, frames, *refs), out_shap...  2.8 us
  transfers between devices with their start and end apart: 7, of which 3 were waited for; matrix products, arithmetic and copies ran while one was open for 0% of the time, Pallas kernels for 42%

profile of v3, /device:TPU:0, one launch (start us, length us, event | category | flops | bytes accessed | tf_op | source)
XLA Modules:
  0.0 41.2 jit_solution(10823682424915387878)
XLA Ops:
  0.0 0.9 %slice.3 = bf16[8,1,64,128]{3,2,1,0:T(8,128)(2,1)S(1)} slice(bf16[8,8,64,128]{3,2,1,0:T(8,128)(2,1)} %refs_4_.2), slice={[0:8], [7:8], [0:64], [0:128]} | slice | bytes 262144 | tf_op jit(solution)/shard_map/slice | solution.py:566
  0.9 4.8 %collective-permute-start = (bf16[8,1,64,128]{3,2,1,0:T(8,128)(2,1)S(1)}, bf16[8,1,64,128]{3,2,1,0:T(8,128)(2,1)S(1)}, u32[]{:S(2)}, u32[]{:S(2)}) collective-permute-start(bf16[8,1,64,128]{3,2,1,0:T(8,128)(2,1)S(1)} %slice.3), channel_id=1, source_target_pairs={{0,1},{1,2},{2,3},{4,5},{5,6},{6,7},{8,9},{9,10},{10,11},{12,13},{... | collective-permute-start | bytes 393224 | tf_op jit(solution)/shard_map/ppermute | solution.py:566
  5.8 0.0 copy-start.1
  5.8 6.8 %fold.1 = (bf16[256,1536]{1,0:T(8,128)(2,1)S(1)}, bf16[256,1536]{1,0:T(8,128)(2,1)S(1)}, f32[1,1536]{1,0:T(1,128)S(1)}, bf16[256,128]{1,0:T(8,128)(2,1)S(1)}, bf...) custom-call(bf16[64,3072]{1,0:T(8,128)(2,1)} %refs_0_.1, ...), custom_call_target="tpu_custom_call" | custom-call | flops 1358954496 | bytes 14270464 | tf_op jit(solution)/shard_map/fold/pallas_call | solution.py:158
  12.6 0.0 collective-permute-done.refs_1_
  12.6 0.0 copy-done.1
  12.6 0.0 copy-start
  12.7 2.9 %conv_side.1 = (bf16[128,128]{1,0:T(8,128)(2,1)S(1)}, bf16[3072,2,512]{2,1,0:T(2,128)(2,1)S(1)}) custom-call(bf16[8,8,64,128]{3,2,1,0:T(8,128)(2,1)S(1)} %get-tuple-element.20.refs_0_, bf16[8,1,64,128]{3,2,1,0:T(8,128)(2,1)S(1)} %collective-permute-done.refs_1_, bf16[3456,256]{1,0:T(8,128)(2,1)S(1)} %get-tuple-element.21.refs_2_, ...), custom_call_target="tpu_custom_call" | custom-call | flops 1811939328 | bytes 9240576 | tf_op jit(solution)/shard_map/conv_side/pallas_call | solution.py:309
  15.6 0.4 collective-permute-start.1
  16.0 2.6 %collective-permute-start.2 = (bf16[128,128]{1,0:T(8,128)(2,1)S(1)}, bf16[128,128]{1,0:T(8,128)(2,1)S(1)}, u32[]{:S(2)}, u32[]{:S(2)}) collective-permute-start(bf16[128,128]{1,0:T(8,128)(2,1)S(1)} %get-tuple-element.22.refs_4_), channel_id=1, source_target_pairs={{0,2},{1,3},{2,0},{3,1},{4,6},{5,7},{6,4},{7,5},{8,10},{9,11},{10,... | collective-permute-start | bytes 98312 | tf_op jit(solution)/shard_map/ppermute | solution.py:564
  18.6 0.5 %collective-permute-start.3 = (bf16[128,128]{1,0:T(8,128)(2,1)S(1)}, bf16[128,128]{1,0:T(8,128)(2,1)S(1)}, u32[]{:S(2)}, u32[]{:S(2)}) collective-permute-start(bf16[128,128]{1,0:T(8,128)(2,1)S(1)} %get-tuple-element.22.refs_4_), channel_id=1, source_target_pairs={{0,1},{1,0},{2,3},{3,2},{4,5},{5,4},{6,7},{7,6},{8,9},{9,8},{10,11... | collective-permute-start | bytes 98312 | tf_op jit(solution)/shard_map/ppermute | solution.py:564
  19.1 0.0 copy-done
  19.1 3.6 %text_side.1 = (bf16[4,256,128]{2,1,0:T(8,128)(2,1)S(1)}, bf16[4,256,128]{2,1,0:T(8,128)(2,1)S(1)}) custom-call(bf16[256,3072]{1,0:T(8,128)(2,1)S(1)} %get-tuple-element.27.stream_ref, f32[2,128]{1,0:T(2,128)S(1)} %copy-done, bf16[3072,2,512]{2,1,0:T(2,128)(2,1)S(1)} %get-tuple-element.28.w_ref), custom_call_target="tpu_custom_call" | custom-call | flops 3221225472 | bytes 7864320 | tf_op jit(solution)/shard_map/text_side/pallas_call | solution.py:223
  22.8 0.0 collective-permute-done.1.refs_1_
  22.8 0.0 collective-permute-done.2.refs_2_
  22.8 0.0 collective-permute-done.3.refs_3_
  22.8 2.8 %first_block.1 = (bf16[256,512]{1,0:T(8,128)(2,1)S(1)}, bf16[512,128]{1,0:T(8,128)(2,1)S(1)}, bf16[4,1280,128]{2,1,0:T(8,128)(2,1)S(1)}, bf16[4,1280,128]{2,1,0:T(8,128)(2,1)S(1)}) custom-call(s32[1]{0:T(128)} %bitcast.refs_0_, bf16[128,128]{1,0:T(8,128)(2,1)S(1)} %collective-permute-done.1.refs_1_, bf16[128,128]{1,0:T(8,128)(2,1)S(1)} %collective-permute-done.2.refs_2_, ...), custom_call_target="tpu_custom_call" | custom-call | flops 805306368 | bytes 3145728 | tf_op jit(solution)/shard_map/first_block/pallas_call | solution.py:422
  25.6 1.2 %collective-permute-start.4 = (bf16[256,512]{1,0:T(8,128)(2,1)S(1)}, bf16[256,512]{1,0:T(8,128)(2,1)S(1)}, u32[]{:S(2)}, u32[]{:S(2)}) collective-permute-start(bf16[256,512]{1,0:T(8,128)(2,1)S(1)} %get-tuple-element.31), channel_id=1, source_target_pairs={{0,3},{1,2},{2,1},{3,0},{4,7},{5,6},{6,5},{7,4},{8,11},{9,10},{10,... | collective-permute-start | bytes 786440 | tf_op jit(solution)/shard_map/ppermute | solution.py:564
  26.8 2.1 %attend.3 = bf16[256,512]{1,0:T(8,128)(2,1)S(1)} custom-call(bf16[512,128]{1,0:T(8,128)(2,1)S(1)} %get-tuple-element.32.refs_2_.refs_0_, bf16[256,1536]{1,0:T(8,128)(2,1)S(1)} %get-tuple-element.23.refs_5_.refs_3_.refs_1_, bf16[256,1536]{1,0:T(8,128)(2,1)S(1)} %get-tuple-element.24.refs_6_.refs_4_.refs_2_, ...), custom_call_target="tpu_custom_call" | custom-call | flops 65536 | bytes 262144 | tf_op jit(solution)/shard_map/attend/pallas_call | solution.py:453
  28.9 1.9 %collective-permute-start.6 = (bf16[256,512]{1,0:T(8,128)(2,1)S(1)}, bf16[256,512]{1,0:T(8,128)(2,1)S(1)}, u32[]{:S(2)}, u32[]{:S(2)}) collective-permute-start(bf16[256,512]{1,0:T(8,128)(2,1)S(1)} %attend.3), channel_id=1, source_target_pairs={{0,1},{1,0},{2,3},{3,2},{4,5},{5,4},{6,7},{7,6},{8,9},{9,8},{10,11... | collective-permute-start | bytes 786440 | tf_op jit(solution)/shard_map/ppermute | solution.py:564
  30.8 1.9 %attend.2 = bf16[256,512]{1,0:T(8,128)(2,1)S(1)} custom-call(bf16[512,128]{1,0:T(8,128)(2,1)S(1)} %get-tuple-element.32.refs_2_.refs_0_, bf16[256,1536]{1,0:T(8,128)(2,1)S(1)} %get-tuple-element.23.refs_5_.refs_3_.refs_1_, bf16[256,1536]{1,0:T(8,128)(2,1)S(1)} %get-tuple-element.24.refs_6_.refs_4_.refs_2_, ...), custom_call_target="tpu_custom_call" | custom-call | flops 65536 | bytes 262144 | tf_op jit(solution)/shard_map/attend/pallas_call | solution.py:453
  32.8 0.6 %collective-permute-start.5 = (bf16[256,512]{1,0:T(8,128)(2,1)S(1)}, bf16[256,512]{1,0:T(8,128)(2,1)S(1)}, u32[]{:S(2)}, u32[]{:S(2)}) collective-permute-start(bf16[256,512]{1,0:T(8,128)(2,1)S(1)} %attend.2), channel_id=1, source_target_pairs={{0,2},{1,3},{2,0},{3,1},{4,6},{5,7},{6,4},{7,5},{8,10},{9,11},{10,... | collective-permute-start | bytes 786440 | tf_op jit(solution)/shard_map/ppermute | solution.py:564
  33.3 2.4 %collective-permute-done.4.refs_1_ = bf16[256,512]{1,0:T(8,128)(2,1)S(1)} collective-permute-done((bf16[256,512]{1,0:T(8,128)(2,1)S(1)}, bf16[256,512]{1,0:T(8,128)(2,1)S(1)}, u32[]{:S(2)}, u32[]{:S(2)}) %collective-permute-start.4) | collective-permute-done | bytes 262176 | tf_op jit(solution)/shard_map/ppermute | solution.py:564
  35.7 2.7 %own_block.1.refs_1_ = bf16[256,2048]{1,0:T(8,128)(2,1)} custom-call(s32[1]{0:T(128)} %bitcast.refs_0_, bf16[256,512]{1,0:T(8,128)(2,1)S(1)} %collective-permute-done.4.refs_1_, bf16[512,128]{1,0:T(8,128)(2,1)S(1)} %get-tuple-element.32.refs_2_.refs_0_, bf16[256,1536]{1,0:T(8,128)(2,1)S(1)} %get-tuple-element.23.refs_5_.refs_3_.refs_1_, ...), custom_call_target="tpu_custom_call" | custom-call | flops 65536 | bytes 262144 | tf_op jit(solution)/shard_map/own_block/pallas_call | solution.py:517
  38.4 0.8 %collective-permute-done.6.refs_3_ = bf16[256,512]{1,0:T(8,128)(2,1)S(1)} collective-permute-done((bf16[256,512]{1,0:T(8,128)(2,1)S(1)}, bf16[256,512]{1,0:T(8,128)(2,1)S(1)}, u32[]{:S(2)}, u32[]{:S(2)}) %collective-permute-start.6) | collective-permute-done | bytes 262176 | tf_op jit(solution)/shard_map/ppermute | solution.py:564
  39.2 1.1 %collective-permute-done.5.refs_2_ = bf16[256,512]{1,0:T(8,128)(2,1)S(1)} collective-permute-done((bf16[256,512]{1,0:T(8,128)(2,1)S(1)}, bf16[256,512]{1,0:T(8,128)(2,1)S(1)}, u32[]{:S(2)}, u32[]{:S(2)}) %collective-permute-start.5) | collective-permute-done | bytes 262176 | tf_op jit(solution)/shard_map/ppermute | solution.py:564
  40.3 0.8 %rest.1 = bf16[256,2048]{1,0:T(8,128)(2,1)} custom-call(s32[1]{0:T(128)} %bitcast.refs_0_, bf16[256,2048]{1,0:T(8,128)(2,1)} %own_block.1.refs_1_, bf16[256,512]{1,0:T(8,128)(2,1)S(1)} %collective-permute-done.5.refs_2_, bf16[256,512]{1,0:T(8,128)(2,1)S(1)} %collective-permute-done.6.refs_3_), custom_call_target="tpu_custom_call", output_to_operand_aliasing={{}: (1, {})} | custom-call | bytes 1048576 | tf_op jit(solution)/shard_map/rest/pallas_call | solution.py:545
Async XLA Ops:
  0.9 11.7 %collective-permute-start = (bf16[8,1,64,128]{3,2,1,0:T(8,128)(2,1)S(1)}, bf16[8,1,64,128]{3,2,1,0:T(8,128)(2,1)S(1)}, u32[]{:S(2)}, u32[]{:S(2)}) collective-permute-start(bf16[8,1,64,128]{3,2,1,0:T(8,128)(2,1)S(1)} %slice.3), channel_id=1, source_target_pairs={{0,1},{1,2},{2,3},{4,5},{5,6},{6,7},{8,9},{9,10},{10,11},{12,13},{... | collective-permute-start | bytes 393224 | tf_op jit(solution)/shard_map/ppermute | solution.py:566
  5.8 6.9 %copy-start.1 = (bf16[256,16]{0,1:T(8,128)(2,1)S(1)}, bf16[256,16]{0,1:T(8,128)(2,1)}, u32[]{:S(2)}) copy-start(bf16[256,16]{0,1:T(8,128)(2,1)} %param.11) | copy-start | bytes 24580
  12.6 6.5 %copy-start = (f32[2,128]{1,0:T(2,128)S(1)}, f32[2,128]{1,0:T(2,128)}, u32[]{:S(2)}) copy-start(f32[2,128]{1,0:T(2,128)} %refs_5_.3) | copy-start | bytes 3076
  15.6 7.2 %collective-permute-start.1 = (bf16[128,128]{1,0:T(8,128)(2,1)S(1)}, bf16[128,128]{1,0:T(8,128)(2,1)S(1)}, u32[]{:S(2)}, u32[]{:S(2)}) collective-permute-start(bf16[128,128]{1,0:T(8,128)(2,1)S(1)} %get-tuple-element.22.refs_4_), channel_id=1, source_target_pairs={{0,3},{1,2},{2,1},{3,0},{4,7},{5,6},{6,5},{7,4},{8,11},{9,10},{10,... | collective-permute-start | bytes 98312 | tf_op jit(solution)/shard_map/ppermute | solution.py:564
  16.0 6.8 %collective-permute-start.2 = (bf16[128,128]{1,0:T(8,128)(2,1)S(1)}, bf16[128,128]{1,0:T(8,128)(2,1)S(1)}, u32[]{:S(2)}, u32[]{:S(2)}) collective-permute-start(bf16[128,128]{1,0:T(8,128)(2,1)S(1)} %get-tuple-element.22.refs_4_), channel_id=1, source_target_pairs={{0,2},{1,3},{2,0},{3,1},{4,6},{5,7},{6,4},{7,5},{8,10},{9,11},{10,... | collective-permute-start | bytes 98312 | tf_op jit(solution)/shard_map/ppermute | solution.py:564
  18.6 4.2 %collective-permute-start.3 = (bf16[128,128]{1,0:T(8,128)(2,1)S(1)}, bf16[128,128]{1,0:T(8,128)(2,1)S(1)}, u32[]{:S(2)}, u32[]{:S(2)}) collective-permute-start(bf16[128,128]{1,0:T(8,128)(2,1)S(1)} %get-tuple-element.22.refs_4_), channel_id=1, source_target_pairs={{0,1},{1,0},{2,3},{3,2},{4,5},{5,4},{6,7},{7,6},{8,9},{9,8},{10,11... | collective-permute-start | bytes 98312 | tf_op jit(solution)/shard_map/ppermute | solution.py:564
  25.6 10.1 %collective-permute-start.4 = (bf16[256,512]{1,0:T(8,128)(2,1)S(1)}, bf16[256,512]{1,0:T(8,128)(2,1)S(1)}, u32[]{:S(2)}, u32[]{:S(2)}) collective-permute-start(bf16[256,512]{1,0:T(8,128)(2,1)S(1)} %get-tuple-element.31), channel_id=1, source_target_pairs={{0,3},{1,2},{2,1},{3,0},{4,7},{5,6},{6,5},{7,4},{8,11},{9,10},{10,... | collective-permute-start | bytes 786440 | tf_op jit(solution)/shard_map/ppermute | solution.py:564
  28.9 10.2 %collective-permute-start.6 = (bf16[256,512]{1,0:T(8,128)(2,1)S(1)}, bf16[256,512]{1,0:T(8,128)(2,1)S(1)}, u32[]{:S(2)}, u32[]{:S(2)}) collective-permute-start(bf16[256,512]{1,0:T(8,128)(2,1)S(1)} %attend.3), channel_id=1, source_target_pairs={{0,1},{1,0},{2,3},{3,2},{4,5},{5,4},{6,7},{7,6},{8,9},{9,8},{10,11... | collective-permute-start | bytes 786440 | tf_op jit(solution)/shard_map/ppermute | solution.py:564
  32.8 7.5 %collective-permute-start.5 = (bf16[256,512]{1,0:T(8,128)(2,1)S(1)}, bf16[256,512]{1,0:T(8,128)(2,1)S(1)}, u32[]{:S(2)}, u32[]{:S(2)}) collective-permute-start(bf16[256,512]{1,0:T(8,128)(2,1)S(1)} %attend.2), channel_id=1, source_target_pairs={{0,2},{1,3},{2,0},{3,1},{4,6},{5,7},{6,4},{7,5},{8,10},{9,11},{10,... | collective-permute-start | bytes 786440 | tf_op jit(solution)/shard_map/ppermute | solution.py:564

commit v4 on v3

v4 whole, which is shorter than its diff:
```python
import math

import jax
import jax.numpy as jnp
from jax import lax
from jax.experimental import pallas as pl
from jax.experimental.pallas import tpu as pltpu
from jax.sharding import PartitionSpec as P

HS = 128
EPS = 1e-06
F32 = jnp.float32
BF16 = jnp.bfloat16
VMEM = pltpu.VMEM
MIB = 1024 * 1024


def vmem_spec():
    return pl.BlockSpec(memory_space=pltpu.VMEM)


def hbm_spec():
    return pl.BlockSpec(memory_space=pltpu.HBM)


def far(x):
    return pltpu.with_memory_space_constraint(x, pltpu.HBM)


def params(mib):
    return pltpu.CompilerParams(vmem_limit_bytes=mib * MIB)


def cost(flops, bytes_accessed, transcendentals=0):
    return pl.CostEstimate(
        flops=int(flops), bytes_accessed=int(bytes_accessed), transcendentals=int(transcendentals)
    )


def nbytes(*arrays):
    return sum(math.prod(a.shape) * a.dtype.itemsize for a in arrays)


def split(x):
    hi = x.astype(BF16)
    return hi, (x - hi.astype(F32)).astype(BF16)


def dot(a, b):
    return jnp.dot(a, b, preferred_element_type=F32)


def dot_nt(a, b):
    return lax.dot_general(a, b, (((1,), (1,)), ((), ())), preferred_element_type=F32)


def head_norm(v, gain):
    return (v * lax.rsqrt(jnp.mean(v * v, -1, keepdims=True) + EPS) * gain).astype(BF16)


def edge_kernel(video_hbm, text_hbm, mod_hbm, halo_ref, text_ref, mod_ref, sem):
    rows = video_hbm.shape[1]
    pairs = (
        (video_hbm.at[:, pl.ds(rows - 1, 1)], halo_ref),
        (mod_hbm, mod_ref),
        (text_hbm, text_ref),
    )
    copies = [pltpu.make_async_copy(src, dst, sem.at[i]) for i, (src, dst) in enumerate(pairs)]
    for c in copies:
        c.start()
    for c in copies:
        c.wait()


def edge(video, text, modulation):
    frames, _, cols, chans = video.shape
    return pl.pallas_call(
        edge_kernel,
        out_shape=(
            jax.ShapeDtypeStruct((frames, 1, cols, chans), BF16),
            jax.ShapeDtypeStruct(text.shape, BF16),
            jax.ShapeDtypeStruct(modulation.shape, F32),
        ),
        in_specs=[hbm_spec()] * 3,
        out_specs=(vmem_spec(),) * 3,
        scratch_shapes=[pltpu.SemaphoreType.DMA((3,))],
        compiler_params=params(4),
        cost_estimate=cost(0, 2 * nbytes(text, modulation)),
        name="edge",
    )(*[far(a) for a in (video, text, modulation)])


def text_kernel(
    chunks,
    text_ref,
    mod_ref,
    gain_ref,
    w_hbm,
    video_hbm,
    conv_hbm,
    e_hbm,
    key_ref,
    value_ref,
    video_ref,
    conv_ref,
    e_ref,
    w_ref,
    stream_ref,
    acc_ref,
    sem,
    w_sem,
):
    depth, parts, width = w_hbm.shape
    deep = depth // chunks
    copies = [
        pltpu.make_async_copy(w_hbm.at[pl.ds(c * deep, deep)], w_ref.at[pl.ds(c * deep, deep)], w_sem.at[c])
        for c in range(chunks)
    ]
    pairs = (
        (video_hbm, video_ref),
        (conv_hbm, conv_ref),
        (e_hbm, e_ref),
    )
    ahead = [pltpu.make_async_copy(src, dst, sem.at[i]) for i, (src, dst) in enumerate(pairs)]
    for c in copies:
        c.start()
    few = 16
    for r in range(0, text_ref.shape[0], few):
        text = text_ref[r : r + few, :].astype(F32)
        centred = text - jnp.mean(text, -1, keepdims=True)
        normed = centred * lax.rsqrt(jnp.mean(centred * centred, -1, keepdims=True) + EPS)
        stream_ref[r : r + few, :] = (normed * (1.0 + mod_ref[3:4, :]) + mod_ref[2:3, :]).astype(BF16)
    step = 128
    row = lax.broadcasted_iota(jnp.int32, (2 * step, 2 * step), 0)
    col = lax.broadcasted_iota(jnp.int32, (2 * step, 2 * step), 1)
    pick = jnp.where(col == 2 * (row % step) + row // step, 1.0, 0.0).astype(BF16)
    flat = w_ref.reshape(depth * parts, width)
    for c in range(chunks):
        copies[c].wait()
        if c == 0:
            for copy in ahead:
                copy.start()
        pieces = ([], [])
        for s in range(deep // step):
            at = 2 * (c * deep + s * step)
            both = dot(pick, flat[at : at + 2 * step, :]).astype(BF16)
            pieces[0].append(both[:step])
            pieces[1].append(both[step:])
        stream = stream_ref[:, c * deep : (c + 1) * deep]
        for p in range(2):
            term = dot(stream, jnp.concatenate(pieces[p], 0))
            if c == 0:
                acc_ref[p] = term
            else:
                acc_ref[p] += term
    for h in range(width // HS):
        at = slice(h * HS, (h + 1) * HS)
        key_ref[h] = head_norm(acc_ref[0, :, at], gain_ref[1:2, :])
        value_ref[h] = acc_ref[1, :, at].astype(BF16)
    for c in ahead:
        c.wait()


def text_side(text, modulation, gain, weight, video, conv_weight, embed_weight):
    depth, parts, width = weight.shape
    count = text.shape[0]
    heads = width // HS
    chunks = 3
    return pl.pallas_call(
        lambda *refs: text_kernel(chunks, *refs),
        out_shape=(
            jax.ShapeDtypeStruct((heads, count, HS), BF16),
            jax.ShapeDtypeStruct((heads, count, HS), BF16),
            jax.ShapeDtypeStruct(video.shape, BF16),
            jax.ShapeDtypeStruct(conv_weight.shape, BF16),
            jax.ShapeDtypeStruct(embed_weight.shape, BF16),
        ),
        in_specs=[vmem_spec()] * 3 + [hbm_spec()] * 4,
        out_specs=(vmem_spec(),) * 5,
        scratch_shapes=[
            VMEM((depth, parts, width), BF16),
            VMEM((count, depth), BF16),
            VMEM((parts, count, width), F32),
            pltpu.SemaphoreType.DMA((3,)),
            pltpu.SemaphoreType.DMA((chunks,)),
        ],
        compiler_params=params(24),
        cost_estimate=cost(4 * count * depth * parts * width, nbytes(weight, text, video, conv_weight)),
        name="text_side",
    )(text, modulation, gain, *[far(a) for a in (weight, video, conv_weight, embed_weight)])


def fold_kernel(
    e_ref,
    mod_ref,
    w0_ref,
    w_hbm,
    rhs0_ref,
    rhs1_ref,
    shift_ref,
    gram_ref,
    lhs_ref,
    both_ref,
    acc_ref,
    w1_ref,
    sem,
):
    parts, deep0, width = w0_ref.shape
    pi, depth = e_ref.shape
    copies = [
        pltpu.make_async_copy(w_hbm.at[p, pl.ds(deep0, depth - deep0)], w1_ref.at[p], sem.at[p])
        for p in range(parts)
    ]
    for c in copies:
        c.start()
    few = 16
    for r in range(0, pi, few):
        e = e_ref[r : r + few, :].astype(F32)
        centred = e - jnp.mean(e, -1, keepdims=True)
        hi, lo = split(centred * (1.0 + mod_ref[1:2, :]))
        lhs_ref[r : r + few, :] = hi
        lhs_ref[pi + r : pi + r + few, :] = lo
        hi, lo = split(centred)
        both_ref[r : r + few, :] = hi
        both_ref[pi + r : pi + r + few, :] = lo
    shift_hi, shift_lo = split(mod_ref[0:1, :])
    lhs_ref[2 * pi :, :] = jnp.concatenate(
        [shift_hi.astype(F32), shift_lo.astype(F32), jnp.zeros((14, depth), F32)], 0
    ).astype(BF16)
    gram = dot_nt(both_ref[...], both_ref[...])
    lane = lax.broadcasted_iota(jnp.int32, (pi, 2 * pi), 1)
    gram = gram[:pi] + jnp.where(lane < pi, gram[pi:], 0.0)
    gram = gram + pltpu.roll(gram, pi, 1)
    gram = jnp.concatenate([gram, gram], 0)
    row = lax.broadcasted_iota(jnp.int32, gram.shape, 0) // pi
    col = lax.broadcasted_iota(jnp.int32, gram.shape, 1) // pi
    ghi, glo = split(jnp.where(row == col, gram * (1.0 / depth), 0.0))
    gram_ref[...] = jnp.concatenate([ghi, glo], 0)
    for p in range(parts):
        at = slice(p * width, (p + 1) * width)
        acc_ref[:, at] = dot(lhs_ref[:, :deep0], w0_ref[p])
    for p in range(parts):
        at = slice(p * width, (p + 1) * width)
        copies[p].wait()
        acc_ref[:, at] += dot(lhs_ref[:, deep0:], w1_ref[p])
    total = acc_ref[...]
    hi, lo = split(total[:pi] + total[pi : 2 * pi])
    none = jnp.zeros_like(hi)
    rhs0_ref[...] = jnp.concatenate([hi, none, lo, none], 0)
    rhs1_ref[...] = jnp.concatenate([none, hi, none, lo], 0)
    shift_ref[...] = total[2 * pi : 2 * pi + 1] + total[2 * pi + 1 : 2 * pi + 2]


def fold(embed_weight, modulation, weight0, weight):
    parts, taken, width = weight0.shape
    pi, depth = embed_weight.shape
    cols = parts * width
    return pl.pallas_call(
        fold_kernel,
        out_shape=(
            jax.ShapeDtypeStruct((4 * pi, cols), BF16),
            jax.ShapeDtypeStruct((4 * pi, cols), BF16),
            jax.ShapeDtypeStruct((1, cols), F32),
            jax.ShapeDtypeStruct((4 * pi, 2 * pi), BF16),
        ),
        in_specs=[vmem_spec()] * 3 + [hbm_spec()],
        out_specs=(vmem_spec(),) * 4,
        scratch_shapes=[
            VMEM((2 * pi + 16, depth), BF16),
            VMEM((2 * pi, depth), BF16),
            VMEM((2 * pi + 16, cols), F32),
            VMEM((parts, depth - taken, width), BF16),
            pltpu.SemaphoreType.DMA((parts,)),
        ],
        compiler_params=params(12),
        cost_estimate=cost(2 * 144 * depth * cols, nbytes(weight, embed_weight, modulation)),
        name="fold",
    )(embed_weight, modulation, weight0, far(weight))


def conv_kernel(
    chunks,
    video_ref,
    halo_ref,
    weight_ref,
    latent_ref,
    qkv_hbm,
    out_ref,
    qkv_ref,
    wide_ref,
    even_ref,
    odd_ref,
    left_ref,
    spread_ref,
    sem,
):
    deep = qkv_ref.shape[1] // chunks
    ahead = [
        pltpu.make_async_copy(
            qkv_hbm.at[p, pl.ds(c * deep, deep)], qkv_ref.at[p, pl.ds(c * deep, deep)], sem.at[p, c]
        )
        for p in range(qkv_ref.shape[0])
        for c in range(chunks)
    ]
    for copy in ahead:
        copy.start()
    frames, rows, cols, chans = video_ref.shape
    block = cols + 8
    half = cols // 2
    quarter = cols // 4
    for r in range(rows + 1):
        for f in range(frames):
            base = (r * frames + f) * block
            pixels = halo_ref[f, 0] if r == 0 else video_ref[f, r - 1]
            wide_ref[base : base + 8, :] = jnp.zeros((8, chans), F32)
            wide_ref[base + 8 : base + block, :] = pixels.astype(F32)
            at = [wide_ref[pl.ds(base + 7 + o, quarter, stride=4), :] for o in range(5)]
            even = jnp.concatenate([at[1], at[3]], 0).astype(BF16)
            odd = jnp.concatenate([at[2], at[4]], 0).astype(BF16)
            left = jnp.concatenate([at[0], at[2]], 0).astype(BF16)
            for t in (range(3) if f == 0 else (f + 2,)):
                even_ref[r, t] = even
                odd_ref[r, t] = odd
                left_ref[r, t] = left
    lat, mid = latent_ref.shape
    tall = rows // 2
    spread_ref[...] = jnp.zeros_like(spread_ref)
    for s in range(2 * tall):
        spread_ref[s * lat : (s + 1) * lat, s * mid : (s + 1) * mid] = latent_ref[...]
    pieces = []
    for j in range(tall):
        taps = []
        for kt in range(3):
            for kr in range(3):
                for ref in (left_ref, even_ref, odd_ref):
                    taps.append(ref[2 * j + kr, kt : kt + frames].reshape(frames * half, chans))
        conv = dot(jnp.concatenate(taps, 1), weight_ref[...])
        act = (conv * (1.0 / (1.0 + jnp.exp(-conv)))).astype(BF16)
        for b in range(2):
            pieces.append(
                jnp.concatenate(
                    [act[f * half + b * quarter : f * half + (b + 1) * quarter] for f in range(frames)], 0
                )
            )
    out_ref[...] = dot_nt(jnp.concatenate(pieces, 1), spread_ref[...]).astype(BF16)
    for copy in ahead:
        copy.wait()


def conv_side(video, halo, weight, latent_weight, qkv_weight, taken):
    frames, rows, cols, chans = video.shape
    parts, depth, width = qkv_weight.shape
    mid = weight.shape[-1]
    lat = latent_weight.shape[1]
    latent = latent_weight.T
    half = cols // 2
    tall = rows // 2
    chunks = 1
    return pl.pallas_call(
        lambda *refs: conv_kernel(chunks, *refs),
        out_shape=(
            jax.ShapeDtypeStruct((frames * half // 2, 2 * tall * lat), BF16),
            jax.ShapeDtypeStruct((parts, taken, width), BF16),
        ),
        in_specs=[vmem_spec()] * 4 + [hbm_spec()],
        out_specs=(vmem_spec(),) * 2,
        scratch_shapes=[VMEM(((rows + 1) * frames * (cols + 8), chans), F32)]
        + [VMEM((rows + 1, frames + 2, half, chans), BF16)] * 3
        + [VMEM((2 * tall * lat, 2 * tall * mid), BF16), pltpu.SemaphoreType.DMA((parts, chunks))],
        compiler_params=params(24),
        cost_estimate=cost(
            2 * frames * tall * half * 27 * chans * mid, nbytes(video, halo, weight)
        ),
        name="conv_side",
    )(video, halo, weight, latent, far(qkv_weight))


def token_scales(x, xx, gram_ref):
    quad = dot(xx, gram_ref[...]) * x.astype(F32)
    lane = lax.broadcasted_iota(jnp.int32, quad.shape, 1)
    low = lane < quad.shape[1] // 2
    scales = []
    for i in range(2):
        var = jnp.sum(jnp.where(low if i == 0 else ~low, quad, 0.0), -1, keepdims=True)
        scales.append(lax.rsqrt(jnp.maximum(var, 0.0) + EPS))
    return scales


def block_queries(n, own, x, xx, scales, rhs_refs, shift_ref, gain_ref, query_ref):
    heads = query_ref.shape[0]
    span = x.shape[0] // n
    grain = span // own
    gain = gain_ref[0:1, :] * (math.log2(math.e) / math.sqrt(HS))
    for i in range(2):
        at = slice(0, heads * HS)
        projected = dot(xx, rhs_refs[i][:, at]) * scales[i] + shift_ref[:, at]
        for h in range(heads):
            v = head_norm(projected[:, h * HS : (h + 1) * HS], gain)
            for s in range(n):
                for f in range(own):
                    to = f * (n * 2 * grain) + (s * 2 + i) * grain
                    come = s * span + f * grain
                    query_ref[h, to : to + grain, :] = v[come : come + grain]


def attention(query_ref, key_ref, value_ref, out_ref):
    heads, total, _ = key_ref.shape
    for h in range(heads):
        weights = jnp.exp2(dot_nt(query_ref[h], key_ref[h]))
        norm = weights[:, :HS]
        for c in range(HS, total, HS):
            norm = norm + weights[:, c : c + HS]
        norm = jnp.sum(norm, -1, keepdims=True)
        attended = dot(weights.astype(BF16), value_ref[h])
        out_ref[:, h * HS : (h + 1) * HS] = (attended / norm).astype(BF16)


def first_kernel(order, frames, *refs):
    n = len(order)
    patch_refs = refs[:n]
    rhs0_ref, rhs1_ref, shift_ref, gram_ref, gain_ref, tkey_ref, tvalue_ref = refs[n : n + 7]
    out_ref, x_ref, key_ref, value_ref, patch_scr, query_ref = refs[n + 7 :]
    me = lax.axis_index("ctx")
    rhs_refs = (rhs0_ref, rhs1_ref)
    heads, count, _ = tkey_ref.shape
    rows = patch_refs[0].shape[1]
    for k, ref in zip(order, patch_refs):
        patch_scr[pl.ds(pl.multiple_of((me ^ k) * rows, rows), rows), :] = ref[...]
    key_ref[:, 0:count, :] = tkey_ref[...]
    value_ref[:, 0:count, :] = tvalue_ref[...]
    own = frames // n
    span = rows // n
    for j, k in enumerate(order):
        for s in range(n):
            at = pl.multiple_of((me ^ k) * span, span) + s * rows
            x_ref[j * rows + s * span : j * rows + (s + 1) * span, :] = patch_scr[
                pl.ds(pl.multiple_of(at, span), span), :
            ]
    x = x_ref[...]
    xx = jnp.concatenate([x, x], 1)
    scales = token_scales(x, xx, gram_ref)
    width = heads * HS
    for i in range(2):
        for p in (1, 2):
            for h0 in range(0, heads, 2):
                at = slice(p * width + h0 * HS, p * width + (h0 + 2) * HS)
                pair = dot(xx, rhs_refs[i][:, at]) * scales[i] + shift_ref[:, at]
                for h in (h0, h0 + 1):
                    v = pair[:, (h - h0) * HS : (h - h0 + 1) * HS]
                    to = slice(count + i * n * rows, count + (i + 1) * n * rows)
                    if p == 1:
                        key_ref[h, to, :] = head_norm(v, gain_ref[1:2, :])
                    else:
                        value_ref[h, to, :] = v.astype(BF16)
    block_queries(
        n, own, x[:rows], xx[:rows], [v[:rows] for v in scales], rhs_refs, shift_ref, gain_ref, query_ref
    )
    attention(query_ref, key_ref, value_ref, out_ref)


def first_block(order, frames, patches, rhs0, rhs1, shift, gram, gain, tkey, tvalue):
    n = len(order)
    heads, count, _ = tkey.shape
    rows = patches[0].shape[1]
    total = count + 2 * n * rows
    return pl.pallas_call(
        lambda *refs: first_kernel(order, frames, *refs),
        out_shape=(
            jax.ShapeDtypeStruct((2 * rows, heads * HS), BF16),
            jax.ShapeDtypeStruct((n * rows, rows), BF16),
            jax.ShapeDtypeStruct((heads, total, HS), BF16),
            jax.ShapeDtypeStruct((heads, total, HS), BF16),
        ),
        in_specs=[vmem_spec()] * (n + 7),
        out_specs=(vmem_spec(),) * 4,
        scratch_shapes=[VMEM((n * rows, rows), BF16), VMEM((heads, 2 * rows, HS), BF16)],
        compiler_params=params(16),
        cost_estimate=cost(2 * 2 * n * rows * 256 * 3 * heads * HS, 4 * nbytes(rhs0)),
        name="first_block",
    )(*patches, rhs0, rhs1, shift, gram, gain, tkey, tvalue)


def attend_kernel(
    n, own, j, x_ref, rhs0_ref, rhs1_ref, shift_ref, gram_ref, gain_ref, key_ref, value_ref, out_ref, query_ref
):
    rows = x_ref.shape[1]
    x = x_ref[j * rows : (j + 1) * rows, :]
    xx = jnp.concatenate([x, x], 1)
    scales = token_scales(x, xx, gram_ref)
    block_queries(n, own, x, xx, scales, (rhs0_ref, rhs1_ref), shift_ref, gain_ref, query_ref)
    attention(query_ref, key_ref, value_ref, out_ref)


def attend(n, frames, j, x, rhs0, rhs1, shift, gram, gain, key, value):
    heads = key.shape[0]
    rows = x.shape[1]
    return pl.pallas_call(
        lambda *refs: attend_kernel(n, frames // n, j, *refs),
        out_shape=jax.ShapeDtypeStruct((2 * rows, heads * HS), BF16),
        in_specs=[vmem_spec()] * 8,
        out_specs=vmem_spec(),
        scratch_shapes=[VMEM((heads, 2 * rows, HS), BF16)],
        compiler_params=params(12),
        cost_estimate=cost(heads * rows * HS, 2 * nbytes(x)),
        name="attend",
    )(x, rhs0, rhs1, shift, gram, gain, key, value)


def place(block, k, out_ref, sem):
    width = block.shape[1]
    at = pl.multiple_of((lax.axis_index("ctx") ^ k) * width, width)
    return pltpu.make_async_copy(block, out_ref.at[:, pl.ds(at, width)], sem)


def own_kernel(
    n,
    own,
    far,
    far_ref,
    x_ref,
    rhs0_ref,
    rhs1_ref,
    shift_ref,
    gram_ref,
    gain_ref,
    key_ref,
    value_ref,
    out_ref,
    query_ref,
    block_ref,
    sem,
):
    first = place(far_ref, far, out_ref, sem.at[0])
    first.start()
    attend_kernel(
        n,
        own,
        n - 1,
        x_ref,
        rhs0_ref,
        rhs1_ref,
        shift_ref,
        gram_ref,
        gain_ref,
        key_ref,
        value_ref,
        block_ref,
        query_ref,
    )
    second = place(block_ref, 0, out_ref, sem.at[1])
    second.start()
    first.wait()
    second.wait()


def own_block(n, frames, far, far_block, x, rhs0, rhs1, shift, gram, gain, key, value):
    heads = key.shape[0]
    rows = x.shape[1]
    width = heads * HS
    return pl.pallas_call(
        lambda *refs: own_kernel(n, frames // n, far, *refs),
        out_shape=jax.ShapeDtypeStruct((2 * rows, n * width), BF16),
        in_specs=[vmem_spec()] * 9,
        out_specs=hbm_spec(),
        scratch_shapes=[
            VMEM((heads, 2 * rows, HS), BF16),
            VMEM((2 * rows, width), BF16),
            pltpu.SemaphoreType.DMA((2,)),
        ],
        compiler_params=params(12),
        cost_estimate=cost(heads * rows * HS, 2 * nbytes(x)),
        name="own_block",
    )(far_block, x, rhs0, rhs1, shift, gram, gain, key, value)


def rest_kernel(order, out_in_ref, *refs):
    n = len(order)
    out_ref, sem = refs[n:]
    copies = [place(refs[j], k, out_ref, sem.at[j]) for j, k in enumerate(order)]
    for c in copies:
        c.start()
    for c in copies:
        c.wait()


def rest(order, out, blocks):
    n = len(order)
    return pl.pallas_call(
        lambda *refs: rest_kernel(order, *refs),
        out_shape=jax.ShapeDtypeStruct(out.shape, BF16),
        in_specs=[hbm_spec()] + [vmem_spec()] * n,
        out_specs=hbm_spec(),
        scratch_shapes=[pltpu.SemaphoreType.DMA((n,))],
        input_output_aliases={0: 0},
        compiler_params=params(4),
        cost_estimate=cost(0, 2 * n * nbytes(blocks[0])),
        name="rest",
    )(out, *blocks)


def shards(video, conv_weight, latent_weight, embed_weight, modulation, qkv_weight, qk_gain, text, text_weight):
    n = lax.axis_size("ctx")
    frames = video.shape[0]

    def swap(x, k):
        return lax.ppermute(x, "ctx", [(i, i ^ k) for i in range(n)])

    weight = qkv_weight.transpose(1, 0, 2)
    edge_row, text_near, mod_near = edge(video, text, modulation)
    halo = lax.ppermute(edge_row, "ctx", [(i, i + 1) for i in range(n - 1)])
    tkey, tvalue, tile, taps, e_near = text_side(
        text_near,
        mod_near,
        qk_gain,
        text_weight,
        video,
        conv_weight.reshape(-1, conv_weight.shape[-1]),
        embed_weight,
    )
    patches, weight_near = conv_side(tile, halo, taps, latent_weight, weight, weight.shape[1] * 2 // 3)
    order = tuple(range(n - 1, -1, -1))
    received = [swap(patches, k) if k else patches for k in order]
    rhs0, rhs1, shift, gram = fold(e_near, mod_near, weight_near, weight)
    block, x, key, value = first_block(
        order, frames, received, rhs0, rhs1, shift, gram, qk_gain, tkey, tvalue
    )
    far_block = swap(block, order[0])
    common = (x, rhs0, rhs1, shift, gram, qk_gain, key, value)
    blocks = [swap(attend(n, frames, j, *common), order[j]) for j in range(1, n - 1)]
    out = own_block(n, frames, order[0], far_block, *common)
    return rest(order[1 : n - 1], out, blocks)


def solution(mesh):
    in_specs = (
        P("dp", "ctx", None, None),
        P(),
        P(),
        P(),
        P("dp", None),
        P(None, None, "ctx"),
        P(),
        P("dp", None),
        P(None, None, "ctx"),
    )
    out_specs = P(("dp", "ctx"), None)
    return jax.shard_map(shards, mesh=mesh, in_specs=in_specs, out_specs=out_specs, check_vma=False)
```

time: 41.4 us -> 39.2 us (0.947)
  waiting for transfers between devices: 4.3 us -> 3.21 us
  local copies, waits for them, and re-layouts: 0.93 us -> 0.01 us
    ppermute x6, waiting for transfers between devices: 4.3 us -> 3.21 us  [swap(): return lax.ppermute(x, 'ctx', [(i, i ^ k) for i in range(n)])]
    slice x1 -> x0, local copies, waits for them, and re-layouts: 0.91 us -> none  [shards(): video[:, -1:]]
    pallas_call x2 -> x3, Pallas kernels: 10.5 us -> 10.1 us  [the longest x1 5.23 us: text_side(): pl.pallas_call(lambda *refs: text_kernel(chunks, *refs), out_shape=(jax.S...]
  transfers between devices with their start and end apart: 7 -> 7, of which waited for: 3 -> 3; matrix products, arithmetic and copies ran while one was open for 0% -> 0% of each run, Pallas kernels for 42% -> 39%
where the time goes in v4:
time: 39.2 us; the launch traced here: 39 us
  Pallas kernels  23.4 us (60%)
  starting transfers between devices  12.1 us (31%)
  waiting for transfers between devices  3.21 us (8%)
    ppermute x6, starting transfers between devices, swap(): return lax.ppermute(x, 'ctx', [(i, i ^ k) for i in range(n)])  7.24 us
    pallas_call x1, Pallas kernels, text_side(): pl.pallas_call(lambda *refs: text_kernel(chunks, *refs), out_shape=(jax.S...  5.23 us
    ppermute x1, starting transfers between devices, shards(): halo = lax.ppermute(edge_row, 'ctx', [(i, i + 1) for i in range(n - 1)])  4.85 us
    pallas_call x2, Pallas kernels, attend(): pl.pallas_call(lambda *refs: attend_kernel(n, frames // n, j, *refs), out...  4.09 us
    pallas_call x1, Pallas kernels, fold(): pl.pallas_call(fold_kernel, out_shape=(jax.ShapeDtypeStruct((4 * pi, cols...  3.28 us
    ppermute x6, waiting for transfers between devices, swap(): return lax.ppermute(x, 'ctx', [(i, i ^ k) for i in range(n)])  3.21 us
    pallas_call x1, Pallas kernels, conv_side(): pl.pallas_call(lambda *refs: conv_kernel(chunks, *refs), out_shape=(jax.S...  2.9 us
    pallas_call x1, Pallas kernels, first_block(): pl.pallas_call(lambda *refs: first_kernel(order, frames, *refs), out_shap...  2.87 us
  transfers between devices with their start and end apart: 7, of which 3 were waited for; matrix products, arithmetic and copies ran while one was open for 0% of the time, Pallas kernels for 39%

profile of v4, /device:TPU:0, one launch (start us, length us, event | category | flops | bytes accessed | tf_op | source)
XLA Modules:
  0.0 39.0 jit_solution(16239039517587967460)
XLA Ops:
  0.0 0.0 copy-start
  0.0 1.6 %edge.1 = (bf16[8,1,64,128]{3,2,1,0:T(8,128)(2,1)S(1)}, bf16[256,3072]{1,0:T(8,128)(2,1)S(1)}, f32[4,3072]{1,0:T(4,128)S(1)}) custom-call(bf16[8,8,64,128]{3,2,1,0:T(8,128)(2,1)} %refs_4_.1, bf16[256,3072]{1,0:T(8,128)(2,1)} %text_hbm.1, f32[4,3072]{1,0:T(4,128)} %mod_hbm.1), custom_call_target="tpu_custom_call" | custom-call | bytes 3244032 | tf_op jit(solution)/shard_map/edge/pallas_call | solution.py:77
  1.6 4.8 %collective-permute-start = (bf16[8,1,64,128]{3,2,1,0:T(8,128)(2,1)S(1)}, bf16[8,1,64,128]{3,2,1,0:T(8,128)(2,1)S(1)}, u32[]{:S(2)}, u32[]{:S(2)}) collective-permute-start(bf16[8,1,64,128]{3,2,1,0:T(8,128)(2,1)S(1)} %get-tuple-element.26), channel_id=1, source_target_pairs={{0,1},{1,2},{2,3},{4,5},{5,6},{6,7},{8,9},{9,10},{10,11},{12,13},{... | collective-permute-start | bytes 393224 | tf_op jit(solution)/shard_map/ppermute | solution.py:610
  6.4 0.0 copy-done
  6.4 0.0 copy-start.1
  6.4 5.2 %text_side.1 = (bf16[4,256,128]{2,1,0:T(8,128)(2,1)S(1)}, bf16[4,256,128]{2,1,0:T(8,128)(2,1)S(1)}, bf16[8,8,64,128]{3,2,1,0:T(8,128)(2,1)S(1)}, bf16[3456,256]{1,0:T(8,128)(2,1)S(1)}, bf16[64,3072]{1,0:T(8,128)(2,1)S(1)}) custom-call(bf16[256,3072]{1,0:T(8,128)(2,1)S(1)} %get-tuple-element.23.refs_0_, f32[4,3072]{1,0:T(4,128)S(1)} %get-tuple-element.24.refs_1_.mod_ref, ...), custom_call_target="tpu_custom_call" | custom-call | flops 3221225472 | bytes 10682368 | tf_op jit(solution)/shard_map/text_side/pallas_call | solution.py:169
  11.7 0.0 collective-permute-done.refs_1_
  11.7 0.0 copy-done.1
  11.7 2.9 %conv_side.1 = (bf16[128,128]{1,0:T(8,128)(2,1)S(1)}, bf16[3,2048,512]{2,1,0:T(8,128)(2,1)S(1)}) custom-call(bf16[8,8,64,128]{3,2,1,0:T(8,128)(2,1)S(1)} %get-tuple-element.25.refs_0_, bf16[8,1,64,128]{3,2,1,0:T(8,128)(2,1)S(1)} %collective-permute-done.refs_1_, bf16[3456,256]{1,0:T(8,128)(2,1)S(1)} %get-tuple-element.27.refs_2_, ...), custom_call_target="tpu_custom_call" | custom-call | flops 1811939328 | bytes 2949120 | tf_op jit(solution)/shard_map/conv_side/pallas_call | solution.py:359
  14.6 1.6 %collective-permute-start.3 = (bf16[128,128]{1,0:T(8,128)(2,1)S(1)}, bf16[128,128]{1,0:T(8,128)(2,1)S(1)}, u32[]{:S(2)}, u32[]{:S(2)}) collective-permute-start(bf16[128,128]{1,0:T(8,128)(2,1)S(1)} %get-tuple-element.28.refs_3_), channel_id=1, source_target_pairs={{0,1},{1,0},{2,3},{3,2},{4,5},{5,4},{6,7},{7,6},{8,9},{9,8},{10,11... | collective-permute-start | bytes 98312 | tf_op jit(solution)/shard_map/ppermute | solution.py:606
  16.2 0.1 collective-permute-start.2
  16.3 1.9 %collective-permute-start.1 = (bf16[128,128]{1,0:T(8,128)(2,1)S(1)}, bf16[128,128]{1,0:T(8,128)(2,1)S(1)}, u32[]{:S(2)}, u32[]{:S(2)}) collective-permute-start(bf16[128,128]{1,0:T(8,128)(2,1)S(1)} %get-tuple-element.28.refs_3_), channel_id=1, source_target_pairs={{0,3},{1,2},{2,1},{3,0},{4,7},{5,6},{6,5},{7,4},{8,11},{9,10},{10,... | collective-permute-start | bytes 98312 | tf_op jit(solution)/shard_map/ppermute | solution.py:606
  18.2 3.3 %fold.1 = (bf16[256,1536]{1,0:T(8,128)(2,1)S(1)}, bf16[256,1536]{1,0:T(8,128)(2,1)S(1)}, f32[1,1536]{1,0:T(1,128)S(1)}, bf16[256,128]{1,0:T(8,128)(2,1)S(1)}) custom-call(bf16[64,3072]{1,0:T(8,128)(2,1)S(1)} %get-tuple-element.29.e_ref, f32[4,3072]{1,0:T(4,128)S(1)} %get-tuple-element.24.refs_1_.mod_ref, bf16[3,2048,512]{2,1,0:T(8,128)(2,1)S(1)} %get-tuple-element.30.w0_ref, ...), custom_call_target="tpu_custom_call" | custom-call | flops 1358954496 | bytes 9879552 | tf_op jit(solution)/shard_map/fold/pallas_call | solution.py:258
  21.5 0.0 collective-permute-done.3.refs_2_
  21.5 0.0 collective-permute-done.2.refs_1_
  21.5 0.0 collective-permute-done.1.refs_0_
  21.5 2.9 %first_block.1 = (bf16[256,512]{1,0:T(8,128)(2,1)S(1)}, bf16[512,128]{1,0:T(8,128)(2,1)S(1)}, bf16[4,1280,128]{2,1,0:T(8,128)(2,1)S(1)}, bf16[4,1280,128]{2,1,0:T(8,128)(2,1)S(1)}) custom-call(bf16[128,128]{1,0:T(8,128)(2,1)S(1)} %collective-permute-done.1.refs_0_, bf16[128,128]{1,0:T(8,128)(2,1)S(1)} %collective-permute-done.2.refs_1_, ...), custom_call_target="tpu_custom_call" | custom-call | flops 805306368 | bytes 3145728 | tf_op jit(solution)/shard_map/first_block/pallas_call | solution.py:466
  24.4 1.6 %collective-permute-start.4 = (bf16[256,512]{1,0:T(8,128)(2,1)S(1)}, bf16[256,512]{1,0:T(8,128)(2,1)S(1)}, u32[]{:S(2)}, u32[]{:S(2)}) collective-permute-start(bf16[256,512]{1,0:T(8,128)(2,1)S(1)} %get-tuple-element.37), channel_id=1, source_target_pairs={{0,3},{1,2},{2,1},{3,0},{4,7},{5,6},{6,5},{7,4},{8,11},{9,10},{10,... | collective-permute-start | bytes 786440 | tf_op jit(solution)/shard_map/ppermute | solution.py:606
  25.9 2.1 %attend.2 = bf16[256,512]{1,0:T(8,128)(2,1)S(1)} custom-call(bf16[512,128]{1,0:T(8,128)(2,1)S(1)} %get-tuple-element.38.refs_1_.refs_0_, bf16[256,1536]{1,0:T(8,128)(2,1)S(1)} %get-tuple-element.31.refs_4_.refs_2_.refs_1_, bf16[256,1536]{1,0:T(8,128)(2,1)S(1)} %get-tuple-element.32.refs_5_.refs_3_.refs_2_, ...), custom_call_target="tpu_custom_call" | custom-call | flops 65536 | bytes 262144 | tf_op jit(solution)/shard_map/attend/pallas_call | solution.py:497
  28.1 1.6 %collective-permute-start.5 = (bf16[256,512]{1,0:T(8,128)(2,1)S(1)}, bf16[256,512]{1,0:T(8,128)(2,1)S(1)}, u32[]{:S(2)}, u32[]{:S(2)}) collective-permute-start(bf16[256,512]{1,0:T(8,128)(2,1)S(1)} %attend.2), channel_id=1, source_target_pairs={{0,2},{1,3},{2,0},{3,1},{4,6},{5,7},{6,4},{7,5},{8,10},{9,11},{10,... | collective-permute-start | bytes 786440 | tf_op jit(solution)/shard_map/ppermute | solution.py:606
  29.6 1.9 %attend.3 = bf16[256,512]{1,0:T(8,128)(2,1)S(1)} custom-call(bf16[512,128]{1,0:T(8,128)(2,1)S(1)} %get-tuple-element.38.refs_1_.refs_0_, bf16[256,1536]{1,0:T(8,128)(2,1)S(1)} %get-tuple-element.31.refs_4_.refs_2_.refs_1_, bf16[256,1536]{1,0:T(8,128)(2,1)S(1)} %get-tuple-element.32.refs_5_.refs_3_.refs_2_, ...), custom_call_target="tpu_custom_call" | custom-call | flops 65536 | bytes 262144 | tf_op jit(solution)/shard_map/attend/pallas_call | solution.py:497
  31.6 0.6 %collective-permute-start.6 = (bf16[256,512]{1,0:T(8,128)(2,1)S(1)}, bf16[256,512]{1,0:T(8,128)(2,1)S(1)}, u32[]{:S(2)}, u32[]{:S(2)}) collective-permute-start(bf16[256,512]{1,0:T(8,128)(2,1)S(1)} %attend.3), channel_id=1, source_target_pairs={{0,1},{1,0},{2,3},{3,2},{4,5},{5,4},{6,7},{7,6},{8,9},{9,8},{10,11... | collective-permute-start | bytes 786440 | tf_op jit(solution)/shard_map/ppermute | solution.py:606
  32.1 0.2 collective-permute-done.4.refs_0_
  32.3 2.7 %own_block.1.refs_0_ = bf16[256,2048]{1,0:T(8,128)(2,1)} custom-call(bf16[256,512]{1,0:T(8,128)(2,1)S(1)} %collective-permute-done.4.refs_0_, bf16[512,128]{1,0:T(8,128)(2,1)S(1)} %get-tuple-element.38.refs_1_.refs_0_, bf16[256,1536]{1,0:T(8,128)(2,1)S(1)} %get-tuple-element.31.refs_4_.refs_2_.refs_1_, ...), custom_call_target="tpu_custom_call" | custom-call | flops 65536 | bytes 262144 | tf_op jit(solution)/shard_map/own_block/pallas_call | solution.py:560
  35.0 2.8 %collective-permute-done.5.refs_1_ = bf16[256,512]{1,0:T(8,128)(2,1)S(1)} collective-permute-done((bf16[256,512]{1,0:T(8,128)(2,1)S(1)}, bf16[256,512]{1,0:T(8,128)(2,1)S(1)}, u32[]{:S(2)}, u32[]{:S(2)}) %collective-permute-start.5) | collective-permute-done | bytes 262176 | tf_op jit(solution)/shard_map/ppermute | solution.py:606
  37.9 0.2 collective-permute-done.6.refs_2_
  38.0 0.8 %rest.1 = bf16[256,2048]{1,0:T(8,128)(2,1)} custom-call(bf16[256,2048]{1,0:T(8,128)(2,1)} %own_block.1.refs_0_, bf16[256,512]{1,0:T(8,128)(2,1)S(1)} %collective-permute-done.5.refs_1_, bf16[256,512]{1,0:T(8,128)(2,1)S(1)} %collective-permute-done.6.refs_2_), custom_call_target="tpu_custom_call", output_to_operand_aliasing={{}: (0, {})} | custom-call | bytes 1048576 | tf_op jit(solution)/shard_map/rest/pallas_call | solution.py:588
Async XLA Ops:
  0.0 6.4 %copy-start = (f32[2,128]{1,0:T(2,128)S(1)}, f32[2,128]{1,0:T(2,128)}, u32[]{:S(2)}) copy-start(f32[2,128]{1,0:T(2,128)} %refs_5_.3) | copy-start | bytes 3076
  1.6 10.1 %collective-permute-start = (bf16[8,1,64,128]{3,2,1,0:T(8,128)(2,1)S(1)}, bf16[8,1,64,128]{3,2,1,0:T(8,128)(2,1)S(1)}, u32[]{:S(2)}, u32[]{:S(2)}) collective-permute-start(bf16[8,1,64,128]{3,2,1,0:T(8,128)(2,1)S(1)} %get-tuple-element.26), channel_id=1, source_target_pairs={{0,1},{1,2},{2,3},{4,5},{5,6},{6,7},{8,9},{9,10},{10,11},{12,13},{... | collective-permute-start | bytes 393224 | tf_op jit(solution)/shard_map/ppermute | solution.py:610
  6.4 5.3 %copy-start.1 = (bf16[256,16]{0,1:T(8,128)(2,1)S(1)}, bf16[256,16]{0,1:T(8,128)(2,1)}, u32[]{:S(2)}) copy-start(bf16[256,16]{0,1:T(8,128)(2,1)} %param.11) | copy-start | bytes 24580
  14.6 6.8 %collective-permute-start.3 = (bf16[128,128]{1,0:T(8,128)(2,1)S(1)}, bf16[128,128]{1,0:T(8,128)(2,1)S(1)}, u32[]{:S(2)}, u32[]{:S(2)}) collective-permute-start(bf16[128,128]{1,0:T(8,128)(2,1)S(1)} %get-tuple-element.28.refs_3_), channel_id=1, source_target_pairs={{0,1},{1,0},{2,3},{3,2},{4,5},{5,4},{6,7},{7,6},{8,9},{9,8},{10,11... | collective-permute-start | bytes 98312 | tf_op jit(solution)/shard_map/ppermute | solution.py:606
  16.2 5.3 %collective-permute-start.2 = (bf16[128,128]{1,0:T(8,128)(2,1)S(1)}, bf16[128,128]{1,0:T(8,128)(2,1)S(1)}, u32[]{:S(2)}, u32[]{:S(2)}) collective-permute-start(bf16[128,128]{1,0:T(8,128)(2,1)S(1)} %get-tuple-element.28.refs_3_), channel_id=1, source_target_pairs={{0,2},{1,3},{2,0},{3,1},{4,6},{5,7},{6,4},{7,5},{8,10},{9,11},{10,... | collective-permute-start | bytes 98312 | tf_op jit(solution)/shard_map/ppermute | solution.py:606
  16.3 5.2 %collective-permute-start.1 = (bf16[128,128]{1,0:T(8,128)(2,1)S(1)}, bf16[128,128]{1,0:T(8,128)(2,1)S(1)}, u32[]{:S(2)}, u32[]{:S(2)}) collective-permute-start(bf16[128,128]{1,0:T(8,128)(2,1)S(1)} %get-tuple-element.28.refs_3_), channel_id=1, source_target_pairs={{0,3},{1,2},{2,1},{3,0},{4,7},{5,6},{6,5},{7,4},{8,11},{9,10},{10,... | collective-permute-start | bytes 98312 | tf_op jit(solution)/shard_map/ppermute | solution.py:606
  24.4 8.0 %collective-permute-start.4 = (bf16[256,512]{1,0:T(8,128)(2,1)S(1)}, bf16[256,512]{1,0:T(8,128)(2,1)S(1)}, u32[]{:S(2)}, u32[]{:S(2)}) collective-permute-start(bf16[256,512]{1,0:T(8,128)(2,1)S(1)} %get-tuple-element.37), channel_id=1, source_target_pairs={{0,3},{1,2},{2,1},{3,0},{4,7},{5,6},{6,5},{7,4},{8,11},{9,10},{10,... | collective-permute-start | bytes 786440 | tf_op jit(solution)/shard_map/ppermute | solution.py:606
  28.1 9.8 %collective-permute-start.5 = (bf16[256,512]{1,0:T(8,128)(2,1)S(1)}, bf16[256,512]{1,0:T(8,128)(2,1)S(1)}, u32[]{:S(2)}, u32[]{:S(2)}) collective-permute-start(bf16[256,512]{1,0:T(8,128)(2,1)S(1)} %attend.2), channel_id=1, source_target_pairs={{0,2},{1,3},{2,0},{3,1},{4,6},{5,7},{6,4},{7,5},{8,10},{9,11},{10,... | collective-permute-start | bytes 786440 | tf_op jit(solution)/shard_map/ppermute | solution.py:606
  31.6 6.4 %collective-permute-start.6 = (bf16[256,512]{1,0:T(8,128)(2,1)S(1)}, bf16[256,512]{1,0:T(8,128)(2,1)S(1)}, u32[]{:S(2)}, u32[]{:S(2)}) collective-permute-start(bf16[256,512]{1,0:T(8,128)(2,1)S(1)} %attend.3), channel_id=1, source_target_pairs={{0,1},{1,0},{2,3},{3,2},{4,5},{5,4},{6,7},{7,6},{8,9},{9,8},{10,11... | collective-permute-start | bytes 786440 | tf_op jit(solution)/shard_map/ppermute | solution.py:606

commit v5 on v4

--- a/solution.py
+++ b/solution.py
@@ -90,28 +90,45 @@
     )(*[far(a) for a in (video, text, modulation)])
 
 
+def add_text(stream, flat, acc_ref, fresh):
+    step = 128
+    row = lax.broadcasted_iota(jnp.int32, (2 * step, 2 * step), 0)
+    col = lax.broadcasted_iota(jnp.int32, (2 * step, 2 * step), 1)
+    pick = jnp.where(col == 2 * (row % step) + row // step, 1.0, 0.0).astype(BF16)
+    pieces = ([], [])
+    for at in range(0, flat.shape[0], 2 * step):
+        both = dot(pick, flat[at : at + 2 * step, :]).astype(BF16)
+        pieces[0].append(both[:step])
+        pieces[1].append(both[step:])
+    for p in range(2):
+        term = dot(stream, jnp.concatenate(pieces[p], 0))
+        if fresh:
+            acc_ref[p] = term
+        else:
+            acc_ref[p] += term
+
+
 def text_kernel(
     chunks,
     text_ref,
     mod_ref,
-    gain_ref,
     w_hbm,
     video_hbm,
     conv_hbm,
     e_hbm,
-    key_ref,
-    value_ref,
+    acc_ref,
+    stream_ref,
+    last_ref,
     video_ref,
     conv_ref,
     e_ref,
     w_ref,
-    stream_ref,
-    acc_ref,
     sem,
     w_sem,
 ):
     depth, parts, width = w_hbm.shape
-    deep = depth // chunks
+    taken = w_ref.shape[0]
+    deep = taken // chunks
     copies = [
         pltpu.make_async_copy(w_hbm.at[pl.ds(c * deep, deep)], w_ref.at[pl.ds(c * deep, deep)], w_sem.at[c])
         for c in range(chunks)
@@ -120,6 +137,7 @@
         (video_hbm, video_ref),
         (conv_hbm, conv_ref),
         (e_hbm, e_ref),
+        (w_hbm.at[pl.ds(taken, depth - taken)], last_ref),
     )
     ahead = [pltpu.make_async_copy(src, dst, sem.at[i]) for i, (src, dst) in enumerate(pairs)]
     for c in copies:
@@ -130,78 +148,65 @@
         centred = text - jnp.mean(text, -1, keepdims=True)
         normed = centred * lax.rsqrt(jnp.mean(centred * centred, -1, keepdims=True) + EPS)
         stream_ref[r : r + few, :] = (normed * (1.0 + mod_ref[3:4, :]) + mod_ref[2:3, :]).astype(BF16)
-    step = 128
-    row = lax.broadcasted_iota(jnp.int32, (2 * step, 2 * step), 0)
-    col = lax.broadcasted_iota(jnp.int32, (2 * step, 2 * step), 1)
-    pick = jnp.where(col == 2 * (row % step) + row // step, 1.0, 0.0).astype(BF16)
-    flat = w_ref.reshape(depth * parts, width)
+    flat = w_ref.reshape(taken * parts, width)
     for c in range(chunks):
         copies[c].wait()
         if c == 0:
             for copy in ahead:
                 copy.start()
-        pieces = ([], [])
-        for s in range(deep // step):
-            at = 2 * (c * deep + s * step)
-            both = dot(pick, flat[at : at + 2 * step, :]).astype(BF16)
-            pieces[0].append(both[:step])
-            pieces[1].append(both[step:])
-        stream = stream_ref[:, c * deep : (c + 1) * deep]
-        for p in range(2):
-            term = dot(stream, jnp.concatenate(pieces[p], 0))
-            if c == 0:
-                acc_ref[p] = term
-            else:
-                acc_ref[p] += term
-    for h in range(width // HS):
-        at = slice(h * HS, (h + 1) * HS)
-        key_ref[h] = head_norm(acc_ref[0, :, at], gain_ref[1:2, :])
-        value_ref[h] = acc_ref[1, :, at].astype(BF16)
+        at = slice(c * deep, (c + 1) * deep)
+        add_text(stream_ref[:, at], flat.at[2 * c * deep : 2 * (c + 1) * deep], acc_ref, c == 0)
     for c in ahead:
         c.wait()
 
 
-def text_side(text, modulation, gain, weight, video, conv_weight, embed_weight):
+def text_side(text, modulation, weight, video, conv_weight, embed_weight):
     depth, parts, width = weight.shape
     count = text.shape[0]
-    heads = width // HS
-    chunks = 3
+    taken = depth * 2 // 3
+    chunks = 2
     return pl.pallas_call(
         lambda *refs: text_kernel(chunks, *refs),
         out_shape=(
-            jax.ShapeDtypeStruct((heads, count, HS), BF16),
-            jax.ShapeDtypeStruct((heads, count, HS), BF16),
+            jax.ShapeDtypeStruct((parts, count, width), F32),
+            jax.ShapeDtypeStruct(text.shape, BF16),
+            jax.ShapeDtypeStruct((depth - taken, parts, width), BF16),
             jax.ShapeDtypeStruct(video.shape, BF16),
             jax.ShapeDtypeStruct(conv_weight.shape, BF16),
             jax.ShapeDtypeStruct(embed_weight.shape, BF16),
         ),
-        in_specs=[vmem_spec()] * 3 + [hbm_spec()] * 4,
-        out_specs=(vmem_spec(),) * 5,
+        in_specs=[vmem_spec()] * 2 + [hbm_spec()] * 4,
+        out_specs=(vmem_spec(),) * 6,
         scratch_shapes=[
-            VMEM((depth, parts, width), BF16),
-            VMEM((count, depth), BF16),
-            VMEM((parts, count, width), F32),
-            pltpu.SemaphoreType.DMA((3,)),
+            VMEM((taken, parts, width), BF16),
+            pltpu.SemaphoreType.DMA((4,)),
             pltpu.SemaphoreType.DMA((chunks,)),
         ],
-        compiler_params=params(24),
+        compiler_params=params(20),
         cost_estimate=cost(4 * count * depth * parts * width, nbytes(weight, text, video, conv_weight)),
         name="text_side",
-    )(text, modulation, gain, *[far(a) for a in (weight, video, conv_weight, embed_weight)])
+    )(text, modulation, *[far(a) for a in (weight, video, conv_weight, embed_weight)])
 
 
 def fold_kernel(
     e_ref,
     mod_ref,
+    gain_ref,
     w0_ref,
+    part_ref,
+    stream_ref,
+    last_ref,
     w_hbm,
     rhs0_ref,
     rhs1_ref,
     shift_ref,
     gram_ref,
+    key_ref,
+    value_ref,
     lhs_ref,
     both_ref,
     acc_ref,
+    sum_ref,
     w1_ref,
     sem,
 ):
@@ -213,6 +218,12 @@
     ]
     for c in copies:
         c.start()
+    last, _, _ = last_ref.shape
+    add_text(stream_ref[:, depth - last :], last_ref.reshape(2 * last, width), sum_ref, True)
+    for h in range(width // HS):
+        at = slice(h * HS, (h + 1) * HS)
+        key_ref[h] = head_norm(part_ref[0, :, at] + sum_ref[0, :, at], gain_ref[1:2, :])
+        value_ref[h] = (part_ref[1, :, at] + sum_ref[1, :, at]).astype(BF16)
     few = 16
     for r in range(0, pi, few):
         e = e_ref[r : r + few, :].astype(F32)
@@ -251,10 +262,12 @@
     shift_ref[...] = total[2 * pi : 2 * pi + 1] + total[2 * pi + 1 : 2 * pi + 2]
 
 
-def fold(embed_weight, modulation, weight0, weight):
+def fold(embed_weight, modulation, gain, weight0, part, stream, last, weight):
     parts, taken, width = weight0.shape
     pi, depth = embed_weight.shape
     cols = parts * width
+    count = stream.shape[0]
+    heads = width // HS
     return pl.pallas_call(
         fold_kernel,
         out_shape=(
@@ -262,20 +275,23 @@
             jax.ShapeDtypeStruct((4 * pi, cols), BF16),
             jax.ShapeDtypeStruct((1, cols), F32),
             jax.ShapeDtypeStruct((4 * pi, 2 * pi), BF16),
+            jax.ShapeDtypeStruct((heads, count, HS), BF16),
+            jax.ShapeDtypeStruct((heads, count, HS), BF16),
         ),
-        in_specs=[vmem_spec()] * 3 + [hbm_spec()],
-        out_specs=(vmem_spec(),) * 4,
+        in_specs=[vmem_spec()] * 7 + [hbm_spec()],
+        out_specs=(vmem_spec(),) * 6,
         scratch_shapes=[
             VMEM((2 * pi + 16, depth), BF16),
             VMEM((2 * pi, depth), BF16),
             VMEM((2 * pi + 16, cols), F32),
+            VMEM(part.shape, F32),
             VMEM((parts, depth - taken, width), BF16),
             pltpu.SemaphoreType.DMA((parts,)),
         ],
-        compiler_params=params(12),
+        compiler_params=params(20),
         cost_estimate=cost(2 * 144 * depth * cols, nbytes(weight, embed_weight, modulation)),
         name="fold",
-    )(embed_weight, modulation, weight0, far(weight))
+    )(embed_weight, modulation, gain, weight0, part, stream, last, far(weight))
 
 
 def conv_kernel(
@@ -311,9 +327,11 @@
     for r in range(rows + 1):
         for f in range(frames):
             base = (r * frames + f) * block
-            pixels = halo_ref[f, 0] if r == 0 else video_ref[f, r - 1]
+            pixels = (halo_ref[f, 0] if r == 0 else video_ref[f, r - 1]).astype(F32)
+            if r == 0:
+                pixels = jnp.where(lax.axis_index("ctx") == 0, 0.0, pixels)
             wide_ref[base : base + 8, :] = jnp.zeros((8, chans), F32)
-            wide_ref[base + 8 : base + block, :] = pixels.astype(F32)
+            wide_ref[base + 8 : base + block, :] = pixels
             at = [wide_ref[pl.ds(base + 7 + o, quarter, stride=4), :] for o in range(5)]
             even = jnp.concatenate([at[1], at[3]], 0).astype(BF16)
             odd = jnp.concatenate([at[2], at[4]], 0).astype(BF16)
@@ -388,7 +406,8 @@
 
 def block_queries(n, own, x, xx, scales, rhs_refs, shift_ref, gain_ref, query_ref):
     heads = query_ref.shape[0]
-    span = x.shape[0] // n
+    rows = x.shape[1]
+    span = rows // n
     grain = span // own
     gain = gain_ref[0:1, :] * (math.log2(math.e) / math.sqrt(HS))
     for i in range(2):
@@ -396,23 +415,29 @@
         projected = dot(xx, rhs_refs[i][:, at]) * scales[i] + shift_ref[:, at]
         for h in range(heads):
             v = head_norm(projected[:, h * HS : (h + 1) * HS], gain)
-            for s in range(n):
-                for f in range(own):
-                    to = f * (n * 2 * grain) + (s * 2 + i) * grain
-                    come = s * span + f * grain
-                    query_ref[h, to : to + grain, :] = v[come : come + grain]
-
-
-def attention(query_ref, key_ref, value_ref, out_ref):
+            for j in range(x.shape[0] // rows):
+                for s in range(n):
+                    for f in range(own):
+                        to = 2 * j * rows + f * (n * 2 * grain) + (s * 2 + i) * grain
+                        come = j * rows + s * span + f * grain
+                        query_ref[h, to : to + grain, :] = v[come : come + grain]
+
+
+def attention(query_ref, key_ref, value_ref, out_refs):
     heads, total, _ = key_ref.shape
-    for h in range(heads):
-        weights = jnp.exp2(dot_nt(query_ref[h], key_ref[h]))
-        norm = weights[:, :HS]
-        for c in range(HS, total, HS):
-            norm = norm + weights[:, c : c + HS]
-        norm = jnp.sum(norm, -1, keepdims=True)
-        attended = dot(weights.astype(BF16), value_ref[h])
-        out_ref[:, h * HS : (h + 1) * HS] = (attended / norm).astype(BF16)
+    rows = query_ref.shape[1] // len(out_refs)
+    for j in range(0, len(out_refs), 2):
+        group = out_refs[j : j + 2]
+        for h in range(heads):
+            query = query_ref[h, j * rows : (j + len(group)) * rows, :]
+            weights = jnp.exp2(dot_nt(query, key_ref[h]))
+            norm = weights[:, :HS]
+            for c in range(HS, total, HS):
+                norm = norm + weights[:, c : c + HS]
+            norm = jnp.sum(norm, -1, keepdims=True)
+            attended = (dot(weights.astype(BF16), value_ref[h]) / norm).astype(BF16)
+            for g, ref in enumerate(group):
+                ref[:, h * HS : (h + 1) * HS] = attended[g * rows : (g + 1) * rows]
 
 
 def first_kernel(order, frames, *refs):
@@ -455,7 +480,7 @@
     block_queries(
         n, own, x[:rows], xx[:rows], [v[:rows] for v in scales], rhs_refs, shift_ref, gain_ref, query_ref
     )
-    attention(query_ref, key_ref, value_ref, out_ref)
+    attention(query_ref, key_ref, value_ref, (out_ref,))
 
 
 def first_block(order, frames, patches, rhs0, rhs1, shift, gram, gain, tkey, tvalue):
@@ -481,26 +506,27 @@
 
 
 def attend_kernel(
-    n, own, j, x_ref, rhs0_ref, rhs1_ref, shift_ref, gram_ref, gain_ref, key_ref, value_ref, out_ref, query_ref
+    n, own, first, x_ref, rhs0_ref, rhs1_ref, shift_ref, gram_ref, gain_ref, key_ref, value_ref, *refs
 ):
+    out_refs, query_ref = refs[:-1], refs[-1]
     rows = x_ref.shape[1]
-    x = x_ref[j * rows : (j + 1) * rows, :]
+    x = x_ref[first * rows : (first + len(out_refs)) * rows, :]
     xx = jnp.concatenate([x, x], 1)
     scales = token_scales(x, xx, gram_ref)
     block_queries(n, own, x, xx, scales, (rhs0_ref, rhs1_ref), shift_ref, gain_ref, query_ref)
-    attention(query_ref, key_ref, value_ref, out_ref)
-
-
-def attend(n, frames, j, x, rhs0, rhs1, shift, gram, gain, key, value):
+    attention(query_ref, key_ref, value_ref, out_refs)
+
+
+def attend(n, frames, first, count, x, rhs0, rhs1, shift, gram, gain, key, value):
     heads = key.shape[0]
     rows = x.shape[1]
     return pl.pallas_call(
-        lambda *refs: attend_kernel(n, frames // n, j, *refs),
-        out_shape=jax.ShapeDtypeStruct((2 * rows, heads * HS), BF16),
+        lambda *refs: attend_kernel(n, frames // n, first, *refs),
+        out_shape=(jax.ShapeDtypeStruct((2 * rows, heads * HS), BF16),) * count,
         in_specs=[vmem_spec()] * 8,
-        out_specs=vmem_spec(),
-        scratch_shapes=[VMEM((heads, 2 * rows, HS), BF16)],
-        compiler_params=params(12),
+        out_specs=(vmem_spec(),) * count,
+        scratch_shapes=[VMEM((heads, count * 2 * rows, HS), BF16)],
+        compiler_params=params(20),
         cost_estimate=cost(heads * rows * HS, 2 * nbytes(x)),
         name="attend",
     )(x, rhs0, rhs1, shift, gram, gain, key, value)
@@ -607,11 +633,10 @@
 
     weight = qkv_weight.transpose(1, 0, 2)
     edge_row, text_near, mod_near = edge(video, text, modulation)
-    halo = lax.ppermute(edge_row, "ctx", [(i, i + 1) for i in range(n - 1)])
-    tkey, tvalue, tile, taps, e_near = text_side(
+    halo = lax.ppermute(edge_row, "ctx", [(i, (i + 1) % n) for i in range(n)])
+    part, stream, last, tile, taps, e_near = text_side(
         text_near,
         mod_near,
-        qk_gain,
         text_weight,
         video,
         conv_weight.reshape(-1, conv_weight.shape[-1]),
@@ -620,13 +645,15 @@
     patches, weight_near = conv_side(tile, halo, taps, latent_weight, weight, weight.shape[1] * 2 // 3)
     order = tuple(range(n - 1, -1, -1))
     received = [swap(patches, k) if k else patches for k in order]
-    rhs0, rhs1, shift, gram = fold(e_near, mod_near, weight_near, weight)
+    rhs0, rhs1, shift, gram, tkey, tvalue = fold(
+        e_near, mod_near, qk_gain, weight_near, part, stream, last, weight
+    )
     block, x, key, value = first_block(
         order, frames, received, rhs0, rhs1, shift, gram, qk_gain, tkey, tvalue
     )
     far_block = swap(block, order[0])
     common = (x, rhs0, rhs1, shift, gram, qk_gain, key, value)
-    blocks = [swap(attend(n, frames, j, *common), order[j]) for j in range(1, n - 1)]
+    blocks = [swap(b, k) for b, k in zip(attend(n, frames, 1, n - 2, *common), order[1:])]
     out = own_block(n, frames, order[0], far_block, *common)
     return rest(order[1 : n - 1], out, blocks)
 

time: 39.2 us -> 37 us (0.944)
  starting transfers between devices: 12.1 us -> 10.2 us
  Pallas kernels: 23.4 us -> 22.7 us
  waiting for transfers between devices: 3.21 us -> 3.65 us
    ppermute x1, starting transfers between devices: 4.85 us -> 2.99 us  [shards(): halo = lax.ppermute(edge_row, 'ctx', [(i, (i + 1) % n) for i in range(n)])]
    pallas_call x1, Pallas kernels: 5.23 us -> 4.37 us  [text_side(): pl.pallas_call(lambda *refs: text_kernel(chunks, *refs), out_shape=(jax.S...]
    pallas_call x1, Pallas kernels: 3.28 us -> 3.92 us  [fold(): pl.pallas_call(fold_kernel, out_shape=(jax.ShapeDtypeStruct((4 * pi, cols...]
    pallas_call x2 -> x1, Pallas kernels: 4.09 us -> 3.65 us  [attend(): pl.pallas_call(lambda *refs: attend_kernel(n, frames // n, first, *refs),...]
  transfers between devices with their start and end apart: 7 -> 7, of which waited for: 3 -> 4; matrix products, arithmetic and copies ran while one was open for 0% -> 0% of each run, Pallas kernels for 39% -> 40%
where the time goes in v5:
time: 37 us; the launch traced here: 36.8 us
  Pallas kernels  22.7 us (61%)
  starting transfers between devices  10.2 us (28%)
  waiting for transfers between devices  3.65 us (10%)
    ppermute x6, starting transfers between devices, swap(): return lax.ppermute(x, 'ctx', [(i, i ^ k) for i in range(n)])  7.17 us
    pallas_call x1, Pallas kernels, text_side(): pl.pallas_call(lambda *refs: text_kernel(chunks, *refs), out_shape=(jax.S...  4.37 us
    pallas_call x1, Pallas kernels, fold(): pl.pallas_call(fold_kernel, out_shape=(jax.ShapeDtypeStruct((4 * pi, cols...  3.92 us
    pallas_call x1, Pallas kernels, attend(): pl.pallas_call(lambda *refs: attend_kernel(n, frames // n, first, *refs),...  3.65 us
    ppermute x6, waiting for transfers between devices, swap(): return lax.ppermute(x, 'ctx', [(i, i ^ k) for i in range(n)])  3.58 us
    ppermute x1, starting transfers between devices, shards(): halo = lax.ppermute(edge_row, 'ctx', [(i, (i + 1) % n) for i in range(n)])  2.99 us
    pallas_call x1, Pallas kernels, conv_side(): pl.pallas_call(lambda *refs: conv_kernel(chunks, *refs), out_shape=(jax.S...  2.91 us
    pallas_call x1, Pallas kernels, first_block(): pl.pallas_call(lambda *refs: first_kernel(order, frames, *refs), out_shap...  2.86 us
  transfers between devices with their start and end apart: 7, of which 4 were waited for; matrix products, arithmetic and copies ran while one was open for 0% of the time, Pallas kernels for 40%

profile of v5, /device:TPU:0, one launch (start us, length us, event | category | flops | bytes accessed | tf_op | source)
XLA Modules:
  0.0 36.8 jit_solution(4193420031647988773)
XLA Ops:
  0.0 1.5 %edge.1 = (bf16[8,1,64,128]{3,2,1,0:T(8,128)(2,1)S(1)}, bf16[256,3072]{1,0:T(8,128)(2,1)S(1)}, f32[4,3072]{1,0:T(4,128)S(1)}) custom-call(bf16[8,8,64,128]{3,2,1,0:T(8,128)(2,1)} %refs_3_.1, bf16[256,3072]{1,0:T(8,128)(2,1)} %text_hbm.1, f32[4,3072]{1,0:T(4,128)} %mod_hbm.1), custom_call_target="tpu_custom_call" | custom-call | bytes 3244032 | tf_op jit(solution)/shard_map/edge/pallas_call | solution.py:77
  1.5 3.0 %collective-permute-start = (bf16[8,1,64,128]{3,2,1,0:T(8,128)(2,1)S(1)}, bf16[8,1,64,128]{3,2,1,0:T(8,128)(2,1)S(1)}, u32[]{:S(2)}, u32[]{:S(2)}) collective-permute-start(bf16[8,1,64,128]{3,2,1,0:T(8,128)(2,1)S(1)} %get-tuple-element.31), channel_id=1, source_target_pairs={{0,1},{1,2},{2,3},{3,0},{4,5},{5,6},{6,7},{7,4},{8,9},{9,10},{10,1... | collective-permute-start | bytes 393224 | tf_op jit(solution)/shard_map/ppermute | solution.py:636
  4.5 0.0 copy-start.1
  4.5 4.4 %text_side.1 = (f32[2,256,512]{2,1,0:T(8,128)S(1)}, bf16[256,3072]{1,0:T(8,128)(2,1)S(1)}, bf16[1024,2,512]{2,1,0:T(2,128)(2,1)S(1)}, bf16[8,8,64,128]{3,2,1,0:T...) custom-call(bf16[256,3072]{1,0:T(8,128)(2,1)S(1)} %get-tuple-element.28.refs_0_, ...), custom_call_target="tpu_custom_call" | custom-call | flops 3221225472 | bytes 10682368 | tf_op jit(solution)/shard_map/text_side/pallas_call | solution.py:168
  8.9 0.1 collective-permute-done.refs_1_
  9.0 0.0 copy-done.1
  9.0 0.0 copy-start
  9.0 2.9 %conv_side.1 = (bf16[128,128]{1,0:T(8,128)(2,1)S(1)}, bf16[3,2048,512]{2,1,0:T(8,128)(2,1)S(1)}) custom-call(bf16[8,8,64,128]{3,2,1,0:T(8,128)(2,1)S(1)} %get-tuple-element.30.refs_0_, bf16[8,1,64,128]{3,2,1,0:T(8,128)(2,1)S(1)} %collective-permute-done.refs_1_, bf16[3456,256]{1,0:T(8,128)(2,1)S(1)} %get-tuple-element.32.refs_2_, ...), custom_call_target="tpu_custom_call" | custom-call | flops 1811939328 | bytes 2949120 | tf_op jit(solution)/shard_map/conv_side/pallas_call | solution.py:377
  11.9 1.5 %collective-permute-start.3 = (bf16[128,128]{1,0:T(8,128)(2,1)S(1)}, bf16[128,128]{1,0:T(8,128)(2,1)S(1)}, u32[]{:S(2)}, u32[]{:S(2)}) collective-permute-start(bf16[128,128]{1,0:T(8,128)(2,1)S(1)} %get-tuple-element.33.refs_3_), channel_id=1, source_target_pairs={{0,1},{1,0},{2,3},{3,2},{4,5},{5,4},{6,7},{7,6},{8,9},{9,8},{10,11... | collective-permute-start | bytes 98312 | tf_op jit(solution)/shard_map/ppermute | solution.py:632
  13.4 0.9 %collective-permute-start.2 = (bf16[128,128]{1,0:T(8,128)(2,1)S(1)}, bf16[128,128]{1,0:T(8,128)(2,1)S(1)}, u32[]{:S(2)}, u32[]{:S(2)}) collective-permute-start(bf16[128,128]{1,0:T(8,128)(2,1)S(1)} %get-tuple-element.33.refs_3_), channel_id=1, source_target_pairs={{0,2},{1,3},{2,0},{3,1},{4,6},{5,7},{6,4},{7,5},{8,10},{9,11},{10,... | collective-permute-start | bytes 98312 | tf_op jit(solution)/shard_map/ppermute | solution.py:632
  14.3 1.2 %collective-permute-start.1 = (bf16[128,128]{1,0:T(8,128)(2,1)S(1)}, bf16[128,128]{1,0:T(8,128)(2,1)S(1)}, u32[]{:S(2)}, u32[]{:S(2)}) collective-permute-start(bf16[128,128]{1,0:T(8,128)(2,1)S(1)} %get-tuple-element.33.refs_3_), channel_id=1, source_target_pairs={{0,3},{1,2},{2,1},{3,0},{4,7},{5,6},{6,5},{7,4},{8,11},{9,10},{10,... | collective-permute-start | bytes 98312 | tf_op jit(solution)/shard_map/ppermute | solution.py:632
  15.5 0.0 copy-done
  15.5 3.9 %fold.1 = (bf16[256,1536]{1,0:T(8,128)(2,1)S(1)}, bf16[256,1536]{1,0:T(8,128)(2,1)S(1)}, f32[1,1536]{1,0:T(1,128)S(1)}, bf16[256,128]{1,0:T(8,128)(2,1)S(1)}, bf...) custom-call(bf16[64,3072]{1,0:T(8,128)(2,1)S(1)} %get-tuple-element.34.e_ref, ...), custom_call_target="tpu_custom_call" | custom-call | flops 1358954496 | bytes 9879552 | tf_op jit(solution)/shard_map/fold/pallas_call | solution.py:271
  19.4 0.0 collective-permute-done.3.refs_2_
  19.4 0.0 collective-permute-done.2.refs_1_
  19.4 0.0 collective-permute-done.1.refs_0_
  19.4 2.9 %first_block.1 = (bf16[256,512]{1,0:T(8,128)(2,1)S(1)}, bf16[512,128]{1,0:T(8,128)(2,1)S(1)}, bf16[4,1280,128]{2,1,0:T(8,128)(2,1)S(1)}, bf16[4,1280,128]{2,1,0:T(8,128)(2,1)S(1)}) custom-call(bf16[128,128]{1,0:T(8,128)(2,1)S(1)} %collective-permute-done.1.refs_0_, bf16[128,128]{1,0:T(8,128)(2,1)S(1)} %collective-permute-done.2.refs_1_, ...), custom_call_target="tpu_custom_call" | custom-call | flops 805306368 | bytes 3145728 | tf_op jit(solution)/shard_map/first_block/pallas_call | solution.py:491
  22.3 1.8 %collective-permute-start.4 = (bf16[256,512]{1,0:T(8,128)(2,1)S(1)}, bf16[256,512]{1,0:T(8,128)(2,1)S(1)}, u32[]{:S(2)}, u32[]{:S(2)}) collective-permute-start(bf16[256,512]{1,0:T(8,128)(2,1)S(1)} %get-tuple-element.45), channel_id=1, source_target_pairs={{0,3},{1,2},{2,1},{3,0},{4,7},{5,6},{6,5},{7,4},{8,11},{9,10},{10,... | collective-permute-start | bytes 786440 | tf_op jit(solution)/shard_map/ppermute | solution.py:632
  24.1 3.6 %attend.1 = (bf16[256,512]{1,0:T(8,128)(2,1)S(1)}, bf16[256,512]{1,0:T(8,128)(2,1)S(1)}) custom-call(bf16[512,128]{1,0:T(8,128)(2,1)S(1)} %get-tuple-element.46.refs_1_.refs_0_, bf16[256,1536]{1,0:T(8,128)(2,1)S(1)} %get-tuple-element.39.refs_4_.refs_2_.refs_1_, bf16[256,1536]{1,0:T(8,128)(2,1)S(1)} %get-tuple-element.40.refs_5_.refs_3_.refs_2_, ...), custom_call_target="tpu_custom_call" | custom-call | flops 65536 | bytes 262144 | tf_op jit(solution)/shard_map/attend/pallas_call | solution.py:523
  27.8 1.2 %collective-permute-start.5 = (bf16[256,512]{1,0:T(8,128)(2,1)S(1)}, bf16[256,512]{1,0:T(8,128)(2,1)S(1)}, u32[]{:S(2)}, u32[]{:S(2)}) collective-permute-start(bf16[256,512]{1,0:T(8,128)(2,1)S(1)} %get-tuple-element.49), channel_id=1, source_target_pairs={{0,2},{1,3},{2,0},{3,1},{4,6},{5,7},{6,4},{7,5},{8,10},{9,11},{10,... | collective-permute-start | bytes 786440 | tf_op jit(solution)/shard_map/ppermute | solution.py:632
  29.0 0.6 %collective-permute-start.6 = (bf16[256,512]{1,0:T(8,128)(2,1)S(1)}, bf16[256,512]{1,0:T(8,128)(2,1)S(1)}, u32[]{:S(2)}, u32[]{:S(2)}) collective-permute-start(bf16[256,512]{1,0:T(8,128)(2,1)S(1)} %get-tuple-element.50), channel_id=1, source_target_pairs={{0,1},{1,0},{2,3},{3,2},{4,5},{5,4},{6,7},{7,6},{8,9},{9,8},{10,11... | collective-permute-start | bytes 786440 | tf_op jit(solution)/shard_map/ppermute | solution.py:632
  29.6 1.1 %collective-permute-done.4.refs_0_ = bf16[256,512]{1,0:T(8,128)(2,1)S(1)} collective-permute-done((bf16[256,512]{1,0:T(8,128)(2,1)S(1)}, bf16[256,512]{1,0:T(8,128)(2,1)S(1)}, u32[]{:S(2)}, u32[]{:S(2)}) %collective-permute-start.4) | collective-permute-done | bytes 262176 | tf_op jit(solution)/shard_map/ppermute | solution.py:632
  30.7 2.7 %own_block.1.refs_0_ = bf16[256,2048]{1,0:T(8,128)(2,1)} custom-call(bf16[256,512]{1,0:T(8,128)(2,1)S(1)} %collective-permute-done.4.refs_0_, bf16[512,128]{1,0:T(8,128)(2,1)S(1)} %get-tuple-element.46.refs_1_.refs_0_, bf16[256,1536]{1,0:T(8,128)(2,1)S(1)} %get-tuple-element.39.refs_4_.refs_2_.refs_1_, ...), custom_call_target="tpu_custom_call" | custom-call | flops 65536 | bytes 262144 | tf_op jit(solution)/shard_map/own_block/pallas_call | solution.py:586
  33.4 2.4 %collective-permute-done.5.refs_1_ = bf16[256,512]{1,0:T(8,128)(2,1)S(1)} collective-permute-done((bf16[256,512]{1,0:T(8,128)(2,1)S(1)}, bf16[256,512]{1,0:T(8,128)(2,1)S(1)}, u32[]{:S(2)}, u32[]{:S(2)}) %collective-permute-start.5) | collective-permute-done | bytes 262176 | tf_op jit(solution)/shard_map/ppermute | solution.py:632
  35.8 0.1 collective-permute-done.6.refs_2_
  35.8 0.8 %rest.1 = bf16[256,2048]{1,0:T(8,128)(2,1)} custom-call(bf16[256,2048]{1,0:T(8,128)(2,1)} %own_block.1.refs_0_, bf16[256,512]{1,0:T(8,128)(2,1)S(1)} %collective-permute-done.5.refs_1_, bf16[256,512]{1,0:T(8,128)(2,1)S(1)} %collective-permute-done.6.refs_2_), custom_call_target="tpu_custom_call", output_to_operand_aliasing={{}: (0, {})} | custom-call | bytes 1048576 | tf_op jit(solution)/shard_map/rest/pallas_call | solution.py:614
Async XLA Ops:
  1.5 7.4 %collective-permute-start = (bf16[8,1,64,128]{3,2,1,0:T(8,128)(2,1)S(1)}, bf16[8,1,64,128]{3,2,1,0:T(8,128)(2,1)S(1)}, u32[]{:S(2)}, u32[]{:S(2)}) collective-permute-start(bf16[8,1,64,128]{3,2,1,0:T(8,128)(2,1)S(1)} %get-tuple-element.31), channel_id=1, source_target_pairs={{0,1},{1,2},{2,3},{3,0},{4,5},{5,6},{6,7},{7,4},{8,9},{9,10},{10,1... | collective-permute-start | bytes 393224 | tf_op jit(solution)/shard_map/ppermute | solution.py:636
  4.5 4.5 %copy-start.1 = (bf16[256,16]{0,1:T(8,128)(2,1)S(1)}, bf16[256,16]{0,1:T(8,128)(2,1)}, u32[]{:S(2)}) copy-start(bf16[256,16]{0,1:T(8,128)(2,1)} %param.11) | copy-start | bytes 24580
  9.0 6.5 %copy-start = (f32[2,128]{1,0:T(2,128)S(1)}, f32[2,128]{1,0:T(2,128)}, u32[]{:S(2)}) copy-start(f32[2,128]{1,0:T(2,128)} %refs_5_.3) | copy-start | bytes 3076
  11.9 7.5 %collective-permute-start.3 = (bf16[128,128]{1,0:T(8,128)(2,1)S(1)}, bf16[128,128]{1,0:T(8,128)(2,1)S(1)}, u32[]{:S(2)}, u32[]{:S(2)}) collective-permute-start(bf16[128,128]{1,0:T(8,128)(2,1)S(1)} %get-tuple-element.33.refs_3_), channel_id=1, source_target_pairs={{0,1},{1,0},{2,3},{3,2},{4,5},{5,4},{6,7},{7,6},{8,9},{9,8},{10,11... | collective-permute-start | bytes 98312 | tf_op jit(solution)/shard_map/ppermute | solution.py:632
  13.4 6.0 %collective-permute-start.2 = (bf16[128,128]{1,0:T(8,128)(2,1)S(1)}, bf16[128,128]{1,0:T(8,128)(2,1)S(1)}, u32[]{:S(2)}, u32[]{:S(2)}) collective-permute-start(bf16[128,128]{1,0:T(8,128)(2,1)S(1)} %get-tuple-element.33.refs_3_), channel_id=1, source_target_pairs={{0,2},{1,3},{2,0},{3,1},{4,6},{5,7},{6,4},{7,5},{8,10},{9,11},{10,... | collective-permute-start | bytes 98312 | tf_op jit(solution)/shard_map/ppermute | solution.py:632
  14.3 5.1 %collective-permute-start.1 = (bf16[128,128]{1,0:T(8,128)(2,1)S(1)}, bf16[128,128]{1,0:T(8,128)(2,1)S(1)}, u32[]{:S(2)}, u32[]{:S(2)}) collective-permute-start(bf16[128,128]{1,0:T(8,128)(2,1)S(1)} %get-tuple-element.33.refs_3_), channel_id=1, source_target_pairs={{0,3},{1,2},{2,1},{3,0},{4,7},{5,6},{6,5},{7,4},{8,11},{9,10},{10,... | collective-permute-start | bytes 98312 | tf_op jit(solution)/shard_map/ppermute | solution.py:632
  22.3 8.4 %collective-permute-start.4 = (bf16[256,512]{1,0:T(8,128)(2,1)S(1)}, bf16[256,512]{1,0:T(8,128)(2,1)S(1)}, u32[]{:S(2)}, u32[]{:S(2)}) collective-permute-start(bf16[256,512]{1,0:T(8,128)(2,1)S(1)} %get-tuple-element.45), channel_id=1, source_target_pairs={{0,3},{1,2},{2,1},{3,0},{4,7},{5,6},{6,5},{7,4},{8,11},{9,10},{10,... | collective-permute-start | bytes 786440 | tf_op jit(solution)/shard_map/ppermute | solution.py:632
  27.8 8.0 %collective-permute-start.5 = (bf16[256,512]{1,0:T(8,128)(2,1)S(1)}, bf16[256,512]{1,0:T(8,128)(2,1)S(1)}, u32[]{:S(2)}, u32[]{:S(2)}) collective-permute-start(bf16[256,512]{1,0:T(8,128)(2,1)S(1)} %get-tuple-element.49), channel_id=1, source_target_pairs={{0,2},{1,3},{2,0},{3,1},{4,6},{5,7},{6,4},{7,5},{8,10},{9,11},{10,... | collective-permute-start | bytes 786440 | tf_op jit(solution)/shard_map/ppermute | solution.py:632
  29.0 6.8 %collective-permute-start.6 = (bf16[256,512]{1,0:T(8,128)(2,1)S(1)}, bf16[256,512]{1,0:T(8,128)(2,1)S(1)}, u32[]{:S(2)}, u32[]{:S(2)}) collective-permute-start(bf16[256,512]{1,0:T(8,128)(2,1)S(1)} %get-tuple-element.50), channel_id=1, source_target_pairs={{0,1},{1,0},{2,3},{3,2},{4,5},{5,4},{6,7},{7,6},{8,9},{9,8},{10,11... | collective-permute-start | bytes 786440 | tf_op jit(solution)/shard_map/ppermute | solution.py:632

commit v6 on v5

--- a/solution.py
+++ b/solution.py
@@ -58,12 +58,12 @@
     return (v * lax.rsqrt(jnp.mean(v * v, -1, keepdims=True) + EPS) * gain).astype(BF16)
 
 
-def edge_kernel(video_hbm, text_hbm, mod_hbm, halo_ref, text_ref, mod_ref, sem):
+def edge_kernel(video_hbm, e_hbm, mod_hbm, halo_ref, e_ref, mod_ref, sem):
     rows = video_hbm.shape[1]
     pairs = (
         (video_hbm.at[:, pl.ds(rows - 1, 1)], halo_ref),
+        (e_hbm, e_ref),
         (mod_hbm, mod_ref),
-        (text_hbm, text_ref),
     )
     copies = [pltpu.make_async_copy(src, dst, sem.at[i]) for i, (src, dst) in enumerate(pairs)]
     for c in copies:
@@ -72,22 +72,22 @@
         c.wait()
 
 
-def edge(video, text, modulation):
+def edge(video, embed_weight, modulation):
     frames, _, cols, chans = video.shape
     return pl.pallas_call(
         edge_kernel,
         out_shape=(
             jax.ShapeDtypeStruct((frames, 1, cols, chans), BF16),
-            jax.ShapeDtypeStruct(text.shape, BF16),
+            jax.ShapeDtypeStruct(embed_weight.shape, BF16),
             jax.ShapeDtypeStruct(modulation.shape, F32),
         ),
         in_specs=[hbm_spec()] * 3,
         out_specs=(vmem_spec(),) * 3,
         scratch_shapes=[pltpu.SemaphoreType.DMA((3,))],
         compiler_params=params(4),
-        cost_estimate=cost(0, 2 * nbytes(text, modulation)),
+        cost_estimate=cost(0, 2 * nbytes(embed_weight, modulation)),
         name="edge",
-    )(*[far(a) for a in (video, text, modulation)])
+    )(*[far(a) for a in (video, embed_weight, modulation)])
 
 
 def add_text(stream, flat, acc_ref, fresh):
@@ -108,20 +108,44 @@
             acc_ref[p] += term
 
 
+def embed_side(e_ref, mod_ref, lhs_ref, gram_ref, centred_ref):
+    pi, depth = e_ref.shape
+    few = 16
+    for r in range(0, pi, few):
+        e = e_ref[r : r + few, :].astype(F32)
+        centred = e - jnp.mean(e, -1, keepdims=True)
+        lhs_ref[r : r + few, :] = (centred * (1.0 + mod_ref[1:2, :])).astype(BF16)
+        centred = centred.astype(BF16)
+        centred_ref[r : r + few, :] = centred
+        centred_ref[pi + r : pi + r + few, :] = centred
+    shift_hi, shift_lo = split(mod_ref[0:1, :])
+    lhs_ref[pi:, :] = jnp.concatenate(
+        [shift_hi.astype(F32), shift_lo.astype(F32), jnp.zeros((few - 2, depth), F32)], 0
+    ).astype(BF16)
+    gram = dot_nt(centred_ref[...], centred_ref[...])
+    row = lax.broadcasted_iota(jnp.int32, gram.shape, 0) // pi
+    col = lax.broadcasted_iota(jnp.int32, gram.shape, 1) // pi
+    ghi, glo = split(jnp.where(row == col, gram * (1.0 / depth), 0.0))
+    gram_ref[...] = jnp.concatenate([ghi, glo], 0)
+
+
 def text_kernel(
     chunks,
-    text_ref,
+    e_ref,
     mod_ref,
+    text_hbm,
     w_hbm,
     video_hbm,
     conv_hbm,
-    e_hbm,
+    lhs_ref,
+    gram_ref,
     acc_ref,
     stream_ref,
     last_ref,
     video_ref,
     conv_ref,
-    e_ref,
+    text_ref,
+    centred_ref,
     w_ref,
     sem,
     w_sem,
@@ -133,15 +157,18 @@
         pltpu.make_async_copy(w_hbm.at[pl.ds(c * deep, deep)], w_ref.at[pl.ds(c * deep, deep)], w_sem.at[c])
         for c in range(chunks)
     ]
+    first = pltpu.make_async_copy(text_hbm, text_ref, sem.at[3])
     pairs = (
         (video_hbm, video_ref),
         (conv_hbm, conv_ref),
-        (e_hbm, e_ref),
         (w_hbm.at[pl.ds(taken, depth - taken)], last_ref),
     )
     ahead = [pltpu.make_async_copy(src, dst, sem.at[i]) for i, (src, dst) in enumerate(pairs)]
+    first.start()
     for c in copies:
         c.start()
+    embed_side(e_ref, mod_ref, lhs_ref, gram_ref, centred_ref)
+    first.wait()
     few = 16
     for r in range(0, text_ref.shape[0], few):
         text = text_ref[r : r + few, :].astype(F32)
@@ -160,24 +187,28 @@
         c.wait()
 
 
-def text_side(text, modulation, weight, video, conv_weight, embed_weight):
+def text_side(embed_weight, modulation, text, weight, video, conv_weight):
     depth, parts, width = weight.shape
     count = text.shape[0]
+    pi = embed_weight.shape[0]
     taken = depth * 2 // 3
     chunks = 2
     return pl.pallas_call(
         lambda *refs: text_kernel(chunks, *refs),
         out_shape=(
+            jax.ShapeDtypeStruct((pi + 16, depth), BF16),
+            jax.ShapeDtypeStruct((4 * pi, 2 * pi), BF16),
             jax.ShapeDtypeStruct((parts, count, width), F32),
             jax.ShapeDtypeStruct(text.shape, BF16),
             jax.ShapeDtypeStruct((depth - taken, parts, width), BF16),
             jax.ShapeDtypeStruct(video.shape, BF16),
             jax.ShapeDtypeStruct(conv_weight.shape, BF16),
-            jax.ShapeDtypeStruct(embed_weight.shape, BF16),
         ),
         in_specs=[vmem_spec()] * 2 + [hbm_spec()] * 4,
-        out_specs=(vmem_spec(),) * 6,
+        out_specs=(vmem_spec(),) * 7,
         scratch_shapes=[
+            VMEM(text.shape, BF16),
+            VMEM((2 * pi, depth), BF16),
             VMEM((taken, parts, width), BF16),
             pltpu.SemaphoreType.DMA((4,)),
             pltpu.SemaphoreType.DMA((chunks,)),
@@ -185,12 +216,11 @@
         compiler_params=params(20),
         cost_estimate=cost(4 * count * depth * parts * width, nbytes(weight, text, video, conv_weight)),
         name="text_side",
-    )(text, modulation, *[far(a) for a in (weight, video, conv_weight, embed_weight)])
+    )(embed_weight, modulation, *[far(a) for a in (text, weight, video, conv_weight)])
 
 
 def fold_kernel(
-    e_ref,
-    mod_ref,
+    lhs_ref,
     gain_ref,
     w0_ref,
     part_ref,
@@ -200,18 +230,16 @@
     rhs0_ref,
     rhs1_ref,
     shift_ref,
-    gram_ref,
     key_ref,
     value_ref,
-    lhs_ref,
-    both_ref,
     acc_ref,
     sum_ref,
     w1_ref,
     sem,
 ):
     parts, deep0, width = w0_ref.shape
-    pi, depth = e_ref.shape
+    depth = lhs_ref.shape[1]
+    pi = lhs_ref.shape[0] - 16
     copies = [
         pltpu.make_async_copy(w_hbm.at[p, pl.ds(deep0, depth - deep0)], w1_ref.at[p], sem.at[p])
         for p in range(parts)
@@ -224,29 +252,6 @@
         at = slice(h * HS, (h + 1) * HS)
         key_ref[h] = head_norm(part_ref[0, :, at] + sum_ref[0, :, at], gain_ref[1:2, :])
         value_ref[h] = (part_ref[1, :, at] + sum_ref[1, :, at]).astype(BF16)
-    few = 16
-    for r in range(0, pi, few):
-        e = e_ref[r : r + few, :].astype(F32)
-        centred = e - jnp.mean(e, -1, keepdims=True)
-        hi, lo = split(centred * (1.0 + mod_ref[1:2, :]))
-        lhs_ref[r : r + few, :] = hi
-        lhs_ref[pi + r : pi + r + few, :] = lo
-        hi, lo = split(centred)
-        both_ref[r : r + few, :] = hi
-        both_ref[pi + r : pi + r + few, :] = lo
-    shift_hi, shift_lo = split(mod_ref[0:1, :])
-    lhs_ref[2 * pi :, :] = jnp.concatenate(
-        [shift_hi.astype(F32), shift_lo.astype(F32), jnp.zeros((14, depth), F32)], 0
-    ).astype(BF16)
-    gram = dot_nt(both_ref[...], both_ref[...])
-    lane = lax.broadcasted_iota(jnp.int32, (pi, 2 * pi), 1)
-    gram = gram[:pi] + jnp.where(lane < pi, gram[pi:], 0.0)
-    gram = gram + pltpu.roll(gram, pi, 1)
-    gram = jnp.concatenate([gram, gram], 0)
-    row = lax.broadcasted_iota(jnp.int32, gram.shape, 0) // pi
-    col = lax.broadcasted_iota(jnp.int32, gram.shape, 1) // pi
-    ghi, glo = split(jnp.where(row == col, gram * (1.0 / depth), 0.0))
-    gram_ref[...] = jnp.concatenate([ghi, glo], 0)
     for p in range(parts):
         at = slice(p * width, (p + 1) * width)
         acc_ref[:, at] = dot(lhs_ref[:, :deep0], w0_ref[p])
@@ -255,43 +260,40 @@
         copies[p].wait()
         acc_ref[:, at] += dot(lhs_ref[:, deep0:], w1_ref[p])
     total = acc_ref[...]
-    hi, lo = split(total[:pi] + total[pi : 2 * pi])
+    hi, lo = split(total[:pi])
     none = jnp.zeros_like(hi)
     rhs0_ref[...] = jnp.concatenate([hi, none, lo, none], 0)
     rhs1_ref[...] = jnp.concatenate([none, hi, none, lo], 0)
-    shift_ref[...] = total[2 * pi : 2 * pi + 1] + total[2 * pi + 1 : 2 * pi + 2]
-
-
-def fold(embed_weight, modulation, gain, weight0, part, stream, last, weight):
+    shift_ref[...] = total[pi : pi + 1] + total[pi + 1 : pi + 2]
+
+
+def fold(lhs, gain, weight0, part, stream, last, weight):
     parts, taken, width = weight0.shape
-    pi, depth = embed_weight.shape
+    rows, depth = lhs.shape
     cols = parts * width
     count = stream.shape[0]
     heads = width // HS
     return pl.pallas_call(
         fold_kernel,
         out_shape=(
-            jax.ShapeDtypeStruct((4 * pi, cols), BF16),
-            jax.ShapeDtypeStruct((4 * pi, cols), BF16),
+            jax.ShapeDtypeStruct((4 * (rows - 16), cols), BF16),
+            jax.ShapeDtypeStruct((4 * (rows - 16), cols), BF16),
             jax.ShapeDtypeStruct((1, cols), F32),
-            jax.ShapeDtypeStruct((4 * pi, 2 * pi), BF16),
             jax.ShapeDtypeStruct((heads, count, HS), BF16),
             jax.ShapeDtypeStruct((heads, count, HS), BF16),
         ),
-        in_specs=[vmem_spec()] * 7 + [hbm_spec()],
-        out_specs=(vmem_spec(),) * 6,
+        in_specs=[vmem_spec()] * 6 + [hbm_spec()],
+        out_specs=(vmem_spec(),) * 5,
         scratch_shapes=[
-            VMEM((2 * pi + 16, depth), BF16),
-            VMEM((2 * pi, depth), BF16),
-            VMEM((2 * pi + 16, cols), F32),
+            VMEM((rows, cols), F32),
             VMEM(part.shape, F32),
             VMEM((parts, depth - taken, width), BF16),
             pltpu.SemaphoreType.DMA((parts,)),
         ],
         compiler_params=params(20),
-        cost_estimate=cost(2 * 144 * depth * cols, nbytes(weight, embed_weight, modulation)),
+        cost_estimate=cost(2 * 144 * depth * cols, nbytes(weight)),
         name="fold",
-    )(embed_weight, modulation, gain, weight0, part, stream, last, far(weight))
+    )(lhs, gain, weight0, part, stream, last, far(weight))
 
 
 def conv_kernel(
@@ -632,22 +634,20 @@
         return lax.ppermute(x, "ctx", [(i, i ^ k) for i in range(n)])
 
     weight = qkv_weight.transpose(1, 0, 2)
-    edge_row, text_near, mod_near = edge(video, text, modulation)
+    edge_row, e_near, mod_near = edge(video, embed_weight, modulation)
     halo = lax.ppermute(edge_row, "ctx", [(i, (i + 1) % n) for i in range(n)])
-    part, stream, last, tile, taps, e_near = text_side(
-        text_near,
+    lhs, gram, part, stream, last, tile, taps = text_side(
+        e_near,
         mod_near,
+        text,
         text_weight,
         video,
         conv_weight.reshape(-1, conv_weight.shape[-1]),
-        embed_weight,
     )
     patches, weight_near = conv_side(tile, halo, taps, latent_weight, weight, weight.shape[1] * 2 // 3)
     order = tuple(range(n - 1, -1, -1))
     received = [swap(patches, k) if k else patches for k in order]
-    rhs0, rhs1, shift, gram, tkey, tvalue = fold(
-        e_near, mod_near, qk_gain, weight_near, part, stream, last, weight
-    )
+    rhs0, rhs1, shift, tkey, tvalue = fold(lhs, qk_gain, weight_near, part, stream, last, weight)
     block, x, key, value = first_block(
         order, frames, received, rhs0, rhs1, shift, gram, qk_gain, tkey, tvalue
     )

time: 37 us -> 36.9 us (level)
    pallas_call x1, Pallas kernels: 4.37 us -> 5.3 us  [text_side(): pl.pallas_call(lambda *refs: text_kernel(chunks, *refs), out_shape=(jax.S...]
    pallas_call x1, Pallas kernels: 3.92 us -> 3.36 us  [fold(): pl.pallas_call(fold_kernel, out_shape=(jax.ShapeDtypeStruct((4 * (rows -...]
    pallas_call x1, Pallas kernels: 1.54 us -> 1.09 us  [edge(): pl.pallas_call(edge_kernel, out_shape=(jax.ShapeDtypeStruct((frames, 1, c...]
  transfers between devices with their start and end apart: 7 -> 7, of which waited for: 4 -> 3; matrix products, arithmetic and copies ran while one was open for 0% -> 0% of each run, Pallas kernels for 40% -> 41%
where the time goes in v6:
time: 36.9 us; the launch traced here: 36.7 us
  Pallas kernels  22.7 us (62%)
  starting transfers between devices  10.2 us (28%)
  waiting for transfers between devices  3.62 us (10%)
    ppermute x6, starting transfers between devices, swap(): return lax.ppermute(x, 'ctx', [(i, i ^ k) for i in range(n)])  7.17 us
    pallas_call x1, Pallas kernels, text_side(): pl.pallas_call(lambda *refs: text_kernel(chunks, *refs), out_shape=(jax.S...  5.3 us
    pallas_call x1, Pallas kernels, attend(): pl.pallas_call(lambda *refs: attend_kernel(n, frames // n, first, *refs),...  3.65 us
    ppermute x6, waiting for transfers between devices, swap(): return lax.ppermute(x, 'ctx', [(i, i ^ k) for i in range(n)])  3.61 us
    pallas_call x1, Pallas kernels, fold(): pl.pallas_call(fold_kernel, out_shape=(jax.ShapeDtypeStruct((4 * (rows -...  3.36 us
    ppermute x1, starting transfers between devices, shards(): halo = lax.ppermute(edge_row, 'ctx', [(i, (i + 1) % n) for i in range(n)])  2.99 us
    pallas_call x1, Pallas kernels, conv_side(): pl.pallas_call(lambda *refs: conv_kernel(chunks, *refs), out_shape=(jax.S...  2.91 us
    pallas_call x1, Pallas kernels, first_block(): pl.pallas_call(lambda *refs: first_kernel(order, frames, *refs), out_shap...  2.86 us
  transfers between devices with their start and end apart: 7, of which 3 were waited for; matrix products, arithmetic and copies ran while one was open for 0% of the time, Pallas kernels for 41%

profile of v6, /device:TPU:0, one launch (start us, length us, event | category | flops | bytes accessed | tf_op | source)
XLA Modules:
  0.0 36.7 jit_solution(13514701118149392084)
XLA Ops:
  0.0 1.1 %edge.1 = (bf16[8,1,64,128]{3,2,1,0:T(8,128)(2,1)S(1)}, bf16[64,3072]{1,0:T(8,128)(2,1)S(1)}, f32[4,3072]{1,0:T(4,128)S(1)}) custom-call(bf16[8,8,64,128]{3,2,1,0:T(8,128)(2,1)} %refs_4_.1, bf16[64,3072]{1,0:T(8,128)(2,1)} %e_hbm.1, f32[4,3072]{1,0:T(4,128)} %mod_hbm.1), custom_call_target="tpu_custom_call" | custom-call | bytes 884736 | tf_op jit(solution)/shard_map/edge/pallas_call | solution.py:77
  1.1 3.0 %collective-permute-start = (bf16[8,1,64,128]{3,2,1,0:T(8,128)(2,1)S(1)}, bf16[8,1,64,128]{3,2,1,0:T(8,128)(2,1)S(1)}, u32[]{:S(2)}, u32[]{:S(2)}) collective-permute-start(bf16[8,1,64,128]{3,2,1,0:T(8,128)(2,1)S(1)} %get-tuple-element.31), channel_id=1, source_target_pairs={{0,1},{1,2},{2,3},{3,0},{4,5},{5,6},{6,7},{7,4},{8,9},{9,10},{10,1... | collective-permute-start | bytes 393224 | tf_op jit(solution)/shard_map/ppermute | solution.py:638
  4.1 0.0 copy-start.1
  4.1 5.3 %text_side.1 = (bf16[80,3072]{1,0:T(8,128)(2,1)S(1)}, bf16[256,128]{1,0:T(8,128)(2,1)S(1)}, f32[2,256,512]{2,1,0:T(8,128)S(1)}, bf16[256,3072]{1,0:T(8,128)(2,1)...) custom-call(bf16[64,3072]{1,0:T(8,128)(2,1)S(1)} %get-tuple-element.28.r, ...), custom_call_target="tpu_custom_call" | custom-call | flops 3221225472 | bytes 10682368 | tf_op jit(solution)/shard_map/text_side/pallas_call | solution.py:196
  9.4 0.0 collective-permute-done.refs_1_
  9.4 0.0 copy-done.1
  9.4 0.0 copy-start
  9.4 2.9 %conv_side.1 = (bf16[128,128]{1,0:T(8,128)(2,1)S(1)}, bf16[3,2048,512]{2,1,0:T(8,128)(2,1)S(1)}) custom-call(bf16[8,8,64,128]{3,2,1,0:T(8,128)(2,1)S(1)} %get-tuple-element.30.refs_0_, bf16[8,1,64,128]{3,2,1,0:T(8,128)(2,1)S(1)} %collective-permute-done.refs_1_, bf16[3456,256]{1,0:T(8,128)(2,1)S(1)} %get-tuple-element.32.refs_2_, ...), custom_call_target="tpu_custom_call" | custom-call | flops 1811939328 | bytes 2949120 | tf_op jit(solution)/shard_map/conv_side/pallas_call | solution.py:379
  12.4 1.6 %collective-permute-start.3 = (bf16[128,128]{1,0:T(8,128)(2,1)S(1)}, bf16[128,128]{1,0:T(8,128)(2,1)S(1)}, u32[]{:S(2)}, u32[]{:S(2)}) collective-permute-start(bf16[128,128]{1,0:T(8,128)(2,1)S(1)} %get-tuple-element.33.refs_3_), channel_id=1, source_target_pairs={{0,1},{1,0},{2,3},{3,2},{4,5},{5,4},{6,7},{7,6},{8,9},{9,8},{10,11... | collective-permute-start | bytes 98312 | tf_op jit(solution)/shard_map/ppermute | solution.py:634
  13.9 0.1 collective-permute-start.2
  14.0 1.9 %collective-permute-start.1 = (bf16[128,128]{1,0:T(8,128)(2,1)S(1)}, bf16[128,128]{1,0:T(8,128)(2,1)S(1)}, u32[]{:S(2)}, u32[]{:S(2)}) collective-permute-start(bf16[128,128]{1,0:T(8,128)(2,1)S(1)} %get-tuple-element.33.refs_3_), channel_id=1, source_target_pairs={{0,3},{1,2},{2,1},{3,0},{4,7},{5,6},{6,5},{7,4},{8,11},{9,10},{10,... | collective-permute-start | bytes 98312 | tf_op jit(solution)/shard_map/ppermute | solution.py:634
  15.9 0.0 copy-done
  15.9 3.4 %fold.1 = (bf16[256,1536]{1,0:T(8,128)(2,1)S(1)}, bf16[256,1536]{1,0:T(8,128)(2,1)S(1)}, f32[1,1536]{1,0:T(1,128)S(1)}, bf16[4,256,128]{2,1,0:T(8,128)(2,1)S(1)}, bf16[4,256,128]{2,1,0:T(8,128)(2,1)S(1)}) custom-call(bf16[80,3072]{1,0:T(8,128)(2,1)S(1)} %get-tuple-element.34.lhs_ref, f32[2,128]{1,0:T(2,128)S(1)} %copy-done, ...), custom_call_target="tpu_custom_call" | custom-call | flops 1358954496 | bytes 9437184 | tf_op jit(solution)/shard_map/fold/pallas_call | solution.py:276
  19.3 0.0 collective-permute-done.3.refs_2_
  19.3 0.0 collective-permute-done.2.refs_1_
  19.3 0.0 collective-permute-done.1.refs_0_
  19.3 2.9 %first_block.1 = (bf16[256,512]{1,0:T(8,128)(2,1)S(1)}, bf16[512,128]{1,0:T(8,128)(2,1)S(1)}, bf16[4,1280,128]{2,1,0:T(8,128)(2,1)S(1)}, bf16[4,1280,128]{2,1,0:T(8,128)(2,1)S(1)}) custom-call(bf16[128,128]{1,0:T(8,128)(2,1)S(1)} %collective-permute-done.1.refs_0_, bf16[128,128]{1,0:T(8,128)(2,1)S(1)} %collective-permute-done.2.refs_1_, ...), custom_call_target="tpu_custom_call" | custom-call | flops 805306368 | bytes 3145728 | tf_op jit(solution)/shard_map/first_block/pallas_call | solution.py:493
  22.2 1.5 %collective-permute-start.4 = (bf16[256,512]{1,0:T(8,128)(2,1)S(1)}, bf16[256,512]{1,0:T(8,128)(2,1)S(1)}, u32[]{:S(2)}, u32[]{:S(2)}) collective-permute-start(bf16[256,512]{1,0:T(8,128)(2,1)S(1)} %get-tuple-element.45), channel_id=1, source_target_pairs={{0,3},{1,2},{2,1},{3,0},{4,7},{5,6},{6,5},{7,4},{8,11},{9,10},{10,... | collective-permute-start | bytes 786440 | tf_op jit(solution)/shard_map/ppermute | solution.py:634
  23.6 3.7 %attend.1 = (bf16[256,512]{1,0:T(8,128)(2,1)S(1)}, bf16[256,512]{1,0:T(8,128)(2,1)S(1)}) custom-call(bf16[512,128]{1,0:T(8,128)(2,1)S(1)} %get-tuple-element.46.refs_1_.refs_0_, bf16[256,1536]{1,0:T(8,128)(2,1)S(1)} %get-tuple-element.39.refs_4_.refs_2_.refs_1_, bf16[256,1536]{1,0:T(8,128)(2,1)S(1)} %get-tuple-element.40.refs_5_.refs_3_.refs_2_, ...), custom_call_target="tpu_custom_call" | custom-call | flops 65536 | bytes 262144 | tf_op jit(solution)/shard_map/attend/pallas_call | solution.py:525
  27.3 1.6 %collective-permute-start.5 = (bf16[256,512]{1,0:T(8,128)(2,1)S(1)}, bf16[256,512]{1,0:T(8,128)(2,1)S(1)}, u32[]{:S(2)}, u32[]{:S(2)}) collective-permute-start(bf16[256,512]{1,0:T(8,128)(2,1)S(1)} %get-tuple-element.49), channel_id=1, source_target_pairs={{0,2},{1,3},{2,0},{3,1},{4,6},{5,7},{6,4},{7,5},{8,10},{9,11},{10,... | collective-permute-start | bytes 786440 | tf_op jit(solution)/shard_map/ppermute | solution.py:634
  28.9 0.5 %collective-permute-start.6 = (bf16[256,512]{1,0:T(8,128)(2,1)S(1)}, bf16[256,512]{1,0:T(8,128)(2,1)S(1)}, u32[]{:S(2)}, u32[]{:S(2)}) collective-permute-start(bf16[256,512]{1,0:T(8,128)(2,1)S(1)} %get-tuple-element.50), channel_id=1, source_target_pairs={{0,1},{1,0},{2,3},{3,2},{4,5},{5,4},{6,7},{7,6},{8,9},{9,8},{10,11... | collective-permute-start | bytes 786440 | tf_op jit(solution)/shard_map/ppermute | solution.py:634
  29.5 1.1 %collective-permute-done.4.refs_0_ = bf16[256,512]{1,0:T(8,128)(2,1)S(1)} collective-permute-done((bf16[256,512]{1,0:T(8,128)(2,1)S(1)}, bf16[256,512]{1,0:T(8,128)(2,1)S(1)}, u32[]{:S(2)}, u32[]{:S(2)}) %collective-permute-start.4) | collective-permute-done | bytes 262176 | tf_op jit(solution)/shard_map/ppermute | solution.py:634
  30.6 2.7 %own_block.1.refs_0_ = bf16[256,2048]{1,0:T(8,128)(2,1)} custom-call(bf16[256,512]{1,0:T(8,128)(2,1)S(1)} %collective-permute-done.4.refs_0_, bf16[512,128]{1,0:T(8,128)(2,1)S(1)} %get-tuple-element.46.refs_1_.refs_0_, bf16[256,1536]{1,0:T(8,128)(2,1)S(1)} %get-tuple-element.39.refs_4_.refs_2_.refs_1_, ...), custom_call_target="tpu_custom_call" | custom-call | flops 65536 | bytes 262144 | tf_op jit(solution)/shard_map/own_block/pallas_call | solution.py:588
  33.2 2.4 %collective-permute-done.5.refs_1_ = bf16[256,512]{1,0:T(8,128)(2,1)S(1)} collective-permute-done((bf16[256,512]{1,0:T(8,128)(2,1)S(1)}, bf16[256,512]{1,0:T(8,128)(2,1)S(1)}, u32[]{:S(2)}, u32[]{:S(2)}) %collective-permute-start.5) | collective-permute-done | bytes 262176 | tf_op jit(solution)/shard_map/ppermute | solution.py:634
  35.7 0.1 collective-permute-done.6.refs_2_
  35.7 0.8 %rest.1 = bf16[256,2048]{1,0:T(8,128)(2,1)} custom-call(bf16[256,2048]{1,0:T(8,128)(2,1)} %own_block.1.refs_0_, bf16[256,512]{1,0:T(8,128)(2,1)S(1)} %collective-permute-done.5.refs_1_, bf16[256,512]{1,0:T(8,128)(2,1)S(1)} %collective-permute-done.6.refs_2_), custom_call_target="tpu_custom_call", output_to_operand_aliasing={{}: (0, {})} | custom-call | bytes 1048576 | tf_op jit(solution)/shard_map/rest/pallas_call | solution.py:616
Async XLA Ops:
  1.1 8.3 %collective-permute-start = (bf16[8,1,64,128]{3,2,1,0:T(8,128)(2,1)S(1)}, bf16[8,1,64,128]{3,2,1,0:T(8,128)(2,1)S(1)}, u32[]{:S(2)}, u32[]{:S(2)}) collective-permute-start(bf16[8,1,64,128]{3,2,1,0:T(8,128)(2,1)S(1)} %get-tuple-element.31), channel_id=1, source_target_pairs={{0,1},{1,2},{2,3},{3,0},{4,5},{5,6},{6,7},{7,4},{8,9},{9,10},{10,1... | collective-permute-start | bytes 393224 | tf_op jit(solution)/shard_map/ppermute | solution.py:638
  4.1 5.3 %copy-start.1 = (bf16[256,16]{0,1:T(8,128)(2,1)S(1)}, bf16[256,16]{0,1:T(8,128)(2,1)}, u32[]{:S(2)}) copy-start(bf16[256,16]{0,1:T(8,128)(2,1)} %param.11) | copy-start | bytes 24580
  9.4 6.5 %copy-start = (f32[2,128]{1,0:T(2,128)S(1)}, f32[2,128]{1,0:T(2,128)}, u32[]{:S(2)}) copy-start(f32[2,128]{1,0:T(2,128)} %refs_5_.1) | copy-start | bytes 3076
  12.4 6.9 %collective-permute-start.3 = (bf16[128,128]{1,0:T(8,128)(2,1)S(1)}, bf16[128,128]{1,0:T(8,128)(2,1)S(1)}, u32[]{:S(2)}, u32[]{:S(2)}) collective-permute-start(bf16[128,128]{1,0:T(8,128)(2,1)S(1)} %get-tuple-element.33.refs_3_), channel_id=1, source_target_pairs={{0,1},{1,0},{2,3},{3,2},{4,5},{5,4},{6,7},{7,6},{8,9},{9,8},{10,11... | collective-permute-start | bytes 98312 | tf_op jit(solution)/shard_map/ppermute | solution.py:634
  13.9 5.4 %collective-permute-start.2 = (bf16[128,128]{1,0:T(8,128)(2,1)S(1)}, bf16[128,128]{1,0:T(8,128)(2,1)S(1)}, u32[]{:S(2)}, u32[]{:S(2)}) collective-permute-start(bf16[128,128]{1,0:T(8,128)(2,1)S(1)} %get-tuple-element.33.refs_3_), channel_id=1, source_target_pairs={{0,2},{1,3},{2,0},{3,1},{4,6},{5,7},{6,4},{7,5},{8,10},{9,11},{10,... | collective-permute-start | bytes 98312 | tf_op jit(solution)/shard_map/ppermute | solution.py:634
  14.0 5.3 %collective-permute-start.1 = (bf16[128,128]{1,0:T(8,128)(2,1)S(1)}, bf16[128,128]{1,0:T(8,128)(2,1)S(1)}, u32[]{:S(2)}, u32[]{:S(2)}) collective-permute-start(bf16[128,128]{1,0:T(8,128)(2,1)S(1)} %get-tuple-element.33.refs_3_), channel_id=1, source_target_pairs={{0,3},{1,2},{2,1},{3,0},{4,7},{5,6},{6,5},{7,4},{8,11},{9,10},{10,... | collective-permute-start | bytes 98312 | tf_op jit(solution)/shard_map/ppermute | solution.py:634
  22.2 8.4 %collective-permute-start.4 = (bf16[256,512]{1,0:T(8,128)(2,1)S(1)}, bf16[256,512]{1,0:T(8,128)(2,1)S(1)}, u32[]{:S(2)}, u32[]{:S(2)}) collective-permute-start(bf16[256,512]{1,0:T(8,128)(2,1)S(1)} %get-tuple-element.45), channel_id=1, source_target_pairs={{0,3},{1,2},{2,1},{3,0},{4,7},{5,6},{6,5},{7,4},{8,11},{9,10},{10,... | collective-permute-start | bytes 786440 | tf_op jit(solution)/shard_map/ppermute | solution.py:634
  27.3 8.4 %collective-permute-start.5 = (bf16[256,512]{1,0:T(8,128)(2,1)S(1)}, bf16[256,512]{1,0:T(8,128)(2,1)S(1)}, u32[]{:S(2)}, u32[]{:S(2)}) collective-permute-start(bf16[256,512]{1,0:T(8,128)(2,1)S(1)} %get-tuple-element.49), channel_id=1, source_target_pairs={{0,2},{1,3},{2,0},{3,1},{4,6},{5,7},{6,4},{7,5},{8,10},{9,11},{10,... | collective-permute-start | bytes 786440 | tf_op jit(solution)/shard_map/ppermute | solution.py:634
  28.9 6.8 %collective-permute-start.6 = (bf16[256,512]{1,0:T(8,128)(2,1)S(1)}, bf16[256,512]{1,0:T(8,128)(2,1)S(1)}, u32[]{:S(2)}, u32[]{:S(2)}) collective-permute-start(bf16[256,512]{1,0:T(8,128)(2,1)S(1)} %get-tuple-element.50), channel_id=1, source_target_pairs={{0,1},{1,0},{2,3},{3,2},{4,5},{5,4},{6,7},{7,6},{8,9},{9,8},{10,11... | collective-permute-start | bytes 786440 | tf_op jit(solution)/shard_map/ppermute | solution.py:634

commit v7 on v6

--- a/solution.py
+++ b/solution.py
@@ -169,6 +169,8 @@
         c.start()
     embed_side(e_ref, mod_ref, lhs_ref, gram_ref, centred_ref)
     first.wait()
+    for copy in ahead:
+        copy.start()
     few = 16
     for r in range(0, text_ref.shape[0], few):
         text = text_ref[r : r + few, :].astype(F32)
@@ -178,9 +180,6 @@
     flat = w_ref.reshape(taken * parts, width)
     for c in range(chunks):
         copies[c].wait()
-        if c == 0:
-            for copy in ahead:
-                copy.start()
         at = slice(c * deep, (c + 1) * deep)
         add_text(stream_ref[:, at], flat.at[2 * c * deep : 2 * (c + 1) * deep], acc_ref, c == 0)
     for c in ahead:
@@ -644,7 +643,7 @@
         video,
         conv_weight.reshape(-1, conv_weight.shape[-1]),
     )
-    patches, weight_near = conv_side(tile, halo, taps, latent_weight, weight, weight.shape[1] * 2 // 3)
+    patches, weight_near = conv_side(tile, halo, taps, latent_weight, weight, weight.shape[1] // 2)
     order = tuple(range(n - 1, -1, -1))
     received = [swap(patches, k) if k else patches for k in order]
     rhs0, rhs1, shift, tkey, tvalue = fold(lhs, qk_gain, weight_near, part, stream, last, weight)

time: 36.9 us -> 36.5 us (0.989)
  Pallas kernels: 22.7 us -> 22.3 us
where the time goes in v7:
time: 36.5 us; the launch traced here: 36.4 us
  Pallas kernels  22.3 us (61%)
  starting transfers between devices  10.2 us (28%)
  waiting for transfers between devices  3.61 us (10%)
    ppermute x6, starting transfers between devices, swap(): return lax.ppermute(x, 'ctx', [(i, i ^ k) for i in range(n)])  7.17 us
    pallas_call x1, Pallas kernels, text_side(): pl.pallas_call(lambda *refs: text_kernel(chunks, *refs), out_shape=(jax.S...  5.24 us
    pallas_call x1, Pallas kernels, attend(): pl.pallas_call(lambda *refs: attend_kernel(n, frames // n, first, *refs),...  3.65 us
    ppermute x6, waiting for transfers between devices, swap(): return lax.ppermute(x, 'ctx', [(i, i ^ k) for i in range(n)])  3.61 us
    pallas_call x1, Pallas kernels, fold(): pl.pallas_call(fold_kernel, out_shape=(jax.ShapeDtypeStruct((4 * (rows -...  3.33 us
    ppermute x1, starting transfers between devices, shards(): halo = lax.ppermute(edge_row, 'ctx', [(i, (i + 1) % n) for i in range(n)])  2.99 us
    pallas_call x1, Pallas kernels, first_block(): pl.pallas_call(lambda *refs: first_kernel(order, frames, *refs), out_shap...  2.86 us
    pallas_call x1, Pallas kernels, own_block(): pl.pallas_call(lambda *refs: own_kernel(n, frames // n, far, *refs), out_...  2.68 us
  transfers between devices with their start and end apart: 7, of which 3 were waited for; matrix products, arithmetic and copies ran while one was open for 0% of the time, Pallas kernels for 41%

profile of v7, /device:TPU:0, one launch (start us, length us, event | category | flops | bytes accessed | tf_op | source)
XLA Modules:
  0.0 36.4 jit_solution(13137319472213306207)
XLA Ops:
  0.0 1.1 %edge.1 = (bf16[8,1,64,128]{3,2,1,0:T(8,128)(2,1)S(1)}, bf16[64,3072]{1,0:T(8,128)(2,1)S(1)}, f32[4,3072]{1,0:T(4,128)S(1)}) custom-call(bf16[8,8,64,128]{3,2,1,0:T(8,128)(2,1)} %refs_4_.1, bf16[64,3072]{1,0:T(8,128)(2,1)} %e_hbm.1, f32[4,3072]{1,0:T(4,128)} %mod_hbm.1), custom_call_target="tpu_custom_call" | custom-call | bytes 884736 | tf_op jit(solution)/shard_map/edge/pallas_call | solution.py:77
  1.1 3.0 %collective-permute-start = (bf16[8,1,64,128]{3,2,1,0:T(8,128)(2,1)S(1)}, bf16[8,1,64,128]{3,2,1,0:T(8,128)(2,1)S(1)}, u32[]{:S(2)}, u32[]{:S(2)}) collective-permute-start(bf16[8,1,64,128]{3,2,1,0:T(8,128)(2,1)S(1)} %get-tuple-element.31), channel_id=1, source_target_pairs={{0,1},{1,2},{2,3},{3,0},{4,5},{5,6},{6,7},{7,4},{8,9},{9,10},{10,1... | collective-permute-start | bytes 393224 | tf_op jit(solution)/shard_map/ppermute | solution.py:637
  4.1 0.0 copy-start.1
  4.1 5.2 %text_side.1 = (bf16[80,3072]{1,0:T(8,128)(2,1)S(1)}, bf16[256,128]{1,0:T(8,128)(2,1)S(1)}, f32[2,256,512]{2,1,0:T(8,128)S(1)}, bf16[256,3072]{1,0:T(8,128)(2,1)...) custom-call(bf16[64,3072]{1,0:T(8,128)(2,1)S(1)} %get-tuple-element.28.r, ...), custom_call_target="tpu_custom_call" | custom-call | flops 3221225472 | bytes 10682368 | tf_op jit(solution)/shard_map/text_side/pallas_call | solution.py:195
  9.3 0.0 collective-permute-done.refs_1_
  9.4 0.0 copy-done.1
  9.4 0.0 copy-start
  9.4 2.7 %conv_side.1 = (bf16[128,128]{1,0:T(8,128)(2,1)S(1)}, bf16[3,1536,512]{2,1,0:T(8,128)(2,1)S(1)}) custom-call(bf16[8,8,64,128]{3,2,1,0:T(8,128)(2,1)S(1)} %get-tuple-element.30.refs_0_, bf16[8,1,64,128]{3,2,1,0:T(8,128)(2,1)S(1)} %collective-permute-done.refs_1_, bf16[3456,256]{1,0:T(8,128)(2,1)S(1)} %get-tuple-element.32.refs_2_, ...), custom_call_target="tpu_custom_call" | custom-call | flops 1811939328 | bytes 2949120 | tf_op jit(solution)/shard_map/conv_side/pallas_call | solution.py:378
  12.1 1.6 %collective-permute-start.3 = (bf16[128,128]{1,0:T(8,128)(2,1)S(1)}, bf16[128,128]{1,0:T(8,128)(2,1)S(1)}, u32[]{:S(2)}, u32[]{:S(2)}) collective-permute-start(bf16[128,128]{1,0:T(8,128)(2,1)S(1)} %get-tuple-element.33.refs_3_), channel_id=1, source_target_pairs={{0,1},{1,0},{2,3},{3,2},{4,5},{5,4},{6,7},{7,6},{8,9},{9,8},{10,11... | collective-permute-start | bytes 98312 | tf_op jit(solution)/shard_map/ppermute | solution.py:633
  13.6 0.1 collective-permute-start.2
  13.7 1.9 %collective-permute-start.1 = (bf16[128,128]{1,0:T(8,128)(2,1)S(1)}, bf16[128,128]{1,0:T(8,128)(2,1)S(1)}, u32[]{:S(2)}, u32[]{:S(2)}) collective-permute-start(bf16[128,128]{1,0:T(8,128)(2,1)S(1)} %get-tuple-element.33.refs_3_), channel_id=1, source_target_pairs={{0,3},{1,2},{2,1},{3,0},{4,7},{5,6},{6,5},{7,4},{8,11},{9,10},{10,... | collective-permute-start | bytes 98312 | tf_op jit(solution)/shard_map/ppermute | solution.py:633
  15.6 0.0 copy-done
  15.6 3.3 %fold.1 = (bf16[256,1536]{1,0:T(8,128)(2,1)S(1)}, bf16[256,1536]{1,0:T(8,128)(2,1)S(1)}, f32[1,1536]{1,0:T(1,128)S(1)}, bf16[4,256,128]{2,1,0:T(8,128)(2,1)S(1)}, bf16[4,256,128]{2,1,0:T(8,128)(2,1)S(1)}) custom-call(bf16[80,3072]{1,0:T(8,128)(2,1)S(1)} %get-tuple-element.34.lhs_ref, f32[2,128]{1,0:T(2,128)S(1)} %copy-done, ...), custom_call_target="tpu_custom_call" | custom-call | flops 1358954496 | bytes 9437184 | tf_op jit(solution)/shard_map/fold/pallas_call | solution.py:275
  19.0 0.0 collective-permute-done.3.refs_2_
  19.0 0.0 collective-permute-done.2.refs_1_
  19.0 0.0 collective-permute-done.1.refs_0_
  19.0 2.9 %first_block.1 = (bf16[256,512]{1,0:T(8,128)(2,1)S(1)}, bf16[512,128]{1,0:T(8,128)(2,1)S(1)}, bf16[4,1280,128]{2,1,0:T(8,128)(2,1)S(1)}, bf16[4,1280,128]{2,1,0:T(8,128)(2,1)S(1)}) custom-call(bf16[128,128]{1,0:T(8,128)(2,1)S(1)} %collective-permute-done.1.refs_0_, bf16[128,128]{1,0:T(8,128)(2,1)S(1)} %collective-permute-done.2.refs_1_, ...), custom_call_target="tpu_custom_call" | custom-call | flops 805306368 | bytes 3145728 | tf_op jit(solution)/shard_map/first_block/pallas_call | solution.py:492
  21.9 1.5 %collective-permute-start.4 = (bf16[256,512]{1,0:T(8,128)(2,1)S(1)}, bf16[256,512]{1,0:T(8,128)(2,1)S(1)}, u32[]{:S(2)}, u32[]{:S(2)}) collective-permute-start(bf16[256,512]{1,0:T(8,128)(2,1)S(1)} %get-tuple-element.45), channel_id=1, source_target_pairs={{0,3},{1,2},{2,1},{3,0},{4,7},{5,6},{6,5},{7,4},{8,11},{9,10},{10,... | collective-permute-start | bytes 786440 | tf_op jit(solution)/shard_map/ppermute | solution.py:633
  23.4 3.6 %attend.1 = (bf16[256,512]{1,0:T(8,128)(2,1)S(1)}, bf16[256,512]{1,0:T(8,128)(2,1)S(1)}) custom-call(bf16[512,128]{1,0:T(8,128)(2,1)S(1)} %get-tuple-element.46.refs_1_.refs_0_, bf16[256,1536]{1,0:T(8,128)(2,1)S(1)} %get-tuple-element.39.refs_4_.refs_2_.refs_1_, bf16[256,1536]{1,0:T(8,128)(2,1)S(1)} %get-tuple-element.40.refs_5_.refs_3_.refs_2_, ...), custom_call_target="tpu_custom_call" | custom-call | flops 65536 | bytes 262144 | tf_op jit(solution)/shard_map/attend/pallas_call | solution.py:524
  27.0 1.6 %collective-permute-start.5 = (bf16[256,512]{1,0:T(8,128)(2,1)S(1)}, bf16[256,512]{1,0:T(8,128)(2,1)S(1)}, u32[]{:S(2)}, u32[]{:S(2)}) collective-permute-start(bf16[256,512]{1,0:T(8,128)(2,1)S(1)} %get-tuple-element.49), channel_id=1, source_target_pairs={{0,2},{1,3},{2,0},{3,1},{4,6},{5,7},{6,4},{7,5},{8,10},{9,11},{10,... | collective-permute-start | bytes 786440 | tf_op jit(solution)/shard_map/ppermute | solution.py:633
  28.6 0.5 %collective-permute-start.6 = (bf16[256,512]{1,0:T(8,128)(2,1)S(1)}, bf16[256,512]{1,0:T(8,128)(2,1)S(1)}, u32[]{:S(2)}, u32[]{:S(2)}) collective-permute-start(bf16[256,512]{1,0:T(8,128)(2,1)S(1)} %get-tuple-element.50), channel_id=1, source_target_pairs={{0,1},{1,0},{2,3},{3,2},{4,5},{5,4},{6,7},{7,6},{8,9},{9,8},{10,11... | collective-permute-start | bytes 786440 | tf_op jit(solution)/shard_map/ppermute | solution.py:633
  29.1 1.1 %collective-permute-done.4.refs_0_ = bf16[256,512]{1,0:T(8,128)(2,1)S(1)} collective-permute-done((bf16[256,512]{1,0:T(8,128)(2,1)S(1)}, bf16[256,512]{1,0:T(8,128)(2,1)S(1)}, u32[]{:S(2)}, u32[]{:S(2)}) %collective-permute-start.4) | collective-permute-done | bytes 262176 | tf_op jit(solution)/shard_map/ppermute | solution.py:633
  30.3 2.7 %own_block.1.refs_0_ = bf16[256,2048]{1,0:T(8,128)(2,1)} custom-call(bf16[256,512]{1,0:T(8,128)(2,1)S(1)} %collective-permute-done.4.refs_0_, bf16[512,128]{1,0:T(8,128)(2,1)S(1)} %get-tuple-element.46.refs_1_.refs_0_, bf16[256,1536]{1,0:T(8,128)(2,1)S(1)} %get-tuple-element.39.refs_4_.refs_2_.refs_1_, ...), custom_call_target="tpu_custom_call" | custom-call | flops 65536 | bytes 262144 | tf_op jit(solution)/shard_map/own_block/pallas_call | solution.py:587
  32.9 2.4 %collective-permute-done.5.refs_1_ = bf16[256,512]{1,0:T(8,128)(2,1)S(1)} collective-permute-done((bf16[256,512]{1,0:T(8,128)(2,1)S(1)}, bf16[256,512]{1,0:T(8,128)(2,1)S(1)}, u32[]{:S(2)}, u32[]{:S(2)}) %collective-permute-start.5) | collective-permute-done | bytes 262176 | tf_op jit(solution)/shard_map/ppermute | solution.py:633
  35.4 0.1 collective-permute-done.6.refs_2_
  35.4 0.8 %rest.1 = bf16[256,2048]{1,0:T(8,128)(2,1)} custom-call(bf16[256,2048]{1,0:T(8,128)(2,1)} %own_block.1.refs_0_, bf16[256,512]{1,0:T(8,128)(2,1)S(1)} %collective-permute-done.5.refs_1_, bf16[256,512]{1,0:T(8,128)(2,1)S(1)} %collective-permute-done.6.refs_2_), custom_call_target="tpu_custom_call", output_to_operand_aliasing={{}: (0, {})} | custom-call | bytes 1048576 | tf_op jit(solution)/shard_map/rest/pallas_call | solution.py:615
Async XLA Ops:
  1.1 8.2 %collective-permute-start = (bf16[8,1,64,128]{3,2,1,0:T(8,128)(2,1)S(1)}, bf16[8,1,64,128]{3,2,1,0:T(8,128)(2,1)S(1)}, u32[]{:S(2)}, u32[]{:S(2)}) collective-permute-start(bf16[8,1,64,128]{3,2,1,0:T(8,128)(2,1)S(1)} %get-tuple-element.31), channel_id=1, source_target_pairs={{0,1},{1,2},{2,3},{3,0},{4,5},{5,6},{6,7},{7,4},{8,9},{9,10},{10,1... | collective-permute-start | bytes 393224 | tf_op jit(solution)/shard_map/ppermute | solution.py:637
  4.1 5.3 %copy-start.1 = (bf16[256,16]{0,1:T(8,128)(2,1)S(1)}, bf16[256,16]{0,1:T(8,128)(2,1)}, u32[]{:S(2)}) copy-start(bf16[256,16]{0,1:T(8,128)(2,1)} %param.11) | copy-start | bytes 24580
  9.4 6.2 %copy-start = (f32[2,128]{1,0:T(2,128)S(1)}, f32[2,128]{1,0:T(2,128)}, u32[]{:S(2)}) copy-start(f32[2,128]{1,0:T(2,128)} %refs_5_.1) | copy-start | bytes 3076
  12.1 6.9 %collective-permute-start.3 = (bf16[128,128]{1,0:T(8,128)(2,1)S(1)}, bf16[128,128]{1,0:T(8,128)(2,1)S(1)}, u32[]{:S(2)}, u32[]{:S(2)}) collective-permute-start(bf16[128,128]{1,0:T(8,128)(2,1)S(1)} %get-tuple-element.33.refs_3_), channel_id=1, source_target_pairs={{0,1},{1,0},{2,3},{3,2},{4,5},{5,4},{6,7},{7,6},{8,9},{9,8},{10,11... | collective-permute-start | bytes 98312 | tf_op jit(solution)/shard_map/ppermute | solution.py:633
  13.6 5.4 %collective-permute-start.2 = (bf16[128,128]{1,0:T(8,128)(2,1)S(1)}, bf16[128,128]{1,0:T(8,128)(2,1)S(1)}, u32[]{:S(2)}, u32[]{:S(2)}) collective-permute-start(bf16[128,128]{1,0:T(8,128)(2,1)S(1)} %get-tuple-element.33.refs_3_), channel_id=1, source_target_pairs={{0,2},{1,3},{2,0},{3,1},{4,6},{5,7},{6,4},{7,5},{8,10},{9,11},{10,... | collective-permute-start | bytes 98312 | tf_op jit(solution)/shard_map/ppermute | solution.py:633
  13.7 5.3 %collective-permute-start.1 = (bf16[128,128]{1,0:T(8,128)(2,1)S(1)}, bf16[128,128]{1,0:T(8,128)(2,1)S(1)}, u32[]{:S(2)}, u32[]{:S(2)}) collective-permute-start(bf16[128,128]{1,0:T(8,128)(2,1)S(1)} %get-tuple-element.33.refs_3_), channel_id=1, source_target_pairs={{0,3},{1,2},{2,1},{3,0},{4,7},{5,6},{6,5},{7,4},{8,11},{9,10},{10,... | collective-permute-start | bytes 98312 | tf_op jit(solution)/shard_map/ppermute | solution.py:633
  21.9 8.4 %collective-permute-start.4 = (bf16[256,512]{1,0:T(8,128)(2,1)S(1)}, bf16[256,512]{1,0:T(8,128)(2,1)S(1)}, u32[]{:S(2)}, u32[]{:S(2)}) collective-permute-start(bf16[256,512]{1,0:T(8,128)(2,1)S(1)} %get-tuple-element.45), channel_id=1, source_target_pairs={{0,3},{1,2},{2,1},{3,0},{4,7},{5,6},{6,5},{7,4},{8,11},{9,10},{10,... | collective-permute-start | bytes 786440 | tf_op jit(solution)/shard_map/ppermute | solution.py:633
  27.0 8.4 %collective-permute-start.5 = (bf16[256,512]{1,0:T(8,128)(2,1)S(1)}, bf16[256,512]{1,0:T(8,128)(2,1)S(1)}, u32[]{:S(2)}, u32[]{:S(2)}) collective-permute-start(bf16[256,512]{1,0:T(8,128)(2,1)S(1)} %get-tuple-element.49), channel_id=1, source_target_pairs={{0,2},{1,3},{2,0},{3,1},{4,6},{5,7},{6,4},{7,5},{8,10},{9,11},{10,... | collective-permute-start | bytes 786440 | tf_op jit(solution)/shard_map/ppermute | solution.py:633
  28.6 6.8 %collective-permute-start.6 = (bf16[256,512]{1,0:T(8,128)(2,1)S(1)}, bf16[256,512]{1,0:T(8,128)(2,1)S(1)}, u32[]{:S(2)}, u32[]{:S(2)}) collective-permute-start(bf16[256,512]{1,0:T(8,128)(2,1)S(1)} %get-tuple-element.50), channel_id=1, source_target_pairs={{0,1},{1,0},{2,3},{3,2},{4,5},{5,4},{6,7},{7,6},{8,9},{9,8},{10,11... | collective-permute-start | bytes 786440 | tf_op jit(solution)/shard_map/ppermute | solution.py:633

commit v8 on v7

--- a/solution.py
+++ b/solution.py
@@ -436,7 +436,7 @@
             for c in range(HS, total, HS):
                 norm = norm + weights[:, c : c + HS]
             norm = jnp.sum(norm, -1, keepdims=True)
-            attended = (dot(weights.astype(BF16), value_ref[h]) / norm).astype(BF16)
+            attended = (dot(weights.astype(BF16), value_ref[h]) * (1.0 / norm)).astype(BF16)
             for g, ref in enumerate(group):
                 ref[:, h * HS : (h + 1) * HS] = attended[g * rows : (g + 1) * rows]
 

time: 36.5 us -> 36.5 us (level)
  no operation moved by 1% of the time
where the time goes in v8:
time: 36.5 us; the launch traced here: 36.4 us
  Pallas kernels  22.3 us (61%)
  starting transfers between devices  10.2 us (28%)
  waiting for transfers between devices  3.61 us (10%)
    ppermute x6, starting transfers between devices, swap(): return lax.ppermute(x, 'ctx', [(i, i ^ k) for i in range(n)])  7.17 us
    pallas_call x1, Pallas kernels, text_side(): pl.pallas_call(lambda *refs: text_kernel(chunks, *refs), out_shape=(jax.S...  5.24 us
    pallas_call x1, Pallas kernels, attend(): pl.pallas_call(lambda *refs: attend_kernel(n, frames // n, first, *refs),...  3.65 us
    ppermute x6, waiting for transfers between devices, swap(): return lax.ppermute(x, 'ctx', [(i, i ^ k) for i in range(n)])  3.61 us
    pallas_call x1, Pallas kernels, fold(): pl.pallas_call(fold_kernel, out_shape=(jax.ShapeDtypeStruct((4 * (rows -...  3.33 us
    ppermute x1, starting transfers between devices, shards(): halo = lax.ppermute(edge_row, 'ctx', [(i, (i + 1) % n) for i in range(n)])  2.99 us
    pallas_call x1, Pallas kernels, first_block(): pl.pallas_call(lambda *refs: first_kernel(order, frames, *refs), out_shap...  2.86 us
    pallas_call x1, Pallas kernels, own_block(): pl.pallas_call(lambda *refs: own_kernel(n, frames // n, far, *refs), out_...  2.68 us
  transfers between devices with their start and end apart: 7, of which 3 were waited for; matrix products, arithmetic and copies ran while one was open for 0% of the time, Pallas kernels for 41%

profile of v8, /device:TPU:0, one launch (start us, length us, event | category | flops | bytes accessed | tf_op | source)
XLA Modules:
  0.0 36.4 jit_solution(13137319472213306207)
XLA Ops:
  0.0 1.1 %edge.1 = (bf16[8,1,64,128]{3,2,1,0:T(8,128)(2,1)S(1)}, bf16[64,3072]{1,0:T(8,128)(2,1)S(1)}, f32[4,3072]{1,0:T(4,128)S(1)}) custom-call(bf16[8,8,64,128]{3,2,1,0:T(8,128)(2,1)} %refs_4_.1, bf16[64,3072]{1,0:T(8,128)(2,1)} %e_hbm.1, f32[4,3072]{1,0:T(4,128)} %mod_hbm.1), custom_call_target="tpu_custom_call" | custom-call | bytes 884736 | tf_op jit(solution)/shard_map/edge/pallas_call | solution.py:77
  1.1 3.0 %collective-permute-start = (bf16[8,1,64,128]{3,2,1,0:T(8,128)(2,1)S(1)}, bf16[8,1,64,128]{3,2,1,0:T(8,128)(2,1)S(1)}, u32[]{:S(2)}, u32[]{:S(2)}) collective-permute-start(bf16[8,1,64,128]{3,2,1,0:T(8,128)(2,1)S(1)} %get-tuple-element.31), channel_id=1, source_target_pairs={{0,1},{1,2},{2,3},{3,0},{4,5},{5,6},{6,7},{7,4},{8,9},{9,10},{10,1... | collective-permute-start | bytes 393224 | tf_op jit(solution)/shard_map/ppermute | solution.py:637
  4.1 0.0 copy-start.1
  4.1 5.2 %text_side.1 = (bf16[80,3072]{1,0:T(8,128)(2,1)S(1)}, bf16[256,128]{1,0:T(8,128)(2,1)S(1)}, f32[2,256,512]{2,1,0:T(8,128)S(1)}, bf16[256,3072]{1,0:T(8,128)(2,1)...) custom-call(bf16[64,3072]{1,0:T(8,128)(2,1)S(1)} %get-tuple-element.28.r, ...), custom_call_target="tpu_custom_call" | custom-call | flops 3221225472 | bytes 10682368 | tf_op jit(solution)/shard_map/text_side/pallas_call | solution.py:195
  9.3 0.0 collective-permute-done.refs_1_
  9.4 0.0 copy-done.1
  9.4 0.0 copy-start
  9.4 2.7 %conv_side.1 = (bf16[128,128]{1,0:T(8,128)(2,1)S(1)}, bf16[3,1536,512]{2,1,0:T(8,128)(2,1)S(1)}) custom-call(bf16[8,8,64,128]{3,2,1,0:T(8,128)(2,1)S(1)} %get-tuple-element.30.refs_0_, bf16[8,1,64,128]{3,2,1,0:T(8,128)(2,1)S(1)} %collective-permute-done.refs_1_, bf16[3456,256]{1,0:T(8,128)(2,1)S(1)} %get-tuple-element.32.refs_2_, ...), custom_call_target="tpu_custom_call" | custom-call | flops 1811939328 | bytes 2949120 | tf_op jit(solution)/shard_map/conv_side/pallas_call | solution.py:378
  12.1 1.6 %collective-permute-start.3 = (bf16[128,128]{1,0:T(8,128)(2,1)S(1)}, bf16[128,128]{1,0:T(8,128)(2,1)S(1)}, u32[]{:S(2)}, u32[]{:S(2)}) collective-permute-start(bf16[128,128]{1,0:T(8,128)(2,1)S(1)} %get-tuple-element.33.refs_3_), channel_id=1, source_target_pairs={{0,1},{1,0},{2,3},{3,2},{4,5},{5,4},{6,7},{7,6},{8,9},{9,8},{10,11... | collective-permute-start | bytes 98312 | tf_op jit(solution)/shard_map/ppermute | solution.py:633
  13.6 0.1 collective-permute-start.2
  13.7 1.9 %collective-permute-start.1 = (bf16[128,128]{1,0:T(8,128)(2,1)S(1)}, bf16[128,128]{1,0:T(8,128)(2,1)S(1)}, u32[]{:S(2)}, u32[]{:S(2)}) collective-permute-start(bf16[128,128]{1,0:T(8,128)(2,1)S(1)} %get-tuple-element.33.refs_3_), channel_id=1, source_target_pairs={{0,3},{1,2},{2,1},{3,0},{4,7},{5,6},{6,5},{7,4},{8,11},{9,10},{10,... | collective-permute-start | bytes 98312 | tf_op jit(solution)/shard_map/ppermute | solution.py:633
  15.6 0.0 copy-done
  15.6 3.3 %fold.1 = (bf16[256,1536]{1,0:T(8,128)(2,1)S(1)}, bf16[256,1536]{1,0:T(8,128)(2,1)S(1)}, f32[1,1536]{1,0:T(1,128)S(1)}, bf16[4,256,128]{2,1,0:T(8,128)(2,1)S(1)}, bf16[4,256,128]{2,1,0:T(8,128)(2,1)S(1)}) custom-call(bf16[80,3072]{1,0:T(8,128)(2,1)S(1)} %get-tuple-element.34.lhs_ref, f32[2,128]{1,0:T(2,128)S(1)} %copy-done, ...), custom_call_target="tpu_custom_call" | custom-call | flops 1358954496 | bytes 9437184 | tf_op jit(solution)/shard_map/fold/pallas_call | solution.py:275
  19.0 0.0 collective-permute-done.3.refs_2_
  19.0 0.0 collective-permute-done.2.refs_1_
  19.0 0.0 collective-permute-done.1.refs_0_
  19.0 2.9 %first_block.1 = (bf16[256,512]{1,0:T(8,128)(2,1)S(1)}, bf16[512,128]{1,0:T(8,128)(2,1)S(1)}, bf16[4,1280,128]{2,1,0:T(8,128)(2,1)S(1)}, bf16[4,1280,128]{2,1,0:T(8,128)(2,1)S(1)}) custom-call(bf16[128,128]{1,0:T(8,128)(2,1)S(1)} %collective-permute-done.1.refs_0_, bf16[128,128]{1,0:T(8,128)(2,1)S(1)} %collective-permute-done.2.refs_1_, ...), custom_call_target="tpu_custom_call" | custom-call | flops 805306368 | bytes 3145728 | tf_op jit(solution)/shard_map/first_block/pallas_call | solution.py:492
  21.9 1.5 %collective-permute-start.4 = (bf16[256,512]{1,0:T(8,128)(2,1)S(1)}, bf16[256,512]{1,0:T(8,128)(2,1)S(1)}, u32[]{:S(2)}, u32[]{:S(2)}) collective-permute-start(bf16[256,512]{1,0:T(8,128)(2,1)S(1)} %get-tuple-element.45), channel_id=1, source_target_pairs={{0,3},{1,2},{2,1},{3,0},{4,7},{5,6},{6,5},{7,4},{8,11},{9,10},{10,... | collective-permute-start | bytes 786440 | tf_op jit(solution)/shard_map/ppermute | solution.py:633
  23.4 3.6 %attend.1 = (bf16[256,512]{1,0:T(8,128)(2,1)S(1)}, bf16[256,512]{1,0:T(8,128)(2,1)S(1)}) custom-call(bf16[512,128]{1,0:T(8,128)(2,1)S(1)} %get-tuple-element.46.refs_1_.refs_0_, bf16[256,1536]{1,0:T(8,128)(2,1)S(1)} %get-tuple-element.39.refs_4_.refs_2_.refs_1_, bf16[256,1536]{1,0:T(8,128)(2,1)S(1)} %get-tuple-element.40.refs_5_.refs_3_.refs_2_, ...), custom_call_target="tpu_custom_call" | custom-call | flops 65536 | bytes 262144 | tf_op jit(solution)/shard_map/attend/pallas_call | solution.py:524
  27.0 1.6 %collective-permute-start.5 = (bf16[256,512]{1,0:T(8,128)(2,1)S(1)}, bf16[256,512]{1,0:T(8,128)(2,1)S(1)}, u32[]{:S(2)}, u32[]{:S(2)}) collective-permute-start(bf16[256,512]{1,0:T(8,128)(2,1)S(1)} %get-tuple-element.49), channel_id=1, source_target_pairs={{0,2},{1,3},{2,0},{3,1},{4,6},{5,7},{6,4},{7,5},{8,10},{9,11},{10,... | collective-permute-start | bytes 786440 | tf_op jit(solution)/shard_map/ppermute | solution.py:633
  28.6 0.5 %collective-permute-start.6 = (bf16[256,512]{1,0:T(8,128)(2,1)S(1)}, bf16[256,512]{1,0:T(8,128)(2,1)S(1)}, u32[]{:S(2)}, u32[]{:S(2)}) collective-permute-start(bf16[256,512]{1,0:T(8,128)(2,1)S(1)} %get-tuple-element.50), channel_id=1, source_target_pairs={{0,1},{1,0},{2,3},{3,2},{4,5},{5,4},{6,7},{7,6},{8,9},{9,8},{10,11... | collective-permute-start | bytes 786440 | tf_op jit(solution)/shard_map/ppermute | solution.py:633
  29.1 1.1 %collective-permute-done.4.refs_0_ = bf16[256,512]{1,0:T(8,128)(2,1)S(1)} collective-permute-done((bf16[256,512]{1,0:T(8,128)(2,1)S(1)}, bf16[256,512]{1,0:T(8,128)(2,1)S(1)}, u32[]{:S(2)}, u32[]{:S(2)}) %collective-permute-start.4) | collective-permute-done | bytes 262176 | tf_op jit(solution)/shard_map/ppermute | solution.py:633
  30.3 2.7 %own_block.1.refs_0_ = bf16[256,2048]{1,0:T(8,128)(2,1)} custom-call(bf16[256,512]{1,0:T(8,128)(2,1)S(1)} %collective-permute-done.4.refs_0_, bf16[512,128]{1,0:T(8,128)(2,1)S(1)} %get-tuple-element.46.refs_1_.refs_0_, bf16[256,1536]{1,0:T(8,128)(2,1)S(1)} %get-tuple-element.39.refs_4_.refs_2_.refs_1_, ...), custom_call_target="tpu_custom_call" | custom-call | flops 65536 | bytes 262144 | tf_op jit(solution)/shard_map/own_block/pallas_call | solution.py:587
  32.9 2.4 %collective-permute-done.5.refs_1_ = bf16[256,512]{1,0:T(8,128)(2,1)S(1)} collective-permute-done((bf16[256,512]{1,0:T(8,128)(2,1)S(1)}, bf16[256,512]{1,0:T(8,128)(2,1)S(1)}, u32[]{:S(2)}, u32[]{:S(2)}) %collective-permute-start.5) | collective-permute-done | bytes 262176 | tf_op jit(solution)/shard_map/ppermute | solution.py:633
  35.4 0.1 collective-permute-done.6.refs_2_
  35.4 0.8 %rest.1 = bf16[256,2048]{1,0:T(8,128)(2,1)} custom-call(bf16[256,2048]{1,0:T(8,128)(2,1)} %own_block.1.refs_0_, bf16[256,512]{1,0:T(8,128)(2,1)S(1)} %collective-permute-done.5.refs_1_, bf16[256,512]{1,0:T(8,128)(2,1)S(1)} %collective-permute-done.6.refs_2_), custom_call_target="tpu_custom_call", output_to_operand_aliasing={{}: (0, {})} | custom-call | bytes 1048576 | tf_op jit(solution)/shard_map/rest/pallas_call | solution.py:615
Async XLA Ops:
  1.1 8.2 %collective-permute-start = (bf16[8,1,64,128]{3,2,1,0:T(8,128)(2,1)S(1)}, bf16[8,1,64,128]{3,2,1,0:T(8,128)(2,1)S(1)}, u32[]{:S(2)}, u32[]{:S(2)}) collective-permute-start(bf16[8,1,64,128]{3,2,1,0:T(8,128)(2,1)S(1)} %get-tuple-element.31), channel_id=1, source_target_pairs={{0,1},{1,2},{2,3},{3,0},{4,5},{5,6},{6,7},{7,4},{8,9},{9,10},{10,1... | collective-permute-start | bytes 393224 | tf_op jit(solution)/shard_map/ppermute | solution.py:637
  4.1 5.3 %copy-start.1 = (bf16[256,16]{0,1:T(8,128)(2,1)S(1)}, bf16[256,16]{0,1:T(8,128)(2,1)}, u32[]{:S(2)}) copy-start(bf16[256,16]{0,1:T(8,128)(2,1)} %param.11) | copy-start | bytes 24580
  9.4 6.2 %copy-start = (f32[2,128]{1,0:T(2,128)S(1)}, f32[2,128]{1,0:T(2,128)}, u32[]{:S(2)}) copy-start(f32[2,128]{1,0:T(2,128)} %refs_5_.1) | copy-start | bytes 3076
  12.1 6.9 %collective-permute-start.3 = (bf16[128,128]{1,0:T(8,128)(2,1)S(1)}, bf16[128,128]{1,0:T(8,128)(2,1)S(1)}, u32[]{:S(2)}, u32[]{:S(2)}) collective-permute-start(bf16[128,128]{1,0:T(8,128)(2,1)S(1)} %get-tuple-element.33.refs_3_), channel_id=1, source_target_pairs={{0,1},{1,0},{2,3},{3,2},{4,5},{5,4},{6,7},{7,6},{8,9},{9,8},{10,11... | collective-permute-start | bytes 98312 | tf_op jit(solution)/shard_map/ppermute | solution.py:633
  13.6 5.4 %collective-permute-start.2 = (bf16[128,128]{1,0:T(8,128)(2,1)S(1)}, bf16[128,128]{1,0:T(8,128)(2,1)S(1)}, u32[]{:S(2)}, u32[]{:S(2)}) collective-permute-start(bf16[128,128]{1,0:T(8,128)(2,1)S(1)} %get-tuple-element.33.refs_3_), channel_id=1, source_target_pairs={{0,2},{1,3},{2,0},{3,1},{4,6},{5,7},{6,4},{7,5},{8,10},{9,11},{10,... | collective-permute-start | bytes 98312 | tf_op jit(solution)/shard_map/ppermute | solution.py:633
  13.7 5.3 %collective-permute-start.1 = (bf16[128,128]{1,0:T(8,128)(2,1)S(1)}, bf16[128,128]{1,0:T(8,128)(2,1)S(1)}, u32[]{:S(2)}, u32[]{:S(2)}) collective-permute-start(bf16[128,128]{1,0:T(8,128)(2,1)S(1)} %get-tuple-element.33.refs_3_), channel_id=1, source_target_pairs={{0,3},{1,2},{2,1},{3,0},{4,7},{5,6},{6,5},{7,4},{8,11},{9,10},{10,... | collective-permute-start | bytes 98312 | tf_op jit(solution)/shard_map/ppermute | solution.py:633
  21.9 8.4 %collective-permute-start.4 = (bf16[256,512]{1,0:T(8,128)(2,1)S(1)}, bf16[256,512]{1,0:T(8,128)(2,1)S(1)}, u32[]{:S(2)}, u32[]{:S(2)}) collective-permute-start(bf16[256,512]{1,0:T(8,128)(2,1)S(1)} %get-tuple-element.45), channel_id=1, source_target_pairs={{0,3},{1,2},{2,1},{3,0},{4,7},{5,6},{6,5},{7,4},{8,11},{9,10},{10,... | collective-permute-start | bytes 786440 | tf_op jit(solution)/shard_map/ppermute | solution.py:633
  27.0 8.4 %collective-permute-start.5 = (bf16[256,512]{1,0:T(8,128)(2,1)S(1)}, bf16[256,512]{1,0:T(8,128)(2,1)S(1)}, u32[]{:S(2)}, u32[]{:S(2)}) collective-permute-start(bf16[256,512]{1,0:T(8,128)(2,1)S(1)} %get-tuple-element.49), channel_id=1, source_target_pairs={{0,2},{1,3},{2,0},{3,1},{4,6},{5,7},{6,4},{7,5},{8,10},{9,11},{10,... | collective-permute-start | bytes 786440 | tf_op jit(solution)/shard_map/ppermute | solution.py:633
  28.6 6.8 %collective-permute-start.6 = (bf16[256,512]{1,0:T(8,128)(2,1)S(1)}, bf16[256,512]{1,0:T(8,128)(2,1)S(1)}, u32[]{:S(2)}, u32[]{:S(2)}) collective-permute-start(bf16[256,512]{1,0:T(8,128)(2,1)S(1)} %get-tuple-element.50), channel_id=1, source_target_pairs={{0,1},{1,0},{2,3},{3,2},{4,5},{5,4},{6,7},{7,6},{8,9},{9,8},{10,11... | collective-permute-start | bytes 786440 | tf_op jit(solution)/shard_map/ppermute | solution.py:633

commit v9 on v8

--- a/solution.py
+++ b/solution.py
@@ -171,7 +171,7 @@
     first.wait()
     for copy in ahead:
         copy.start()
-    few = 16
+    few = 32
     for r in range(0, text_ref.shape[0], few):
         text = text_ref[r : r + few, :].astype(F32)
         centred = text - jnp.mean(text, -1, keepdims=True)

time: 36.5 us -> 36.5 us (level)
  no operation moved by 1% of the time
where the time goes in v9:
time: 36.5 us; the launch traced here: 36.4 us
  Pallas kernels  22.3 us (61%)
  starting transfers between devices  10.2 us (28%)
  waiting for transfers between devices  3.6 us (10%)
    ppermute x6, starting transfers between devices, swap(): return lax.ppermute(x, 'ctx', [(i, i ^ k) for i in range(n)])  7.18 us
    pallas_call x1, Pallas kernels, text_side(): pl.pallas_call(lambda *refs: text_kernel(chunks, *refs), out_shape=(jax.S...  5.22 us
    pallas_call x1, Pallas kernels, attend(): pl.pallas_call(lambda *refs: attend_kernel(n, frames // n, first, *refs),...  3.65 us
    ppermute x6, waiting for transfers between devices, swap(): return lax.ppermute(x, 'ctx', [(i, i ^ k) for i in range(n)])  3.6 us
    pallas_call x1, Pallas kernels, fold(): pl.pallas_call(fold_kernel, out_shape=(jax.ShapeDtypeStruct((4 * (rows -...  3.34 us
    ppermute x1, starting transfers between devices, shards(): halo = lax.ppermute(edge_row, 'ctx', [(i, (i + 1) % n) for i in range(n)])  2.99 us
    pallas_call x1, Pallas kernels, first_block(): pl.pallas_call(lambda *refs: first_kernel(order, frames, *refs), out_shap...  2.86 us
    pallas_call x1, Pallas kernels, own_block(): pl.pallas_call(lambda *refs: own_kernel(n, frames // n, far, *refs), out_...  2.68 us
  transfers between devices with their start and end apart: 7, of which 3 were waited for; matrix products, arithmetic and copies ran while one was open for 0% of the time, Pallas kernels for 41%

profile of v9, /device:TPU:0, one launch (start us, length us, event | category | flops | bytes accessed | tf_op | source)
XLA Modules:
  0.0 36.4 jit_solution(17661263686715051869)
XLA Ops:
  0.0 1.1 %edge.1 = (bf16[8,1,64,128]{3,2,1,0:T(8,128)(2,1)S(1)}, bf16[64,3072]{1,0:T(8,128)(2,1)S(1)}, f32[4,3072]{1,0:T(4,128)S(1)}) custom-call(bf16[8,8,64,128]{3,2,1,0:T(8,128)(2,1)} %refs_4_.1, bf16[64,3072]{1,0:T(8,128)(2,1)} %e_hbm.1, f32[4,3072]{1,0:T(4,128)} %mod_hbm.1), custom_call_target="tpu_custom_call" | custom-call | bytes 884736 | tf_op jit(solution)/shard_map/edge/pallas_call | solution.py:77
  1.1 3.0 %collective-permute-start = (bf16[8,1,64,128]{3,2,1,0:T(8,128)(2,1)S(1)}, bf16[8,1,64,128]{3,2,1,0:T(8,128)(2,1)S(1)}, u32[]{:S(2)}, u32[]{:S(2)}) collective-permute-start(bf16[8,1,64,128]{3,2,1,0:T(8,128)(2,1)S(1)} %get-tuple-element.31), channel_id=1, source_target_pairs={{0,1},{1,2},{2,3},{3,0},{4,5},{5,6},{6,7},{7,4},{8,9},{9,10},{10,1... | collective-permute-start | bytes 393224 | tf_op jit(solution)/shard_map/ppermute | solution.py:637
  4.1 0.0 copy-start.1
  4.1 5.2 %text_side.1 = (bf16[80,3072]{1,0:T(8,128)(2,1)S(1)}, bf16[256,128]{1,0:T(8,128)(2,1)S(1)}, f32[2,256,512]{2,1,0:T(8,128)S(1)}, bf16[256,3072]{1,0:T(8,128)(2,1)...) custom-call(bf16[64,3072]{1,0:T(8,128)(2,1)S(1)} %get-tuple-element.28.r, ...), custom_call_target="tpu_custom_call" | custom-call | flops 3221225472 | bytes 10682368 | tf_op jit(solution)/shard_map/text_side/pallas_call | solution.py:195
  9.3 0.0 collective-permute-done.refs_1_
  9.3 0.0 copy-done.1
  9.3 0.0 copy-start
  9.4 2.7 %conv_side.1 = (bf16[128,128]{1,0:T(8,128)(2,1)S(1)}, bf16[3,1536,512]{2,1,0:T(8,128)(2,1)S(1)}) custom-call(bf16[8,8,64,128]{3,2,1,0:T(8,128)(2,1)S(1)} %get-tuple-element.30.refs_0_, bf16[8,1,64,128]{3,2,1,0:T(8,128)(2,1)S(1)} %collective-permute-done.refs_1_, bf16[3456,256]{1,0:T(8,128)(2,1)S(1)} %get-tuple-element.32.refs_2_, ...), custom_call_target="tpu_custom_call" | custom-call | flops 1811939328 | bytes 2949120 | tf_op jit(solution)/shard_map/conv_side/pallas_call | solution.py:378
  12.0 1.6 %collective-permute-start.3 = (bf16[128,128]{1,0:T(8,128)(2,1)S(1)}, bf16[128,128]{1,0:T(8,128)(2,1)S(1)}, u32[]{:S(2)}, u32[]{:S(2)}) collective-permute-start(bf16[128,128]{1,0:T(8,128)(2,1)S(1)} %get-tuple-element.33.refs_3_), channel_id=1, source_target_pairs={{0,1},{1,0},{2,3},{3,2},{4,5},{5,4},{6,7},{7,6},{8,9},{9,8},{10,11... | collective-permute-start | bytes 98312 | tf_op jit(solution)/shard_map/ppermute | solution.py:633
  13.6 0.1 collective-permute-start.2
  13.7 1.9 %collective-permute-start.1 = (bf16[128,128]{1,0:T(8,128)(2,1)S(1)}, bf16[128,128]{1,0:T(8,128)(2,1)S(1)}, u32[]{:S(2)}, u32[]{:S(2)}) collective-permute-start(bf16[128,128]{1,0:T(8,128)(2,1)S(1)} %get-tuple-element.33.refs_3_), channel_id=1, source_target_pairs={{0,3},{1,2},{2,1},{3,0},{4,7},{5,6},{6,5},{7,4},{8,11},{9,10},{10,... | collective-permute-start | bytes 98312 | tf_op jit(solution)/shard_map/ppermute | solution.py:633
  15.6 0.0 copy-done
  15.6 3.3 %fold.1 = (bf16[256,1536]{1,0:T(8,128)(2,1)S(1)}, bf16[256,1536]{1,0:T(8,128)(2,1)S(1)}, f32[1,1536]{1,0:T(1,128)S(1)}, bf16[4,256,128]{2,1,0:T(8,128)(2,1)S(1)}, bf16[4,256,128]{2,1,0:T(8,128)(2,1)S(1)}) custom-call(bf16[80,3072]{1,0:T(8,128)(2,1)S(1)} %get-tuple-element.34.lhs_ref, f32[2,128]{1,0:T(2,128)S(1)} %copy-done, ...), custom_call_target="tpu_custom_call" | custom-call | flops 1358954496 | bytes 9437184 | tf_op jit(solution)/shard_map/fold/pallas_call | solution.py:275
  18.9 0.0 collective-permute-done.3.refs_2_
  18.9 0.0 collective-permute-done.2.refs_1_
  19.0 0.0 collective-permute-done.1.refs_0_
  19.0 2.9 %first_block.1 = (bf16[256,512]{1,0:T(8,128)(2,1)S(1)}, bf16[512,128]{1,0:T(8,128)(2,1)S(1)}, bf16[4,1280,128]{2,1,0:T(8,128)(2,1)S(1)}, bf16[4,1280,128]{2,1,0:T(8,128)(2,1)S(1)}) custom-call(bf16[128,128]{1,0:T(8,128)(2,1)S(1)} %collective-permute-done.1.refs_0_, bf16[128,128]{1,0:T(8,128)(2,1)S(1)} %collective-permute-done.2.refs_1_, ...), custom_call_target="tpu_custom_call" | custom-call | flops 805306368 | bytes 3145728 | tf_op jit(solution)/shard_map/first_block/pallas_call | solution.py:492
  21.8 1.5 %collective-permute-start.4 = (bf16[256,512]{1,0:T(8,128)(2,1)S(1)}, bf16[256,512]{1,0:T(8,128)(2,1)S(1)}, u32[]{:S(2)}, u32[]{:S(2)}) collective-permute-start(bf16[256,512]{1,0:T(8,128)(2,1)S(1)} %get-tuple-element.45), channel_id=1, source_target_pairs={{0,3},{1,2},{2,1},{3,0},{4,7},{5,6},{6,5},{7,4},{8,11},{9,10},{10,... | collective-permute-start | bytes 786440 | tf_op jit(solution)/shard_map/ppermute | solution.py:633
  23.3 3.7 %attend.1 = (bf16[256,512]{1,0:T(8,128)(2,1)S(1)}, bf16[256,512]{1,0:T(8,128)(2,1)S(1)}) custom-call(bf16[512,128]{1,0:T(8,128)(2,1)S(1)} %get-tuple-element.46.refs_1_.refs_0_, bf16[256,1536]{1,0:T(8,128)(2,1)S(1)} %get-tuple-element.39.refs_4_.refs_2_.refs_1_, bf16[256,1536]{1,0:T(8,128)(2,1)S(1)} %get-tuple-element.40.refs_5_.refs_3_.refs_2_, ...), custom_call_target="tpu_custom_call" | custom-call | flops 65536 | bytes 262144 | tf_op jit(solution)/shard_map/attend/pallas_call | solution.py:524
  27.0 1.6 %collective-permute-start.5 = (bf16[256,512]{1,0:T(8,128)(2,1)S(1)}, bf16[256,512]{1,0:T(8,128)(2,1)S(1)}, u32[]{:S(2)}, u32[]{:S(2)}) collective-permute-start(bf16[256,512]{1,0:T(8,128)(2,1)S(1)} %get-tuple-element.49), channel_id=1, source_target_pairs={{0,2},{1,3},{2,0},{3,1},{4,6},{5,7},{6,4},{7,5},{8,10},{9,11},{10,... | collective-permute-start | bytes 786440 | tf_op jit(solution)/shard_map/ppermute | solution.py:633
  28.6 0.5 %collective-permute-start.6 = (bf16[256,512]{1,0:T(8,128)(2,1)S(1)}, bf16[256,512]{1,0:T(8,128)(2,1)S(1)}, u32[]{:S(2)}, u32[]{:S(2)}) collective-permute-start(bf16[256,512]{1,0:T(8,128)(2,1)S(1)} %get-tuple-element.50), channel_id=1, source_target_pairs={{0,1},{1,0},{2,3},{3,2},{4,5},{5,4},{6,7},{7,6},{8,9},{9,8},{10,11... | collective-permute-start | bytes 786440 | tf_op jit(solution)/shard_map/ppermute | solution.py:633
  29.1 1.1 %collective-permute-done.4.refs_0_ = bf16[256,512]{1,0:T(8,128)(2,1)S(1)} collective-permute-done((bf16[256,512]{1,0:T(8,128)(2,1)S(1)}, bf16[256,512]{1,0:T(8,128)(2,1)S(1)}, u32[]{:S(2)}, u32[]{:S(2)}) %collective-permute-start.4) | collective-permute-done | bytes 262176 | tf_op jit(solution)/shard_map/ppermute | solution.py:633
  30.3 2.7 %own_block.1.refs_0_ = bf16[256,2048]{1,0:T(8,128)(2,1)} custom-call(bf16[256,512]{1,0:T(8,128)(2,1)S(1)} %collective-permute-done.4.refs_0_, bf16[512,128]{1,0:T(8,128)(2,1)S(1)} %get-tuple-element.46.refs_1_.refs_0_, bf16[256,1536]{1,0:T(8,128)(2,1)S(1)} %get-tuple-element.39.refs_4_.refs_2_.refs_1_, ...), custom_call_target="tpu_custom_call" | custom-call | flops 65536 | bytes 262144 | tf_op jit(solution)/shard_map/own_block/pallas_call | solution.py:587
  32.9 2.4 %collective-permute-done.5.refs_1_ = bf16[256,512]{1,0:T(8,128)(2,1)S(1)} collective-permute-done((bf16[256,512]{1,0:T(8,128)(2,1)S(1)}, bf16[256,512]{1,0:T(8,128)(2,1)S(1)}, u32[]{:S(2)}, u32[]{:S(2)}) %collective-permute-start.5) | collective-permute-done | bytes 262176 | tf_op jit(solution)/shard_map/ppermute | solution.py:633
  35.3 0.1 collective-permute-done.6.refs_2_
  35.4 0.8 %rest.1 = bf16[256,2048]{1,0:T(8,128)(2,1)} custom-call(bf16[256,2048]{1,0:T(8,128)(2,1)} %own_block.1.refs_0_, bf16[256,512]{1,0:T(8,128)(2,1)S(1)} %collective-permute-done.5.refs_1_, bf16[256,512]{1,0:T(8,128)(2,1)S(1)} %collective-permute-done.6.refs_2_), custom_call_target="tpu_custom_call", output_to_operand_aliasing={{}: (0, {})} | custom-call | bytes 1048576 | tf_op jit(solution)/shard_map/rest/pallas_call | solution.py:615
Async XLA Ops:
  1.1 8.2 %collective-permute-start = (bf16[8,1,64,128]{3,2,1,0:T(8,128)(2,1)S(1)}, bf16[8,1,64,128]{3,2,1,0:T(8,128)(2,1)S(1)}, u32[]{:S(2)}, u32[]{:S(2)}) collective-permute-start(bf16[8,1,64,128]{3,2,1,0:T(8,128)(2,1)S(1)} %get-tuple-element.31), channel_id=1, source_target_pairs={{0,1},{1,2},{2,3},{3,0},{4,5},{5,6},{6,7},{7,4},{8,9},{9,10},{10,1... | collective-permute-start | bytes 393224 | tf_op jit(solution)/shard_map/ppermute | solution.py:637
  4.1 5.2 %copy-start.1 = (bf16[256,16]{0,1:T(8,128)(2,1)S(1)}, bf16[256,16]{0,1:T(8,128)(2,1)}, u32[]{:S(2)}) copy-start(bf16[256,16]{0,1:T(8,128)(2,1)} %param.11) | copy-start | bytes 24580
  9.3 6.2 %copy-start = (f32[2,128]{1,0:T(2,128)S(1)}, f32[2,128]{1,0:T(2,128)}, u32[]{:S(2)}) copy-start(f32[2,128]{1,0:T(2,128)} %refs_5_.1) | copy-start | bytes 3076
  12.0 6.9 %collective-permute-start.3 = (bf16[128,128]{1,0:T(8,128)(2,1)S(1)}, bf16[128,128]{1,0:T(8,128)(2,1)S(1)}, u32[]{:S(2)}, u32[]{:S(2)}) collective-permute-start(bf16[128,128]{1,0:T(8,128)(2,1)S(1)} %get-tuple-element.33.refs_3_), channel_id=1, source_target_pairs={{0,1},{1,0},{2,3},{3,2},{4,5},{5,4},{6,7},{7,6},{8,9},{9,8},{10,11... | collective-permute-start | bytes 98312 | tf_op jit(solution)/shard_map/ppermute | solution.py:633
  13.6 5.4 %collective-permute-start.2 = (bf16[128,128]{1,0:T(8,128)(2,1)S(1)}, bf16[128,128]{1,0:T(8,128)(2,1)S(1)}, u32[]{:S(2)}, u32[]{:S(2)}) collective-permute-start(bf16[128,128]{1,0:T(8,128)(2,1)S(1)} %get-tuple-element.33.refs_3_), channel_id=1, source_target_pairs={{0,2},{1,3},{2,0},{3,1},{4,6},{5,7},{6,4},{7,5},{8,10},{9,11},{10,... | collective-permute-start | bytes 98312 | tf_op jit(solution)/shard_map/ppermute | solution.py:633
  13.7 5.3 %collective-permute-start.1 = (bf16[128,128]{1,0:T(8,128)(2,1)S(1)}, bf16[128,128]{1,0:T(8,128)(2,1)S(1)}, u32[]{:S(2)}, u32[]{:S(2)}) collective-permute-start(bf16[128,128]{1,0:T(8,128)(2,1)S(1)} %get-tuple-element.33.refs_3_), channel_id=1, source_target_pairs={{0,3},{1,2},{2,1},{3,0},{4,7},{5,6},{6,5},{7,4},{8,11},{9,10},{10,... | collective-permute-start | bytes 98312 | tf_op jit(solution)/shard_map/ppermute | solution.py:633
  21.8 8.4 %collective-permute-start.4 = (bf16[256,512]{1,0:T(8,128)(2,1)S(1)}, bf16[256,512]{1,0:T(8,128)(2,1)S(1)}, u32[]{:S(2)}, u32[]{:S(2)}) collective-permute-start(bf16[256,512]{1,0:T(8,128)(2,1)S(1)} %get-tuple-element.45), channel_id=1, source_target_pairs={{0,3},{1,2},{2,1},{3,0},{4,7},{5,6},{6,5},{7,4},{8,11},{9,10},{10,... | collective-permute-start | bytes 786440 | tf_op jit(solution)/shard_map/ppermute | solution.py:633
  27.0 8.4 %collective-permute-start.5 = (bf16[256,512]{1,0:T(8,128)(2,1)S(1)}, bf16[256,512]{1,0:T(8,128)(2,1)S(1)}, u32[]{:S(2)}, u32[]{:S(2)}) collective-permute-start(bf16[256,512]{1,0:T(8,128)(2,1)S(1)} %get-tuple-element.49), channel_id=1, source_target_pairs={{0,2},{1,3},{2,0},{3,1},{4,6},{5,7},{6,4},{7,5},{8,10},{9,11},{10,... | collective-permute-start | bytes 786440 | tf_op jit(solution)/shard_map/ppermute | solution.py:633
  28.6 6.8 %collective-permute-start.6 = (bf16[256,512]{1,0:T(8,128)(2,1)S(1)}, bf16[256,512]{1,0:T(8,128)(2,1)S(1)}, u32[]{:S(2)}, u32[]{:S(2)}) collective-permute-start(bf16[256,512]{1,0:T(8,128)(2,1)S(1)} %get-tuple-element.50), channel_id=1, source_target_pairs={{0,1},{1,0},{2,3},{3,2},{4,5},{5,4},{6,7},{7,6},{8,9},{9,8},{10,11... | collective-permute-start | bytes 786440 | tf_op jit(solution)/shard_map/ppermute | solution.py:633
